TPU v7x, 256 devices: a whole 4x4x8 slice. The times are simulated.
256 devices in a mesh: blk: 128 (over y_hi, z, x, core), cat: 2 (over y_lo).
Axes of the slice: x: 4, y: 4 (y_hi: 2, y_lo: 2; y = y_hi * 2 + y_lo), z: 8, core: 2. Of those that a mesh axis runs over, the one named last changes fastest.
Arguments:
- item_content: bfloat16 [262144, 512], P('blk', 'cat'), may hold values from -6 to 6
- projection: bfloat16 [512, 256], replicated, may hold values from -0.06591797 to 0.06591797
- send_order: int32 [256, 1024], P(('blk', 'cat')), may hold values from 0 to 1023, each once within a row
- user_factors: float32 [131072, 256], P(('blk', 'cat')), may hold values from -1.5 to 1.5
- ratings: int32 [131072, 4, 1024], P(('blk', 'cat')), may hold values from 0 to 5, as said below
Outputs:
- users_out: float32 [131072, 256], P(('blk', 'cat'))
- items_out: float32 [262144, 256], P(('blk', 'cat'))
Inputs may be any that keep to these rules, and one draw needn't show every extreme that they name: `send_order`: each row is a permutation of 0 .. 1023. `ratings`: 0 means no rating, 1 to 5 a rating.
All inputs are finite; a program needn't handle non-finite values.
Results may differ from a plain program's by a relative error of at most 0.0003.
Values may be sent and summed in bfloat16 or wider, within the bound.
No kernel may reach another device: no remote copies, remote signals or barrier semaphores. Data moves between devices by JAX's collectives and lax.ppermute only.
A program may use at most 64 MiB of HBM per device.

v0:
```python
import functools

import jax
import jax.numpy as jnp
from jax import lax
from jax.experimental import pallas as pl
from jax.experimental.pallas import tpu as pltpu
from jax.sharding import PartitionSpec as P

ROUNDS = 4
learn_rate = 0.004
shrink = 0.05
KEEP = 1.0 - learn_rate * shrink
CONTENT_BOUND = 6.0
LOG_RANGE = 14.0
TOP = 32767.0
EVEN_PIECES = 2
ODD_PIECES = 2
EVEN_TAIL = 16
ODD_TAIL = 8
F32 = jnp.float32
BF16 = jnp.bfloat16
I32 = jnp.int32

VM = pl.BlockSpec(memory_space=pltpu.VMEM)
SM = pl.BlockSpec(memory_space=pltpu.SMEM)
ANY = pl.BlockSpec(memory_space=pl.ANY)


def params(limit=12):
    return pltpu.CompilerParams(vmem_limit_bytes=limit << 20)


def cost(flops, moved):
    return pl.CostEstimate(flops=flops, bytes_accessed=moved, transcendentals=0)


def split(x):
    hi = x.astype(BF16)
    return hi, (x - hi.astype(F32)).astype(BF16)


def mm(a, b, dims=((1,), (0,))):
    return lax.dot_general(a, b, (dims, ((), ())), preferred_element_type=F32)


def pack(a, b):
    return lax.shift_left(a, 16) | (b & 0xFFFF)


def unpack(w):
    return (
        lax.shift_right_arithmetic(w, 16).astype(F32),
        lax.shift_right_arithmetic(lax.shift_left(w, 16), 16).astype(F32),
    )


def rounded(x):
    return jnp.round(x).astype(I32)


def log_scale(bound):
    floor = bound * (2.0 ** -LOG_RANGE)
    return floor, TOP / (jnp.log2(1.0 + 2.0 ** LOG_RANGE) * 1.0001)


def log_code(x, bound):
    floor, scale = log_scale(bound)
    size = jnp.minimum(jnp.log2(1.0 + jnp.abs(x) / floor) * scale, TOP)
    return rounded(jnp.where(x < 0, -size, size))


def log_value(code, bound):
    floor, scale = log_scale(bound)
    size = (jnp.exp2(jnp.abs(code) * (1.0 / scale)) - 1.0) * floor
    return jnp.where(code < 0, -size, size)


def put_users(p, users, left, left_t):
    hi, lo = split(p)
    if users is not None:
        users[...] = p
    left[0] = hi
    left[1] = lo
    hi_t, lo_t = split(p.T)
    left_t[0] = hi_t
    left_t[1] = lo_t


def before_kernel(flags, order, content, weights, users, deal, partial, meta, left, left_t, rows, sem):
    n = order.shape[1]
    part = flags[0]
    copy = pltpu.make_async_copy(content.at[pl.ds(pl.multiple_of(part * n, n), n), :], rows, sem)
    copy.start()
    column_sums = jnp.sum(jnp.abs(weights[...].astype(F32)), axis=0, keepdims=True)
    bound = jnp.maximum(jnp.max(column_sums, axis=1, keepdims=True) * (CONTENT_BOUND * 1.001), 1e-30)
    meta[...] = jnp.broadcast_to(bound, meta.shape)
    lanes = lax.broadcasted_iota(I32, (128, n), 1)
    for at in range(0, n, 128):
        wide = jnp.broadcast_to(order[:, at:at + 128], (128, 128)).T
        picked = jnp.concatenate([wide] * (n // 128), axis=1) == lanes
        deal[at:at + 128, :] = jnp.where(picked, 1.0, 0.0).astype(BF16)
    put_users(users[...], None, left, left_t)
    copy.wait()
    depth = content.shape[1]
    mine = weights[pl.ds(pl.multiple_of(part * depth, depth), depth), :]
    partial[...] = mm(mm(deal[...], rows[...]).astype(BF16), mine)


def project_kernel(flags, deal, first, second, weights, partial, meta, out):
    other = 1 - flags[0]
    depth = first.shape[1]
    half = first.shape[0]
    theirs = weights[pl.ds(pl.multiple_of(other * depth, depth), depth), :]
    rows = mm(deal[:, :half], first[...]) + mm(deal[:, half:], second[...])
    x = partial[...] + mm(rows.astype(BF16), theirs)
    code = log_code(x, meta[0:1, 0:1])
    mid = x.shape[1] // 2
    out[...] = pack(code[:, :mid], code[:, mid:])


def ratings_kernel(ratings, *outs):
    for t, out in enumerate(outs):
        out[...] = ratings[:, t, :].astype(F32).astype(BF16)


def encode(x):
    top = jnp.maximum(jnp.max(jnp.abs(x), axis=0, keepdims=True), 1e-30)
    level = jnp.ceil(jnp.log2(top) * 65536.0).astype(I32) + 4
    scale = TOP / jnp.exp2(level.astype(F32) * (1.0 / 65536.0))
    code = rounded(jnp.clip(x * scale, -TOP, TOP))
    mid = x.shape[0] // 2
    return pack(code[:mid], code[mid:]), level


def decode(w, rank):
    rows = rank // 2
    a, b = unpack(w[:rows, :])
    scale = jnp.exp2(w[rows:rows + 1, :].astype(F32) * (1.0 / 65536.0)) * (1.0 / TOP)
    return jnp.concatenate([a, b], axis=0) * scale


def errors_and_items(q, cols, left, left_t, values, err, right):
    q_hi, q_lo = split(q)
    if right is not None:
        right[0, :, cols] = q_hi
        right[1, :, cols] = q_lo
    guess = mm(left[0], q_hi) + mm(left[0], q_lo) + mm(left[1], q_hi)
    v = values[:, cols].astype(F32)
    e_hi, e_lo = split(jnp.where(v > 0, v - guess, 0.0))
    err[0, :, cols] = e_hi
    err[1, :, cols] = e_lo
    grad = mm(left_t[0], e_hi) + mm(left_t[0], e_lo) + mm(left_t[1], e_hi)
    return KEEP * q + learn_rate * grad


def first_items(dealt, meta, cols):
    w = dealt[cols, :].T
    a, b = unpack(w)
    return log_value(jnp.concatenate([a, b], axis=0), meta[0:1, 0:1])


CHUNK = 256


def piece(refs, at):
    wide = refs[0].shape[1]
    return refs[at // wide], slice(at % wide, at % wide + CHUNK)


def push_kernel(turn, first, pieces, *refs):
    flags, left, left_t, values = refs[:4]
    refs = refs[4:]
    if first:
        dealt, meta = refs[:2]
        refs = refs[2:]
    else:
        got = refs[:-2 - pieces]
        refs = refs[-2 - pieces:]
    err, right = refs[:2]
    outs = refs[2:]
    n = values.shape[1]

    @pl.when(flags[1] == turn)
    def _():
        for at in range(0, n, CHUNK):
            cols = slice(at, at + CHUNK)
            if first:
                q = first_items(dealt, meta, cols)
            else:
                ref, here = piece(got, at)
                q = decode(ref[:, here], right.shape[1])
            words, level = encode(errors_and_items(q, cols, left, left_t, values, err, right))
            rows = words.shape[0]
            ref, here = piece(outs, at)
            ref[:rows, here] = words
            ref[rows:, here] = jnp.broadcast_to(level, (ref.shape[0] - rows, CHUNK))


def user_step(users, err, right):
    dims = ((1,), (1,))
    grad = mm(err[0], right[0], dims) + mm(err[0], right[1], dims) + mm(err[1], right[0], dims)
    return KEEP * users[...] + learn_rate * grad


def pull_kernel(flags, users, err_odd, right_odd, err_even, right_even, new_users, left, left_t):
    for turn, err, right in ((1, err_odd, right_odd), (0, err_even, right_even)):

        @pl.when(flags[1] == turn)
        def _():
            put_users(user_step(users, err, right), new_users, left, left_t)


def last_kernel(flags, left, left_t, values, users, *refs):
    even = refs[:EVEN_PIECES]
    odd = refs[EVEN_PIECES:EVEN_PIECES + ODD_PIECES]
    users_out, items_out, err, right = refs[EVEN_PIECES + ODD_PIECES:]
    is_odd = flags[1] == 1
    for at in range(0, values.shape[1], CHUNK):
        cols = slice(at, at + CHUNK)
        (a, at_a), (b, at_b) = piece(odd, at), piece(even, at)
        live = right.shape[1] // 2 + 8
        q = decode(jnp.where(is_odd, a[:live, at_a], b[:live, at_b]), right.shape[1])
        items_out[cols, :] = errors_and_items(q, cols, left, left_t, values, err, right).T
    users_out[...] = user_step(users, err, right)


def struct(shape, dtype):
    return jax.ShapeDtypeStruct(shape, dtype)


def body(n_blk, item_content, projection, send_order, user_factors, ratings):
    n_users, rank = user_factors.shape
    n_items = send_order.shape[1]
    depth = item_content.shape[1]
    share = n_items // n_blk
    wide = n_items // 2
    part = lax.axis_index("cat")
    place = lax.axis_index("blk")
    flags = jnp.stack([part, lax.rem(place, 2)]).astype(I32)
    swap = [(0, 1), (1, 0)]
    away = lax.dynamic_slice_in_dim(item_content, (1 - part) * n_items, n_items, axis=0)
    came = [lax.ppermute(away[i * wide:(i + 1) * wide], "cat", swap) for i in range(2)]
    split_shapes = [struct((2, n_users, rank), BF16), struct((2, rank, n_users), BF16)]
    deal, partial, meta, left, left_t = pl.pallas_call(
        before_kernel,
        out_shape=[
            struct((n_items, n_items), BF16),
            struct((n_items, rank), F32),
            struct((8, 128), F32),
        ] + split_shapes,
        in_specs=[SM, VM, ANY, VM, VM],
        out_specs=[VM] * 5,
        scratch_shapes=[pltpu.VMEM((n_items, depth), BF16), pltpu.SemaphoreType.DMA],
        compiler_params=params(),
        cost_estimate=cost(2 * n_items * n_items * depth, 6 << 20),
        name="before",
    )(flags, send_order, item_content, projection, user_factors)
    coded = pl.pallas_call(
        project_kernel,
        out_shape=struct((n_items, rank // 2), I32),
        in_specs=[SM] + [VM] * 6,
        out_specs=VM,
        compiler_params=params(),
        cost_estimate=cost(2 * n_items * n_items * depth, 4 << 20),
        name="project",
    )(flags, deal, came[0], came[1], projection, partial, meta)
    dealt = lax.all_to_all(
        coded.reshape(n_blk, share, rank // 2), "blk", split_axis=0, concat_axis=0, tiled=True
    ).reshape(n_items, rank // 2)
    ratings, coded = lax.optimization_barrier((ratings, coded))
    rows = 64
    values = pl.pallas_call(
        ratings_kernel,
        out_shape=[struct((n_users, n_items), BF16)] * ROUNDS,
        grid=(n_users // rows,),
        in_specs=[pl.BlockSpec((rows, ROUNDS, n_items), lambda i: (i, 0, 0))],
        out_specs=[pl.BlockSpec((rows, n_items), lambda i: (i, 0))] * ROUNDS,
        compiler_params=params(32),
        cost_estimate=cost(1 << 20, 12 << 20),
        name="ratings",
    )(ratings)

    state_shapes = [struct((2, n_users, n_items), BF16), struct((2, rank, n_items), BF16)]
    round_cost = cost(2 * n_users * n_items * rank * 6, 6 << 20)
    to_even = [(i, (i + 1) % n_blk) for i in range(1, n_blk, 2)]
    to_odd = [(i, i + 1) for i in range(0, n_blk, 2)]

    def push(turn, source, pieces, tail, flags=flags):
        sent_shapes = [struct((rank // 2 + tail, n_items // pieces), I32)] * pieces
        first = len(source) == 2 and source[0].shape[0] == n_items
        ins = [flags, left, left_t, values[t], *source]
        got = pl.pallas_call(
            functools.partial(push_kernel, turn, first, pieces),
            out_shape=state_shapes + sent_shapes,
            in_specs=[SM] + [VM] * (len(ins) - 1),
            out_specs=[VM] * (2 + pieces),
            compiler_params=params(),
            cost_estimate=cost(1 << 10, 1 << 10),
            name="push",
        )(*ins)
        return got[:2], got[2:]

    users = user_factors
    for_odd = for_even = [dealt, meta]
    for t in range(ROUNDS - 1):
        state_odd, sent = push(1, for_odd, EVEN_PIECES, EVEN_TAIL)
        next_even = [lax.ppermute(x, "blk", to_even) for x in sent]
        later, _ = lax.optimization_barrier((flags, sent[0]))
        state_even, sent = push(0, for_even, ODD_PIECES, ODD_TAIL, later)
        next_odd = [lax.ppermute(x, "blk", to_odd) for x in sent]
        users, left, left_t = pl.pallas_call(
            pull_kernel,
            out_shape=[struct((n_users, rank), F32)] + split_shapes,
            in_specs=[SM] + [VM] * 5,
            out_specs=[VM] * 3,
            compiler_params=params(),
            cost_estimate=cost(1 << 10, 1 << 10),
            name="pull",
        )(flags, users, *state_odd, *state_even)
        for_even, for_odd = next_even, next_odd
    return tuple(pl.pallas_call(
        last_kernel,
        out_shape=[struct((n_users, rank), F32), struct((n_items, rank), F32)],
        in_specs=[SM] + [VM] * (4 + EVEN_PIECES + ODD_PIECES),
        out_specs=[VM] * 2,
        scratch_shapes=[
            pltpu.VMEM((2, n_users, n_items), BF16),
            pltpu.VMEM((2, rank, n_items), BF16),
        ],
        compiler_params=params(),
        cost_estimate=round_cost,
        name="last",
    )(flags, left, left_t, values[ROUNDS - 1], users, *for_even, *for_odd))


def solution(mesh):
    placed = (
        P("blk", "cat"),
        P(),
        P(("blk", "cat"), None),
        P(("blk", "cat"), None),
        P(("blk", "cat"), None, None),
    )
    return jax.shard_map(
        functools.partial(body, mesh.shape["blk"]),
        mesh=mesh,
        in_specs=placed,
        out_specs=(P(("blk", "cat"), None), P(("blk", "cat"), None)),
        check_vma=False,
    )
```

profile of v0, /device:TPU:8, one launch (start us, length us, event | category | flops | bytes accessed | tf_op | source)
XLA Modules:
  0.0 104.4 jit_solution(9589084400543263564)
XLA Ops:
  1.7 2.3 %collective-permute-start.1 = (bf16[512,256]{1,0:T(8,128)(2,1)S(1)}, bf16[512,256]{1,0:T(8,128)(2,1)S(1)}, u32[]{:S(2)}, u32[]{:S(2)}) collective-permute-start(bf16[512,256]{1,0:T(8,128)(2,1)S(1)} %get-tuple-element.94), channel_id=1, source_target_pairs={{0,1},{1,0},{2,3},{3,2},{4,5},{5,4},{6,7},{7,6},{8,9},{9,8},{10,11... | collective-permute-start | bytes 786440 | tf_op jit(solution)/shard_map/ppermute | solution.py:243
  5.2 1.2 %copy-done.7 = bf16[2048,256]{1,0:T(8,128)(2,1)S(1)} copy-done((bf16[2048,256]{1,0:T(8,128)(2,1)S(1)}, bf16[2048,256]{1,0:T(8,128)(2,1)}, u32[]{:S(2)}) %copy-start.7) | copy-done | bytes 1048600
  8.1 2.1 %before.1 = (bf16[1024,1024]{1,0:T(8,128)(2,1)S(1)}, f32[1024,256]{1,0:T(8,128)S(1)}, f32[8,128]{1,0:T(8,128)S(1)}, bf16[2,512,256]{2,1,0:T(8,128)(2,1)S(1)}, bf16[2,256,512]{2,1,0:T(8,128)(2,1)S(1)}) custom-call(s32[2]{0:T(128)S(1)} %pad_add_fusion.flags.refs_0_, s32[1,1024]{1,0:T(1,128)S(1)} %copy-done.11, bf16[2048,256]{1,0:T(8,128)(2,1)S(1)} %copy-done.7, ...), custom_call_target="tpu_custom_call" | custom-call | flops 536870912 | bytes 6291456 | tf_op jit(solution)/shard_map/before/pallas_call | solution.py:245
  11.2 4.3 %collective-permute-done.first = bf16[512,256]{1,0:T(8,128)(2,1)S(1)} collective-permute-done((bf16[512,256]{1,0:T(8,128)(2,1)S(1)}, bf16[512,256]{1,0:T(8,128)(2,1)S(1)}, u32[]{:S(2)}, u32[]{:S(2)}) %collective-permute-start) | collective-permute-done | bytes 262176 | tf_op jit(solution)/shard_map/ppermute | solution.py:243
  15.5 2.5 %project.1 = s32[1024,128]{1,0:T(8,128)} custom-call(s32[2]{0:T(128)S(1)} %pad_add_fusion.flags.refs_0_, bf16[1024,1024]{1,0:T(8,128)(2,1)S(1)} %get-tuple-element.50.deal, bf16[512,256]{1,0:T(8,128)(2,1)S(1)} %collective-permute-done.first, bf16[512,256]{1,0:T(8,128)(2,1)S(1)} %collective-permute-done.1.second, bf16[512,256]{1,0:T(8,128)(2,1)S(1)} %copy-done.8, ...), custom_call_target="tpu_custom_call" | custom-call | flops 536870912 | bytes 4194304 | tf_op jit(solution)/shard_map/project/pallas_call | solution.py:259
  18.0 14.9 %all-to-all-start = ((s32[128,8,128]{2,1,0:T(8,128)}), s32[128,8,128]{2,1,0:T(8,128)S(1)}, u32[]{:S(2)}, u32[]{:S(2)}) async-start(s32[128,8,128]{2,1,0:T(8,128)} %bitcast.2), calls=%async_computation | async-start | bytes 1048576 | tf_op jit(solution)/shard_map/all_to_all | solution.py:268
  32.9 3.4 %copy-done = s32[512,4,1024]{2,1,0:T(4,128)S(1)} copy-done((s32[512,4,1024]{2,1,0:T(4,128)S(1)}, s32[512,4,1024]{2,1,0:T(4,128)}, u32[]{:S(2)}) %copy-start) | copy-done | bytes 8388632
  36.2 10.8 %ratings.1 = (bf16[512,1024]{1,0:T(8,128)(2,1)S(1)}, bf16[512,1024]{1,0:T(8,128)(2,1)S(1)}, bf16[512,1024]{1,0:T(8,128)(2,1)S(1)}, bf16[512,1024]{1,0:T(8,128)(2,1)S(1)}) custom-call(s32[512,4,1024]{2,1,0:T(4,128)S(1)} %copy-done), custom_call_target="tpu_custom_call" | custom-call | flops 1048576 | bytes 12582912 | tf_op jit(solution)/shard_map/ratings/pallas_call | solution.py:273
  49.0 5.3 %all-to-all-done = s32[128,8,128]{2,1,0:T(8,128)S(1)} async-done(((s32[128,8,128]{2,1,0:T(8,128)}), s32[128,8,128]{2,1,0:T(8,128)S(1)}, u32[]{:S(2)}, u32[]{:S(2)}) %all-to-all-start) | async-done | bytes 524320 | tf_op jit(solution)/shard_map/all_to_all | solution.py:268
  54.3 1.2 %copy-done.2 = bf16[512,1024]{1,0:T(8,128)(2,1)S(1)} copy-done((bf16[512,1024]{1,0:T(8,128)(2,1)S(1)}, bf16[512,1024]{1,0:T(8,128)(2,1)}, u32[]{:S(2)}) %copy-start.2) | copy-done | bytes 1048600
  57.1 1.3 %collective-permute-start.5 = (s32[144,512]{1,0:T(8,128)S(1)}, s32[144,512]{1,0:T(8,128)S(1)}, u32[]{:S(2)}, u32[]{:S(2)}) collective-permute-start(s32[144,512]{1,0:T(8,128)S(1)} %get-tuple-element.71), channel_id=1, source_target_pairs={{2,4},{6,8},{10,12},{14,16},{18,20},{22,24},{26,28},{30,32},{34,36... | collective-permute-start | bytes 884744 | tf_op jit(solution)/shard_map/ppermute | solution.py:308
  58.4 1.3 %collective-permute-start.4 = (s32[144,512]{1,0:T(8,128)S(1)}, s32[144,512]{1,0:T(8,128)S(1)}, u32[]{:S(2)}, u32[]{:S(2)}) collective-permute-start(s32[144,512]{1,0:T(8,128)S(1)} %get-tuple-element.57), channel_id=1, source_target_pairs={{2,4},{6,8},{10,12},{14,16},{18,20},{22,24},{26,28},{30,32},{34,36... | collective-permute-start | bytes 884744 | tf_op jit(solution)/shard_map/ppermute | solution.py:308
  59.7 3.7 %push.7 = (bf16[2,512,1024]{2,1,0:T(8,128)(2,1)S(1)}, bf16[2,256,1024]{2,1,0:T(8,128)(2,1)S(1)}, s32[136,512]{1,0:T(8,128)S(1)}, s32[136,512]{1,0:T(8,128)S(1)}) custom-call(s32[2]{0:T(128)S(1)} %pad_add_fusion.flags.refs_0_, bf16[2,512,256]{2,1,0:T(8,128)(2,1)S(1)} %get-tuple-element.48.refs_1_, bf16[2,256,512]{2,1,0:T(8,128)(2,1)S(1)} %copy-done.4, ...), custom_call_target="tpu_custom_call" | custom-call | flops 1024 | bytes 1024 | tf_op jit(solution)/shard_map/push/pallas_call | solution.py:293
  63.4 2.2 %collective-permute-start.2 = (s32[136,512]{1,0:T(8,128)S(1)}, s32[136,512]{1,0:T(8,128)S(1)}, u32[]{:S(2)}, u32[]{:S(2)}) collective-permute-start(s32[136,512]{1,0:T(8,128)S(1)} %get-tuple-element.65), channel_id=1, source_target_pairs={{0,2},{4,6},{8,10},{12,14},{16,18},{20,22},{24,26},{28,30},{32,34}... | collective-permute-start | bytes 835592 | tf_op jit(solution)/shard_map/ppermute | solution.py:311
  65.6 1.3 %collective-permute-start.3 = (s32[136,512]{1,0:T(8,128)S(1)}, s32[136,512]{1,0:T(8,128)S(1)}, u32[]{:S(2)}, u32[]{:S(2)}) collective-permute-start(s32[136,512]{1,0:T(8,128)S(1)} %get-tuple-element.66), channel_id=1, source_target_pairs={{0,2},{4,6},{8,10},{12,14},{16,18},{20,22},{24,26},{28,30},{32,34}... | collective-permute-start | bytes 835592 | tf_op jit(solution)/shard_map/ppermute | solution.py:311
  66.9 1.7 %pull.3 = (f32[512,256]{1,0:T(8,128)S(1)}, bf16[2,512,256]{2,1,0:T(8,128)(2,1)S(1)}, bf16[2,256,512]{2,1,0:T(8,128)(2,1)S(1)}) custom-call(s32[2]{0:T(128)S(1)} %pad_add_fusion.flags.refs_0_, f32[512,256]{1,0:T(8,128)S(1)} %copy-done.6, bf16[2,512,1024]{2,1,0:T(8,128)(2,1)S(1)} %get-tuple-element.55.err_odd, ...), custom_call_target="tpu_custom_call" | custom-call | flops 1024 | bytes 1024 | tf_op jit(solution)/shard_map/pull/pallas_call | solution.py:312
  69.2 1.3 %collective-permute-start.8 = (s32[144,512]{1,0:T(8,128)S(1)}, s32[144,512]{1,0:T(8,128)S(1)}, u32[]{:S(2)}, u32[]{:S(2)}) collective-permute-start(s32[144,512]{1,0:T(8,128)S(1)} %get-tuple-element.69), channel_id=1, source_target_pairs={{2,4},{6,8},{10,12},{14,16},{18,20},{22,24},{26,28},{30,32},{34,36... | collective-permute-start | bytes 884744 | tf_op jit(solution)/shard_map/ppermute | solution.py:308
  70.5 1.3 %collective-permute-start.9 = (s32[144,512]{1,0:T(8,128)S(1)}, s32[144,512]{1,0:T(8,128)S(1)}, u32[]{:S(2)}, u32[]{:S(2)}) collective-permute-start(s32[144,512]{1,0:T(8,128)S(1)} %get-tuple-element.84), channel_id=1, source_target_pairs={{2,4},{6,8},{10,12},{14,16},{18,20},{22,24},{26,28},{30,32},{34,36... | collective-permute-start | bytes 884744 | tf_op jit(solution)/shard_map/ppermute | solution.py:308
  71.8 2.2 %collective-permute-done.4.refs_4_ = s32[144,512]{1,0:T(8,128)S(1)} collective-permute-done((s32[144,512]{1,0:T(8,128)S(1)}, s32[144,512]{1,0:T(8,128)S(1)}, u32[]{:S(2)}, u32[]{:S(2)}) %collective-permute-start.4) | collective-permute-done | bytes 294944 | tf_op jit(solution)/shard_map/ppermute | solution.py:308
  74.1 3.3 %push.9 = (bf16[2,512,1024]{2,1,0:T(8,128)(2,1)S(1)}, bf16[2,256,1024]{2,1,0:T(8,128)(2,1)S(1)}, s32[136,512]{1,0:T(8,128)S(1)}, s32[136,512]{1,0:T(8,128)S(1)}) custom-call(s32[2]{0:T(128)S(1)} %pad_add_fusion.flags.refs_0_, bf16[2,512,256]{2,1,0:T(8,128)(2,1)S(1)} %get-tuple-element.62.refs_1_, bf16[2,256,512]{2,1,0:T(8,128)(2,1)S(1)} %get-tuple-element.63.refs_2_, ...), custom_call_target="tpu_custom_call" | custom-call | flops 1024 | bytes 1024 | tf_op jit(solution)/shard_map/push/pallas_call | solution.py:293
  77.4 1.3 %collective-permute-start.6 = (s32[136,512]{1,0:T(8,128)S(1)}, s32[136,512]{1,0:T(8,128)S(1)}, u32[]{:S(2)}, u32[]{:S(2)}) collective-permute-start(s32[136,512]{1,0:T(8,128)S(1)} %get-tuple-element.78), channel_id=1, source_target_pairs={{0,2},{4,6},{8,10},{12,14},{16,18},{20,22},{24,26},{28,30},{32,34}... | collective-permute-start | bytes 835592 | tf_op jit(solution)/shard_map/ppermute | solution.py:311
  78.7 1.3 %collective-permute-start.7 = (s32[136,512]{1,0:T(8,128)S(1)}, s32[136,512]{1,0:T(8,128)S(1)}, u32[]{:S(2)}, u32[]{:S(2)}) collective-permute-start(s32[136,512]{1,0:T(8,128)S(1)} %get-tuple-element.79), channel_id=1, source_target_pairs={{0,2},{4,6},{8,10},{12,14},{16,18},{20,22},{24,26},{28,30},{32,34}... | collective-permute-start | bytes 835592 | tf_op jit(solution)/shard_map/ppermute | solution.py:311
  80.0 1.7 %pull.4 = (f32[512,256]{1,0:T(8,128)S(1)}, bf16[2,512,256]{2,1,0:T(8,128)(2,1)S(1)}, bf16[2,256,512]{2,1,0:T(8,128)(2,1)S(1)}) custom-call(s32[2]{0:T(128)S(1)} %pad_add_fusion.flags.refs_0_, f32[512,256]{1,0:T(8,128)S(1)} %get-tuple-element.61.users, bf16[2,512,1024]{2,1,0:T(8,128)(2,1)S(1)} %get-tuple-element.67.err_odd, ...), custom_call_target="tpu_custom_call" | custom-call | flops 1024 | bytes 1024 | tf_op jit(solution)/shard_map/pull/pallas_call | solution.py:312
  82.5 1.3 %collective-permute-start.11 = (s32[144,512]{1,0:T(8,128)S(1)}, s32[144,512]{1,0:T(8,128)S(1)}, u32[]{:S(2)}, u32[]{:S(2)}) collective-permute-start(s32[144,512]{1,0:T(8,128)S(1)} %get-tuple-element.91), channel_id=1, source_target_pairs={{2,4},{6,8},{10,12},{14,16},{18,20},{22,24},{26,28},{30,32},{34,36... | collective-permute-start | bytes 884744 | tf_op jit(solution)/shard_map/ppermute | solution.py:308
  83.8 1.3 %collective-permute-start.10 = (s32[144,512]{1,0:T(8,128)S(1)}, s32[144,512]{1,0:T(8,128)S(1)}, u32[]{:S(2)}, u32[]{:S(2)}) collective-permute-start(s32[144,512]{1,0:T(8,128)S(1)} %get-tuple-element.82), channel_id=1, source_target_pairs={{2,4},{6,8},{10,12},{14,16},{18,20},{22,24},{26,28},{30,32},{34,36... | collective-permute-start | bytes 884744 | tf_op jit(solution)/shard_map/ppermute | solution.py:308
  86.1 3.3 %push.11 = (bf16[2,512,1024]{2,1,0:T(8,128)(2,1)S(1)}, bf16[2,256,1024]{2,1,0:T(8,128)(2,1)S(1)}, s32[136,512]{1,0:T(8,128)S(1)}, s32[136,512]{1,0:T(8,128)S(1)}) custom-call(s32[2]{0:T(128)S(1)} %pad_add_fusion.flags.refs_0_, bf16[2,512,256]{2,1,0:T(8,128)(2,1)S(1)} %get-tuple-element.75.refs_1_, bf16[2,256,512]{2,1,0:T(8,128)(2,1)S(1)} %get-tuple-element.76.refs_2_, ...), custom_call_target="tpu_custom_call" | custom-call | flops 1024 | bytes 1024 | tf_op jit(solution)/shard_map/push/pallas_call | solution.py:293
  89.5 1.3 %collective-permute-start.12 = (s32[136,512]{1,0:T(8,128)S(1)}, s32[136,512]{1,0:T(8,128)S(1)}, u32[]{:S(2)}, u32[]{:S(2)}) collective-permute-start(s32[136,512]{1,0:T(8,128)S(1)} %get-tuple-element.92), channel_id=1, source_target_pairs={{0,2},{4,6},{8,10},{12,14},{16,18},{20,22},{24,26},{28,30},{32,34}... | collective-permute-start | bytes 835592 | tf_op jit(solution)/shard_map/ppermute | solution.py:311
  90.8 1.3 %collective-permute-start.13 = (s32[136,512]{1,0:T(8,128)S(1)}, s32[136,512]{1,0:T(8,128)S(1)}, u32[]{:S(2)}, u32[]{:S(2)}) collective-permute-start(s32[136,512]{1,0:T(8,128)S(1)} %get-tuple-element.93), channel_id=1, source_target_pairs={{0,2},{4,6},{8,10},{12,14},{16,18},{20,22},{24,26},{28,30},{32,34}... | collective-permute-start | bytes 835592 | tf_op jit(solution)/shard_map/ppermute | solution.py:311
  92.1 1.7 %pull.5 = (f32[512,256]{1,0:T(8,128)S(1)}, bf16[2,512,256]{2,1,0:T(8,128)(2,1)S(1)}, bf16[2,256,512]{2,1,0:T(8,128)(2,1)S(1)}) custom-call(s32[2]{0:T(128)S(1)} %pad_add_fusion.flags.refs_0_, f32[512,256]{1,0:T(8,128)S(1)} %get-tuple-element.74.users, bf16[2,512,1024]{2,1,0:T(8,128)(2,1)S(1)} %get-tuple-element.80.err_odd, ...), custom_call_target="tpu_custom_call" | custom-call | flops 1024 | bytes 1024 | tf_op jit(solution)/shard_map/pull/pallas_call | solution.py:312
  93.8 2.5 %collective-permute-done.11.refs_1_ = s32[144,512]{1,0:T(8,128)S(1)} collective-permute-done((s32[144,512]{1,0:T(8,128)S(1)}, s32[144,512]{1,0:T(8,128)S(1)}, u32[]{:S(2)}, u32[]{:S(2)}) %collective-permute-start.11) | collective-permute-done | bytes 294944 | tf_op jit(solution)/shard_map/ppermute | solution.py:308
  96.3 3.2 %collective-permute-done.10.refs_0_ = s32[144,512]{1,0:T(8,128)S(1)} collective-permute-done((s32[144,512]{1,0:T(8,128)S(1)}, s32[144,512]{1,0:T(8,128)S(1)}, u32[]{:S(2)}, u32[]{:S(2)}) %collective-permute-start.10) | collective-permute-done | bytes 294944 | tf_op jit(solution)/shard_map/ppermute | solution.py:308
  99.4 5.0 %last.1 = (f32[512,256]{1,0:T(8,128)}, f32[1024,256]{1,0:T(8,128)}) custom-call(s32[2]{0:T(128)S(1)} %pad_add_fusion.flags.refs_0_, bf16[2,512,256]{2,1,0:T(8,128)(2,1)S(1)} %get-tuple-element.87.left, bf16[2,256,512]{2,1,0:T(8,128)(2,1)S(1)} %get-tuple-element.88.left_t, bf16[512,1024]{1,0:T(8,128)(2,1)S(1)} %copy-done.10, ...), custom_call_target="tpu_custom_call" | custom-call | flops 1610612736 | bytes 6291456 | tf_op jit(solution)/shard_map/last/pallas_call | solution.py:322
  (37 shorter events, 10.8 us)
Async XLA Ops:
  1.7 9.5 %collective-permute-start.1 = (bf16[512,256]{1,0:T(8,128)(2,1)S(1)}, bf16[512,256]{1,0:T(8,128)(2,1)S(1)}, u32[]{:S(2)}, u32[]{:S(2)}) collective-permute-start(bf16[512,256]{1,0:T(8,128)(2,1)S(1)} %get-tuple-element.94), channel_id=1, source_target_pairs={{0,1},{1,0},{2,3},{3,2},{4,5},{5,4},{6,7},{7,6},{8,9},{9,8},{10,11... | collective-permute-start | bytes 786440 | tf_op jit(solution)/shard_map/ppermute | solution.py:243
  4.0 11.5 %collective-permute-start = (bf16[512,256]{1,0:T(8,128)(2,1)S(1)}, bf16[512,256]{1,0:T(8,128)(2,1)S(1)}, u32[]{:S(2)}, u32[]{:S(2)}) collective-permute-start(bf16[512,256]{1,0:T(8,128)(2,1)S(1)} %get-tuple-element.95), channel_id=1, source_target_pairs={{0,1},{1,0},{2,3},{3,2},{4,5},{5,4},{6,7},{7,6},{8,9},{9,8},{10,11... | collective-permute-start | bytes 786440 | tf_op jit(solution)/shard_map/ppermute | solution.py:243
  4.2 1.0 copy-start.5
  5.2 1.2 %copy-start.7 = (bf16[2048,256]{1,0:T(8,128)(2,1)S(1)}, bf16[2048,256]{1,0:T(8,128)(2,1)}, u32[]{:S(2)}) copy-start(bf16[2048,256]{1,0:T(8,128)(2,1)} %content.1) | copy-start | bytes 3145732
  6.4 0.9 copy-start.8
  7.4 0.7 copy-start.11
  10.2 7.8 %copy-start.3 = (bf16[2,256,512]{2,1,0:T(8,128)(2,1)}, bf16[2,256,512]{2,1,0:T(8,128)(2,1)S(1)}, u32[]{:S(2)}) copy-start(bf16[2,256,512]{2,1,0:T(8,128)(2,1)S(1)} %get-tuple-element.49.refs_2_) | copy-start | bytes 1572868
  18.0 36.4 %all-to-all-start = ((s32[128,8,128]{2,1,0:T(8,128)}), s32[128,8,128]{2,1,0:T(8,128)S(1)}, u32[]{:S(2)}, u32[]{:S(2)}) async-start(s32[128,8,128]{2,1,0:T(8,128)} %bitcast.2), calls=%async_computation | async-start | bytes 1048576 | tf_op jit(solution)/shard_map/all_to_all | solution.py:268
  32.9 3.4 %copy-start = (s32[512,4,1024]{2,1,0:T(4,128)S(1)}, s32[512,4,1024]{2,1,0:T(4,128)}, u32[]{:S(2)}) copy-start(s32[512,4,1024]{2,1,0:T(4,128)} %ratings.2) | copy-start | bytes 25165828
  47.0 1.0 copy-start.1
  48.0 1.0 copy-start.9
  54.3 1.2 %copy-start.2 = (bf16[512,1024]{1,0:T(8,128)(2,1)S(1)}, bf16[512,1024]{1,0:T(8,128)(2,1)}, u32[]{:S(2)}) copy-start(bf16[512,1024]{1,0:T(8,128)(2,1)} %copy-done.1) | copy-start | bytes 3145732
  55.5 1.0 copy-start.4
  56.6 10.4 %copy-start.6 = (f32[512,256]{1,0:T(8,128)S(1)}, f32[512,256]{1,0:T(8,128)}, u32[]{:S(2)}) copy-start(f32[512,256]{1,0:T(8,128)} %users.3) | copy-start | bytes 1572868
  57.1 14.7 %collective-permute-start.5 = (s32[144,512]{1,0:T(8,128)S(1)}, s32[144,512]{1,0:T(8,128)S(1)}, u32[]{:S(2)}, u32[]{:S(2)}) collective-permute-start(s32[144,512]{1,0:T(8,128)S(1)} %get-tuple-element.71), channel_id=1, source_target_pairs={{2,4},{6,8},{10,12},{14,16},{18,20},{22,24},{26,28},{30,32},{34,36... | collective-permute-start | bytes 884744 | tf_op jit(solution)/shard_map/ppermute | solution.py:308
  58.4 15.6 %collective-permute-start.4 = (s32[144,512]{1,0:T(8,128)S(1)}, s32[144,512]{1,0:T(8,128)S(1)}, u32[]{:S(2)}, u32[]{:S(2)}) collective-permute-start(s32[144,512]{1,0:T(8,128)S(1)} %get-tuple-element.57), channel_id=1, source_target_pairs={{2,4},{6,8},{10,12},{14,16},{18,20},{22,24},{26,28},{30,32},{34,36... | collective-permute-start | bytes 884744 | tf_op jit(solution)/shard_map/ppermute | solution.py:308
  63.4 5.2 %collective-permute-start.2 = (s32[136,512]{1,0:T(8,128)S(1)}, s32[136,512]{1,0:T(8,128)S(1)}, u32[]{:S(2)}, u32[]{:S(2)}) collective-permute-start(s32[136,512]{1,0:T(8,128)S(1)} %get-tuple-element.65), channel_id=1, source_target_pairs={{0,2},{4,6},{8,10},{12,14},{16,18},{20,22},{24,26},{28,30},{32,34}... | collective-permute-start | bytes 835592 | tf_op jit(solution)/shard_map/ppermute | solution.py:311
  65.6 3.0 %collective-permute-start.3 = (s32[136,512]{1,0:T(8,128)S(1)}, s32[136,512]{1,0:T(8,128)S(1)}, u32[]{:S(2)}, u32[]{:S(2)}) collective-permute-start(s32[136,512]{1,0:T(8,128)S(1)} %get-tuple-element.66), channel_id=1, source_target_pairs={{0,2},{4,6},{8,10},{12,14},{16,18},{20,22},{24,26},{28,30},{32,34}... | collective-permute-start | bytes 835592 | tf_op jit(solution)/shard_map/ppermute | solution.py:311
  69.2 16.9 %collective-permute-start.8 = (s32[144,512]{1,0:T(8,128)S(1)}, s32[144,512]{1,0:T(8,128)S(1)}, u32[]{:S(2)}, u32[]{:S(2)}) collective-permute-start(s32[144,512]{1,0:T(8,128)S(1)} %get-tuple-element.69), channel_id=1, source_target_pairs={{2,4},{6,8},{10,12},{14,16},{18,20},{22,24},{26,28},{30,32},{34,36... | collective-permute-start | bytes 884744 | tf_op jit(solution)/shard_map/ppermute | solution.py:308
  70.5 15.6 %collective-permute-start.9 = (s32[144,512]{1,0:T(8,128)S(1)}, s32[144,512]{1,0:T(8,128)S(1)}, u32[]{:S(2)}, u32[]{:S(2)}) collective-permute-start(s32[144,512]{1,0:T(8,128)S(1)} %get-tuple-element.84), channel_id=1, source_target_pairs={{2,4},{6,8},{10,12},{14,16},{18,20},{22,24},{26,28},{30,32},{34,36... | collective-permute-start | bytes 884744 | tf_op jit(solution)/shard_map/ppermute | solution.py:308
  77.4 4.3 %collective-permute-start.6 = (s32[136,512]{1,0:T(8,128)S(1)}, s32[136,512]{1,0:T(8,128)S(1)}, u32[]{:S(2)}, u32[]{:S(2)}) collective-permute-start(s32[136,512]{1,0:T(8,128)S(1)} %get-tuple-element.78), channel_id=1, source_target_pairs={{0,2},{4,6},{8,10},{12,14},{16,18},{20,22},{24,26},{28,30},{32,34}... | collective-permute-start | bytes 835592 | tf_op jit(solution)/shard_map/ppermute | solution.py:311
  78.7 3.0 %collective-permute-start.7 = (s32[136,512]{1,0:T(8,128)S(1)}, s32[136,512]{1,0:T(8,128)S(1)}, u32[]{:S(2)}, u32[]{:S(2)}) collective-permute-start(s32[136,512]{1,0:T(8,128)S(1)} %get-tuple-element.79), channel_id=1, source_target_pairs={{0,2},{4,6},{8,10},{12,14},{16,18},{20,22},{24,26},{28,30},{32,34}... | collective-permute-start | bytes 835592 | tf_op jit(solution)/shard_map/ppermute | solution.py:311
  82.5 13.8 %collective-permute-start.11 = (s32[144,512]{1,0:T(8,128)S(1)}, s32[144,512]{1,0:T(8,128)S(1)}, u32[]{:S(2)}, u32[]{:S(2)}) collective-permute-start(s32[144,512]{1,0:T(8,128)S(1)} %get-tuple-element.91), channel_id=1, source_target_pairs={{2,4},{6,8},{10,12},{14,16},{18,20},{22,24},{26,28},{30,32},{34,36... | collective-permute-start | bytes 884744 | tf_op jit(solution)/shard_map/ppermute | solution.py:308
  83.8 15.6 %collective-permute-start.10 = (s32[144,512]{1,0:T(8,128)S(1)}, s32[144,512]{1,0:T(8,128)S(1)}, u32[]{:S(2)}, u32[]{:S(2)}) collective-permute-start(s32[144,512]{1,0:T(8,128)S(1)} %get-tuple-element.82), channel_id=1, source_target_pairs={{2,4},{6,8},{10,12},{14,16},{18,20},{22,24},{26,28},{30,32},{34,36... | collective-permute-start | bytes 884744 | tf_op jit(solution)/shard_map/ppermute | solution.py:308
  89.5 4.3 %collective-permute-start.12 = (s32[136,512]{1,0:T(8,128)S(1)}, s32[136,512]{1,0:T(8,128)S(1)}, u32[]{:S(2)}, u32[]{:S(2)}) collective-permute-start(s32[136,512]{1,0:T(8,128)S(1)} %get-tuple-element.92), channel_id=1, source_target_pairs={{0,2},{4,6},{8,10},{12,14},{16,18},{20,22},{24,26},{28,30},{32,34}... | collective-permute-start | bytes 835592 | tf_op jit(solution)/shard_map/ppermute | solution.py:311
  90.8 3.0 %collective-permute-start.13 = (s32[136,512]{1,0:T(8,128)S(1)}, s32[136,512]{1,0:T(8,128)S(1)}, u32[]{:S(2)}, u32[]{:S(2)}) collective-permute-start(s32[136,512]{1,0:T(8,128)S(1)} %get-tuple-element.93), channel_id=1, source_target_pairs={{0,2},{4,6},{8,10},{12,14},{16,18},{20,22},{24,26},{28,30},{32,34}... | collective-permute-start | bytes 835592 | tf_op jit(solution)/shard_map/ppermute | solution.py:311
  92.1 7.3 %copy-start.10 = (bf16[512,1024]{1,0:T(8,128)(2,1)S(1)}, bf16[512,1024]{1,0:T(8,128)(2,1)}, u32[]{:S(2)}) copy-start(bf16[512,1024]{1,0:T(8,128)(2,1)} %copy-done.9) | copy-start | bytes 3145732
where the time goes:
time: 105 us; the launch traced here: 104 us
  Pallas kernels  37.6 us (36%)
  starting transfers between devices  33.7 us (32%)
  waiting for transfers between devices  19.5 us (19%)
  local copies, waits for them, and re-layouts  12.6 us (12%)
    all_to_all x1, starting transfers between devices, body(): lax.all_to_all(coded.reshape(n_blk, share, rank // 2), 'blk', split_axis=...  14.9 us
    pallas_call x6, Pallas kernels, push(): pl.pallas_call(functools.partial(push_kernel, turn, first, pieces), out_s...  12.2 us
    unnamed x24, local copies, waits for them, and re-layouts  11.5 us
    pallas_call x1, Pallas kernels, body(): pl.pallas_call(ratings_kernel, out_shape=[struct((n_users, n_items), BF16...  10.8 us
    ppermute x6, waiting for transfers between devices, body(): next_even = [lax.ppermute(x, 'blk', to_even) for x in sent]  8.88 us
    ppermute x6, starting transfers between devices, body(): next_odd = [lax.ppermute(x, 'blk', to_odd) for x in sent]  8.71 us
    ppermute x6, starting transfers between devices, body(): next_even = [lax.ppermute(x, 'blk', to_even) for x in sent]  7.75 us
    all_to_all x1, waiting for transfers between devices, body(): lax.all_to_all(coded.reshape(n_blk, share, rank // 2), 'blk', split_axis=...  5.34 us
  transfers between devices with their start and end apart: 15, of which 7 were waited for; matrix products, arithmetic and copies ran while one was open for 0% of the time, Pallas kernels for 28%

commit v1 on v0

--- a/solution.py
+++ b/solution.py
@@ -24,7 +24,7 @@
 
 VM = pl.BlockSpec(memory_space=pltpu.VMEM)
 SM = pl.BlockSpec(memory_space=pltpu.SMEM)
-ANY = pl.BlockSpec(memory_space=pl.ANY)
+HBM = pl.BlockSpec(memory_space=pltpu.HBM)
 
 
 def params(limit=12):
@@ -87,11 +87,13 @@
     left_t[1] = lo_t
 
 
-def before_kernel(flags, order, content, weights, users, deal, partial, meta, left, left_t, rows, sem):
+def before_kernel(flags, order, content, weights, users, deal, partial, meta, left, left_t, rows, held, sems):
     n = order.shape[1]
     part = flags[0]
-    copy = pltpu.make_async_copy(content.at[pl.ds(pl.multiple_of(part * n, n), n), :], rows, sem)
+    copy = pltpu.make_async_copy(content.at[pl.ds(pl.multiple_of(part * n, n), n), :], rows, sems.at[0])
     copy.start()
+    users_copy = pltpu.make_async_copy(users, held, sems.at[1])
+    users_copy.start()
     column_sums = jnp.sum(jnp.abs(weights[...].astype(F32)), axis=0, keepdims=True)
     bound = jnp.maximum(jnp.max(column_sums, axis=1, keepdims=True) * (CONTENT_BOUND * 1.001), 1e-30)
     meta[...] = jnp.broadcast_to(bound, meta.shape)
@@ -100,7 +102,8 @@
         wide = jnp.broadcast_to(order[:, at:at + 128], (128, 128)).T
         picked = jnp.concatenate([wide] * (n // 128), axis=1) == lanes
         deal[at:at + 128, :] = jnp.where(picked, 1.0, 0.0).astype(BF16)
-    put_users(users[...], None, left, left_t)
+    users_copy.wait()
+    put_users(held[...], None, left, left_t)
     copy.wait()
     depth = content.shape[1]
     mine = weights[pl.ds(pl.multiple_of(part * depth, depth), depth), :]
@@ -119,9 +122,15 @@
     out[...] = pack(code[:, :mid], code[:, mid:])
 
 
-def ratings_kernel(ratings, *outs):
-    for t, out in enumerate(outs):
-        out[...] = ratings[:, t, :].astype(F32).astype(BF16)
+def ratings_kernel(ratings, out):
+    n, wide = out.shape
+    groups = wide // 128
+    for g in range(groups):
+        word = None
+        for t in reversed(range(ROUNDS)):
+            rows = ratings[pl.ds(g * ROUNDS + t, n, stride=groups * ROUNDS), :]
+            word = rows if word is None else lax.shift_left(word, 3) | rows
+        out[:, g * 128:(g + 1) * 128] = word.astype(jnp.int16)
 
 
 def encode(x):
@@ -140,13 +149,13 @@
     return jnp.concatenate([a, b], axis=0) * scale
 
 
-def errors_and_items(q, cols, left, left_t, values, err, right):
+def errors_and_items(q, cols, left, left_t, values, t, err, right):
     q_hi, q_lo = split(q)
     if right is not None:
         right[0, :, cols] = q_hi
         right[1, :, cols] = q_lo
     guess = mm(left[0], q_hi) + mm(left[0], q_lo) + mm(left[1], q_hi)
-    v = values[:, cols].astype(F32)
+    v = (lax.shift_right_logical(values[:, cols].astype(I32), 3 * t) & 7).astype(F32)
     e_hi, e_lo = split(jnp.where(v > 0, v - guess, 0.0))
     err[0, :, cols] = e_hi
     err[1, :, cols] = e_lo
@@ -168,7 +177,8 @@
     return refs[at // wide], slice(at % wide, at % wide + CHUNK)
 
 
-def push_kernel(turn, first, pieces, *refs):
+def push_kernel(turn, t, pieces, *refs):
+    first = t == 0
     flags, left, left_t, values = refs[:4]
     refs = refs[4:]
     if first:
@@ -190,7 +200,7 @@
             else:
                 ref, here = piece(got, at)
                 q = decode(ref[:, here], right.shape[1])
-            words, level = encode(errors_and_items(q, cols, left, left_t, values, err, right))
+            words, level = encode(errors_and_items(q, cols, left, left_t, values, t, err, right))
             rows = words.shape[0]
             ref, here = piece(outs, at)
             ref[:rows, here] = words
@@ -216,12 +226,13 @@
     odd = refs[EVEN_PIECES:EVEN_PIECES + ODD_PIECES]
     users_out, items_out, err, right = refs[EVEN_PIECES + ODD_PIECES:]
     is_odd = flags[1] == 1
+    t = ROUNDS - 1
     for at in range(0, values.shape[1], CHUNK):
         cols = slice(at, at + CHUNK)
         (a, at_a), (b, at_b) = piece(odd, at), piece(even, at)
         live = right.shape[1] // 2 + 8
         q = decode(jnp.where(is_odd, a[:live, at_a], b[:live, at_b]), right.shape[1])
-        items_out[cols, :] = errors_and_items(q, cols, left, left_t, values, err, right).T
+        items_out[cols, :] = errors_and_items(q, cols, left, left_t, values, t, err, right).T
     users_out[...] = user_step(users, err, right)
 
 
@@ -249,9 +260,13 @@
             struct((n_items, rank), F32),
             struct((8, 128), F32),
         ] + split_shapes,
-        in_specs=[SM, VM, ANY, VM, VM],
+        in_specs=[SM, VM, HBM, VM, HBM],
         out_specs=[VM] * 5,
-        scratch_shapes=[pltpu.VMEM((n_items, depth), BF16), pltpu.SemaphoreType.DMA],
+        scratch_shapes=[
+            pltpu.VMEM((n_items, depth), BF16),
+            pltpu.VMEM((n_users, rank), F32),
+            pltpu.SemaphoreType.DMA((2,)),
+        ],
         compiler_params=params(),
         cost_estimate=cost(2 * n_items * n_items * depth, 6 << 20),
         name="before",
@@ -270,13 +285,16 @@
     ).reshape(n_items, rank // 2)
     ratings, coded = lax.optimization_barrier((ratings, coded))
     rows = 64
+    groups = n_items // 128
+    ratings = ratings.reshape(n_users, ROUNDS, groups, 128).transpose(0, 2, 1, 3)
+    ratings = ratings.reshape(n_users * groups * ROUNDS, 128)
     values = pl.pallas_call(
         ratings_kernel,
-        out_shape=[struct((n_users, n_items), BF16)] * ROUNDS,
+        out_shape=struct((n_users, n_items), jnp.int16),
         grid=(n_users // rows,),
-        in_specs=[pl.BlockSpec((rows, ROUNDS, n_items), lambda i: (i, 0, 0))],
-        out_specs=[pl.BlockSpec((rows, n_items), lambda i: (i, 0))] * ROUNDS,
-        compiler_params=params(32),
+        in_specs=[pl.BlockSpec((rows * groups * ROUNDS, 128), lambda i: (i, 0))],
+        out_specs=pl.BlockSpec((rows, n_items), lambda i: (i, 0)),
+        compiler_params=params(52),
         cost_estimate=cost(1 << 20, 12 << 20),
         name="ratings",
     )(ratings)
@@ -284,14 +302,13 @@
     state_shapes = [struct((2, n_users, n_items), BF16), struct((2, rank, n_items), BF16)]
     round_cost = cost(2 * n_users * n_items * rank * 6, 6 << 20)
     to_even = [(i, (i + 1) % n_blk) for i in range(1, n_blk, 2)]
-    to_odd = [(i, i + 1) for i in range(0, n_blk, 2)]
+    to_odd = [(i, i ^ 1) for i in range(n_blk)]
 
     def push(turn, source, pieces, tail, flags=flags):
         sent_shapes = [struct((rank // 2 + tail, n_items // pieces), I32)] * pieces
-        first = len(source) == 2 and source[0].shape[0] == n_items
-        ins = [flags, left, left_t, values[t], *source]
+        ins = [flags, left, left_t, values, *source]
         got = pl.pallas_call(
-            functools.partial(push_kernel, turn, first, pieces),
+            functools.partial(push_kernel, turn, t, pieces),
             out_shape=state_shapes + sent_shapes,
             in_specs=[SM] + [VM] * (len(ins) - 1),
             out_specs=[VM] * (2 + pieces),
@@ -331,7 +348,7 @@
         compiler_params=params(),
         cost_estimate=round_cost,
         name="last",
-    )(flags, left, left_t, values[ROUNDS - 1], users, *for_even, *for_odd))
+    )(flags, left, left_t, values, users, *for_even, *for_odd))
 
 
 def solution(mesh):

time: 105 us -> 100 us (0.952)
  waiting for transfers between devices: 19.5 us -> 32.1 us
  local copies, waits for them, and re-layouts: 12.6 us -> 4.97 us
  starting transfers between devices: 33.7 us -> 27 us
  Pallas kernels: 37.6 us -> 34.7 us
    all_to_all x1, waiting for transfers between devices: 5.34 us -> 13.2 us  [body(): lax.all_to_all(coded.reshape(n_blk, share, rank // 2), 'blk', split_axis=...]
    unnamed x24 -> x10, local copies, waits for them, and re-layouts: 11.5 us -> 3.9 us
    ppermute x6, starting transfers between devices: 8.71 us -> 1.96 us  [body(): next_odd = [lax.ppermute(x, 'blk', to_odd) for x in sent]]
    ppermute x6, waiting for transfers between devices: 8.88 us -> 13.7 us  [body(): next_even = [lax.ppermute(x, 'blk', to_even) for x in sent]]
    pallas_call x7, Pallas kernels: 23 us -> 20.1 us  [the longest x6 11.8 us: push(): pl.pallas_call(functools.partial(push_kernel, turn, t, pieces), out_shape...]
  transfers between devices with their start and end apart: 15 -> 15, of which waited for: 7 -> 8; matrix products, arithmetic and copies ran while one was open for 0% -> 0% of each run, Pallas kernels for 28% -> 27%
where the time goes in v1:
time: 100 us; the launch traced here: 99.7 us
  Pallas kernels  34.7 us (35%)
  waiting for transfers between devices  32.1 us (32%)
  starting transfers between devices  27 us (27%)
  local copies, waits for them, and re-layouts  4.97 us (5%)
    all_to_all x1, starting transfers between devices, body(): lax.all_to_all(coded.reshape(n_blk, share, rank // 2), 'blk', split_axis=...  14.9 us
    ppermute x6, waiting for transfers between devices, body(): next_even = [lax.ppermute(x, 'blk', to_even) for x in sent]  13.7 us
    all_to_all x1, waiting for transfers between devices, body(): lax.all_to_all(coded.reshape(n_blk, share, rank // 2), 'blk', split_axis=...  13.2 us
    pallas_call x6, Pallas kernels, push(): pl.pallas_call(functools.partial(push_kernel, turn, t, pieces), out_shape...  11.8 us
    pallas_call x1, Pallas kernels, body(): pl.pallas_call(ratings_kernel, out_shape=struct((n_users, n_items), jnp.i...  8.24 us
    ppermute x6, starting transfers between devices, body(): next_even = [lax.ppermute(x, 'blk', to_even) for x in sent]  7.75 us
    ppermute x2, waiting for transfers between devices, body(): lax.ppermute(away[i * wide:(i + 1) * wide], 'cat', swap)  5.16 us
    pallas_call x3, Pallas kernels, body(): pl.pallas_call(pull_kernel, out_shape=[struct((n_users, rank), F32)] + sp...  5.01 us
  transfers between devices with their start and end apart: 15, of which 8 were waited for; matrix products, arithmetic and copies ran while one was open for 0% of the time, Pallas kernels for 27%

profile of v1, /device:TPU:8, one launch (start us, length us, event | category | flops | bytes accessed | tf_op | source)
XLA Modules:
  0.0 99.7 jit_solution(11361992864979328246)
XLA Ops:
  0.6 1.1 %constant_dynamic-slice_fusion.1 = (bf16[512,256]{1,0:T(8,128)(2,1)S(1)}, bf16[512,256]{1,0:T(8,128)(2,1)S(1)}) fusion(bf16[2048,256]{1,0:T(8,128)(2,1)} %content.1, s32[]{:T(128)S(6)} %add.5, s32[]{:T(128)S(6)} %select_n.3), kind=kLoop, calls=%fused_computation.2 | loop fusion | bytes 1048584 | tf_op jit(solution)/shard_map/slice | solution.py:254
  1.7 2.3 %collective-permute-start.1 = (bf16[512,256]{1,0:T(8,128)(2,1)S(1)}, bf16[512,256]{1,0:T(8,128)(2,1)S(1)}, u32[]{:S(2)}, u32[]{:S(2)}) collective-permute-start(bf16[512,256]{1,0:T(8,128)(2,1)S(1)} %get-tuple-element.86), channel_id=1, source_target_pairs={{0,1},{1,0},{2,3},{3,2},{4,5},{5,4},{6,7},{7,6},{8,9},{9,8},{10,11... | collective-permute-start | bytes 786440 | tf_op jit(solution)/shard_map/ppermute | solution.py:254
  4.2 1.0 %copy-done = f32[512,256]{1,0:T(8,128)S(1)} copy-done((f32[512,256]{1,0:T(8,128)S(1)}, f32[512,256]{1,0:T(8,128)}, u32[]{:S(2)}) %copy-start) | copy-done | bytes 524312
  5.2 1.2 %copy-done.2 = bf16[2048,256]{1,0:T(8,128)(2,1)S(1)} copy-done((bf16[2048,256]{1,0:T(8,128)(2,1)S(1)}, bf16[2048,256]{1,0:T(8,128)(2,1)}, u32[]{:S(2)}) %copy-start.2) | copy-done | bytes 1048600
  6.4 0.9 copy-done.3
  7.4 0.7 copy-done.4
  8.1 2.2 %before.1 = (bf16[1024,1024]{1,0:T(8,128)(2,1)S(1)}, f32[1024,256]{1,0:T(8,128)S(1)}, f32[8,128]{1,0:T(8,128)S(1)}, bf16[2,512,256]{2,1,0:T(8,128)(2,1)S(1)}, bf16[2,256,512]{2,1,0:T(8,128)(2,1)S(1)}) custom-call(s32[2]{0:T(128)S(1)} %pad_add_fusion.flags.refs_0_, s32[1,1024]{1,0:T(1,128)S(1)} %copy-done.4, bf16[2048,256]{1,0:T(8,128)(2,1)S(1)} %copy-done.2, ...), custom_call_target="tpu_custom_call" | custom-call | flops 536870912 | bytes 6291456 | tf_op jit(solution)/shard_map/before/pallas_call | solution.py:256
  10.3 0.9 collective-permute-done.1.second
  11.2 4.3 %collective-permute-done.first = bf16[512,256]{1,0:T(8,128)(2,1)S(1)} collective-permute-done((bf16[512,256]{1,0:T(8,128)(2,1)S(1)}, bf16[512,256]{1,0:T(8,128)(2,1)S(1)}, u32[]{:S(2)}, u32[]{:S(2)}) %collective-permute-start) | collective-permute-done | bytes 262176 | tf_op jit(solution)/shard_map/ppermute | solution.py:254
  15.5 2.5 %project.1 = s32[1024,128]{1,0:T(8,128)} custom-call(s32[2]{0:T(128)S(1)} %pad_add_fusion.flags.refs_0_, bf16[1024,1024]{1,0:T(8,128)(2,1)S(1)} %get-tuple-element.46.deal, bf16[512,256]{1,0:T(8,128)(2,1)S(1)} %collective-permute-done.first, bf16[512,256]{1,0:T(8,128)(2,1)S(1)} %collective-permute-done.1.second, bf16[512,256]{1,0:T(8,128)(2,1)S(1)} %copy-done.3, ...), custom_call_target="tpu_custom_call" | custom-call | flops 536870912 | bytes 4194304 | tf_op jit(solution)/shard_map/project/pallas_call | solution.py:274
  18.0 14.9 %all-to-all-start = ((s32[128,8,128]{2,1,0:T(8,128)}), s32[128,8,128]{2,1,0:T(8,128)S(1)}, u32[]{:S(2)}, u32[]{:S(2)}) async-start(s32[128,8,128]{2,1,0:T(8,128)} %bitcast.5), calls=%async_computation | async-start | bytes 1048576 | tf_op jit(solution)/shard_map/all_to_all | solution.py:283
  32.9 8.2 %ratings.1.refs_3_.values = s16[512,1024]{1,0:T(8,128)(2,1)S(1)} custom-call(s32[16384,128]{1,0:T(8,128)} %bitcast.11), custom_call_target="tpu_custom_call" | custom-call | flops 1048576 | bytes 12582912 | tf_op jit(solution)/shard_map/ratings/pallas_call | solution.py:291
  41.1 13.2 %all-to-all-done = s32[128,8,128]{2,1,0:T(8,128)S(1)} async-done(((s32[128,8,128]{2,1,0:T(8,128)}), s32[128,8,128]{2,1,0:T(8,128)S(1)}, u32[]{:S(2)}, u32[]{:S(2)}) %all-to-all-start) | async-done | bytes 524320 | tf_op jit(solution)/shard_map/all_to_all | solution.py:283
  54.9 1.3 %collective-permute-start.5 = (s32[144,512]{1,0:T(8,128)S(1)}, s32[144,512]{1,0:T(8,128)S(1)}, u32[]{:S(2)}, u32[]{:S(2)}) collective-permute-start(s32[144,512]{1,0:T(8,128)S(1)} %get-tuple-element.65), channel_id=1, source_target_pairs={{2,4},{6,8},{10,12},{14,16},{18,20},{22,24},{26,28},{30,32},{34,36... | collective-permute-start | bytes 884744 | tf_op jit(solution)/shard_map/ppermute | solution.py:325
  56.2 1.3 %collective-permute-start.4 = (s32[144,512]{1,0:T(8,128)S(1)}, s32[144,512]{1,0:T(8,128)S(1)}, u32[]{:S(2)}, u32[]{:S(2)}) collective-permute-start(s32[144,512]{1,0:T(8,128)S(1)} %get-tuple-element.52), channel_id=1, source_target_pairs={{2,4},{6,8},{10,12},{14,16},{18,20},{22,24},{26,28},{30,32},{34,36... | collective-permute-start | bytes 884744 | tf_op jit(solution)/shard_map/ppermute | solution.py:325
  57.5 3.5 %push.7 = (bf16[2,512,1024]{2,1,0:T(8,128)(2,1)S(1)}, bf16[2,256,1024]{2,1,0:T(8,128)(2,1)S(1)}, s32[136,512]{1,0:T(8,128)S(1)}, s32[136,512]{1,0:T(8,128)S(1)}) custom-call(s32[2]{0:T(128)S(1)} %pad_add_fusion.flags.refs_0_, bf16[2,512,256]{2,1,0:T(8,128)(2,1)S(1)} %get-tuple-element.44.refs_1_, bf16[2,256,512]{2,1,0:T(8,128)(2,1)S(1)} %get-tuple-element.45.refs_2_, ...), custom_call_target="tpu_custom_call" | custom-call | flops 1024 | bytes 1024 | tf_op jit(solution)/shard_map/push/pallas_call | solution.py:310
  61.8 1.7 %pull.3 = (f32[512,256]{1,0:T(8,128)S(1)}, bf16[2,512,256]{2,1,0:T(8,128)(2,1)S(1)}, bf16[2,256,512]{2,1,0:T(8,128)(2,1)S(1)}) custom-call(s32[2]{0:T(128)S(1)} %pad_add_fusion.flags.refs_0_, f32[512,256]{1,0:T(8,128)S(1)} %copy-done.1, bf16[2,512,1024]{2,1,0:T(8,128)(2,1)S(1)} %get-tuple-element.50.err_odd, ...), custom_call_target="tpu_custom_call" | custom-call | flops 1024 | bytes 1024 | tf_op jit(solution)/shard_map/pull/pallas_call | solution.py:329
  63.5 0.6 push.8
  64.1 1.3 %collective-permute-start.8 = (s32[144,512]{1,0:T(8,128)S(1)}, s32[144,512]{1,0:T(8,128)S(1)}, u32[]{:S(2)}, u32[]{:S(2)}) collective-permute-start(s32[144,512]{1,0:T(8,128)S(1)} %get-tuple-element.63), channel_id=1, source_target_pairs={{2,4},{6,8},{10,12},{14,16},{18,20},{22,24},{26,28},{30,32},{34,36... | collective-permute-start | bytes 884744 | tf_op jit(solution)/shard_map/ppermute | solution.py:325
  65.4 1.3 %collective-permute-start.9 = (s32[144,512]{1,0:T(8,128)S(1)}, s32[144,512]{1,0:T(8,128)S(1)}, u32[]{:S(2)}, u32[]{:S(2)}) collective-permute-start(s32[144,512]{1,0:T(8,128)S(1)} %get-tuple-element.77), channel_id=1, source_target_pairs={{2,4},{6,8},{10,12},{14,16},{18,20},{22,24},{26,28},{30,32},{34,36... | collective-permute-start | bytes 884744 | tf_op jit(solution)/shard_map/ppermute | solution.py:325
  66.7 2.0 %collective-permute-done.5.refs_5_ = s32[144,512]{1,0:T(8,128)S(1)} collective-permute-done((s32[144,512]{1,0:T(8,128)S(1)}, s32[144,512]{1,0:T(8,128)S(1)}, u32[]{:S(2)}, u32[]{:S(2)}) %collective-permute-start.5) | collective-permute-done | bytes 294944 | tf_op jit(solution)/shard_map/ppermute | solution.py:325
  68.6 3.2 %collective-permute-done.4.refs_4_ = s32[144,512]{1,0:T(8,128)S(1)} collective-permute-done((s32[144,512]{1,0:T(8,128)S(1)}, s32[144,512]{1,0:T(8,128)S(1)}, u32[]{:S(2)}, u32[]{:S(2)}) %collective-permute-start.4) | collective-permute-done | bytes 294944 | tf_op jit(solution)/shard_map/ppermute | solution.py:325
  71.8 3.2 %push.9 = (bf16[2,512,1024]{2,1,0:T(8,128)(2,1)S(1)}, bf16[2,256,1024]{2,1,0:T(8,128)(2,1)S(1)}, s32[136,512]{1,0:T(8,128)S(1)}, s32[136,512]{1,0:T(8,128)S(1)}) custom-call(s32[2]{0:T(128)S(1)} %pad_add_fusion.flags.refs_0_, bf16[2,512,256]{2,1,0:T(8,128)(2,1)S(1)} %get-tuple-element.57.refs_1_, bf16[2,256,512]{2,1,0:T(8,128)(2,1)S(1)} %get-tuple-element.58.refs_2_, ...), custom_call_target="tpu_custom_call" | custom-call | flops 1024 | bytes 1024 | tf_op jit(solution)/shard_map/push/pallas_call | solution.py:310
  75.6 1.7 %pull.4 = (f32[512,256]{1,0:T(8,128)S(1)}, bf16[2,512,256]{2,1,0:T(8,128)(2,1)S(1)}, bf16[2,256,512]{2,1,0:T(8,128)(2,1)S(1)}) custom-call(s32[2]{0:T(128)S(1)} %pad_add_fusion.flags.refs_0_, f32[512,256]{1,0:T(8,128)S(1)} %get-tuple-element.56.users, bf16[2,512,1024]{2,1,0:T(8,128)(2,1)S(1)} %get-tuple-element.61.err_odd, ...), custom_call_target="tpu_custom_call" | custom-call | flops 1024 | bytes 1024 | tf_op jit(solution)/shard_map/pull/pallas_call | solution.py:329
  77.3 0.6 push.10
  77.9 1.3 %collective-permute-start.11 = (s32[144,512]{1,0:T(8,128)S(1)}, s32[144,512]{1,0:T(8,128)S(1)}, u32[]{:S(2)}, u32[]{:S(2)}) collective-permute-start(s32[144,512]{1,0:T(8,128)S(1)} %get-tuple-element.83), channel_id=1, source_target_pairs={{2,4},{6,8},{10,12},{14,16},{18,20},{22,24},{26,28},{30,32},{34,36... | collective-permute-start | bytes 884744 | tf_op jit(solution)/shard_map/ppermute | solution.py:325
  79.2 1.3 %collective-permute-start.10 = (s32[144,512]{1,0:T(8,128)S(1)}, s32[144,512]{1,0:T(8,128)S(1)}, u32[]{:S(2)}, u32[]{:S(2)}) collective-permute-start(s32[144,512]{1,0:T(8,128)S(1)} %get-tuple-element.75), channel_id=1, source_target_pairs={{2,4},{6,8},{10,12},{14,16},{18,20},{22,24},{26,28},{30,32},{34,36... | collective-permute-start | bytes 884744 | tf_op jit(solution)/shard_map/ppermute | solution.py:325
  81.0 3.4 %push.11 = (bf16[2,512,1024]{2,1,0:T(8,128)(2,1)S(1)}, bf16[2,256,1024]{2,1,0:T(8,128)(2,1)S(1)}, s32[136,512]{1,0:T(8,128)S(1)}, s32[136,512]{1,0:T(8,128)S(1)}) custom-call(s32[2]{0:T(128)S(1)} %pad_add_fusion.flags.refs_0_, bf16[2,512,256]{2,1,0:T(8,128)(2,1)S(1)} %get-tuple-element.69.refs_1_, bf16[2,256,512]{2,1,0:T(8,128)(2,1)S(1)} %get-tuple-element.70.refs_2_, ...), custom_call_target="tpu_custom_call" | custom-call | flops 1024 | bytes 1024 | tf_op jit(solution)/shard_map/push/pallas_call | solution.py:310
  85.0 1.7 %pull.5 = (f32[512,256]{1,0:T(8,128)S(1)}, bf16[2,512,256]{2,1,0:T(8,128)(2,1)S(1)}, bf16[2,256,512]{2,1,0:T(8,128)(2,1)S(1)}) custom-call(s32[2]{0:T(128)S(1)} %pad_add_fusion.flags.refs_0_, f32[512,256]{1,0:T(8,128)S(1)} %get-tuple-element.68.users, bf16[2,512,1024]{2,1,0:T(8,128)(2,1)S(1)} %get-tuple-element.73.err_odd, ...), custom_call_target="tpu_custom_call" | custom-call | flops 1024 | bytes 1024 | tf_op jit(solution)/shard_map/pull/pallas_call | solution.py:329
  86.7 4.9 %collective-permute-done.11.refs_1_ = s32[144,512]{1,0:T(8,128)S(1)} collective-permute-done((s32[144,512]{1,0:T(8,128)S(1)}, s32[144,512]{1,0:T(8,128)S(1)}, u32[]{:S(2)}, u32[]{:S(2)}) %collective-permute-start.11) | collective-permute-done | bytes 294944 | tf_op jit(solution)/shard_map/ppermute | solution.py:325
  91.6 3.2 %collective-permute-done.10.refs_0_ = s32[144,512]{1,0:T(8,128)S(1)} collective-permute-done((s32[144,512]{1,0:T(8,128)S(1)}, s32[144,512]{1,0:T(8,128)S(1)}, u32[]{:S(2)}, u32[]{:S(2)}) %collective-permute-start.10) | collective-permute-done | bytes 294944 | tf_op jit(solution)/shard_map/ppermute | solution.py:325
  94.8 4.9 %last.1 = (f32[512,256]{1,0:T(8,128)}, f32[1024,256]{1,0:T(8,128)}) custom-call(s32[2]{0:T(128)S(1)} %pad_add_fusion.flags.refs_0_, bf16[2,512,256]{2,1,0:T(8,128)(2,1)S(1)} %get-tuple-element.80.left, bf16[2,256,512]{2,1,0:T(8,128)(2,1)S(1)} %get-tuple-element.81.left_t, s16[512,1024]{1,0:T(8,128)(2,1)S(1)} %ratings.1.refs_3_.values, ...), custom_call_target="tpu_custom_call" | custom-call | flops 1610612736 | bytes 6291456 | tf_op jit(solution)/shard_map/last/pallas_call | solution.py:339
  (23 shorter events, 3.2 us)
Async XLA Ops:
  1.7 9.5 %collective-permute-start.1 = (bf16[512,256]{1,0:T(8,128)(2,1)S(1)}, bf16[512,256]{1,0:T(8,128)(2,1)S(1)}, u32[]{:S(2)}, u32[]{:S(2)}) collective-permute-start(bf16[512,256]{1,0:T(8,128)(2,1)S(1)} %get-tuple-element.86), channel_id=1, source_target_pairs={{0,1},{1,0},{2,3},{3,2},{4,5},{5,4},{6,7},{7,6},{8,9},{9,8},{10,11... | collective-permute-start | bytes 786440 | tf_op jit(solution)/shard_map/ppermute | solution.py:254
  4.0 11.5 %collective-permute-start = (bf16[512,256]{1,0:T(8,128)(2,1)S(1)}, bf16[512,256]{1,0:T(8,128)(2,1)S(1)}, u32[]{:S(2)}, u32[]{:S(2)}) collective-permute-start(bf16[512,256]{1,0:T(8,128)(2,1)S(1)} %get-tuple-element.87), channel_id=1, source_target_pairs={{0,1},{1,0},{2,3},{3,2},{4,5},{5,4},{6,7},{7,6},{8,9},{9,8},{10,11... | collective-permute-start | bytes 786440 | tf_op jit(solution)/shard_map/ppermute | solution.py:254
  4.2 1.0 %copy-start = (f32[512,256]{1,0:T(8,128)S(1)}, f32[512,256]{1,0:T(8,128)}, u32[]{:S(2)}) copy-start(f32[512,256]{1,0:T(8,128)} %users.3) | copy-start | bytes 1572868
  5.2 1.2 %copy-start.2 = (bf16[2048,256]{1,0:T(8,128)(2,1)S(1)}, bf16[2048,256]{1,0:T(8,128)(2,1)}, u32[]{:S(2)}) copy-start(bf16[2048,256]{1,0:T(8,128)(2,1)} %content.1) | copy-start | bytes 3145732
  6.4 0.9 copy-start.3
  7.4 0.7 copy-start.4
  18.0 36.3 %all-to-all-start = ((s32[128,8,128]{2,1,0:T(8,128)}), s32[128,8,128]{2,1,0:T(8,128)S(1)}, u32[]{:S(2)}, u32[]{:S(2)}) async-start(s32[128,8,128]{2,1,0:T(8,128)} %bitcast.5), calls=%async_computation | async-start | bytes 1048576 | tf_op jit(solution)/shard_map/all_to_all | solution.py:283
  54.3 7.5 %copy-start.1 = (f32[512,256]{1,0:T(8,128)S(1)}, f32[512,256]{1,0:T(8,128)}, u32[]{:S(2)}) copy-start(f32[512,256]{1,0:T(8,128)} %users.3) | copy-start | bytes 1572868
  54.9 13.8 %collective-permute-start.5 = (s32[144,512]{1,0:T(8,128)S(1)}, s32[144,512]{1,0:T(8,128)S(1)}, u32[]{:S(2)}, u32[]{:S(2)}) collective-permute-start(s32[144,512]{1,0:T(8,128)S(1)} %get-tuple-element.65), channel_id=1, source_target_pairs={{2,4},{6,8},{10,12},{14,16},{18,20},{22,24},{26,28},{30,32},{34,36... | collective-permute-start | bytes 884744 | tf_op jit(solution)/shard_map/ppermute | solution.py:325
  56.2 15.6 %collective-permute-start.4 = (s32[144,512]{1,0:T(8,128)S(1)}, s32[144,512]{1,0:T(8,128)S(1)}, u32[]{:S(2)}, u32[]{:S(2)}) collective-permute-start(s32[144,512]{1,0:T(8,128)S(1)} %get-tuple-element.52), channel_id=1, source_target_pairs={{2,4},{6,8},{10,12},{14,16},{18,20},{22,24},{26,28},{30,32},{34,36... | collective-permute-start | bytes 884744 | tf_op jit(solution)/shard_map/ppermute | solution.py:325
  61.0 2.5 %collective-permute-start.2 = (s32[136,512]{1,0:T(8,128)S(1)}, s32[136,512]{1,0:T(8,128)S(1)}, u32[]{:S(2)}, u32[]{:S(2)}) collective-permute-start(s32[136,512]{1,0:T(8,128)S(1)} %get-tuple-element.59), channel_id=1, source_target_pairs={{0,2},{2,0},{4,6},{6,4},{8,10},{10,8},{12,14},{14,12},{16,18},{18,... | collective-permute-start | bytes 835592 | tf_op jit(solution)/shard_map/ppermute | solution.py:328
  61.5 1.9 %collective-permute-start.3 = (s32[136,512]{1,0:T(8,128)S(1)}, s32[136,512]{1,0:T(8,128)S(1)}, u32[]{:S(2)}, u32[]{:S(2)}) collective-permute-start(s32[136,512]{1,0:T(8,128)S(1)} %get-tuple-element.60), channel_id=1, source_target_pairs={{0,2},{2,0},{4,6},{6,4},{8,10},{10,8},{12,14},{14,12},{16,18},{18,... | collective-permute-start | bytes 835592 | tf_op jit(solution)/shard_map/ppermute | solution.py:328
  64.1 16.9 %collective-permute-start.8 = (s32[144,512]{1,0:T(8,128)S(1)}, s32[144,512]{1,0:T(8,128)S(1)}, u32[]{:S(2)}, u32[]{:S(2)}) collective-permute-start(s32[144,512]{1,0:T(8,128)S(1)} %get-tuple-element.63), channel_id=1, source_target_pairs={{2,4},{6,8},{10,12},{14,16},{18,20},{22,24},{26,28},{30,32},{34,36... | collective-permute-start | bytes 884744 | tf_op jit(solution)/shard_map/ppermute | solution.py:325
  65.4 15.6 %collective-permute-start.9 = (s32[144,512]{1,0:T(8,128)S(1)}, s32[144,512]{1,0:T(8,128)S(1)}, u32[]{:S(2)}, u32[]{:S(2)}) collective-permute-start(s32[144,512]{1,0:T(8,128)S(1)} %get-tuple-element.77), channel_id=1, source_target_pairs={{2,4},{6,8},{10,12},{14,16},{18,20},{22,24},{26,28},{30,32},{34,36... | collective-permute-start | bytes 884744 | tf_op jit(solution)/shard_map/ppermute | solution.py:325
  75.0 2.3 %collective-permute-start.6 = (s32[136,512]{1,0:T(8,128)S(1)}, s32[136,512]{1,0:T(8,128)S(1)}, u32[]{:S(2)}, u32[]{:S(2)}) collective-permute-start(s32[136,512]{1,0:T(8,128)S(1)} %get-tuple-element.71), channel_id=1, source_target_pairs={{0,2},{2,0},{4,6},{6,4},{8,10},{10,8},{12,14},{14,12},{16,18},{18,... | collective-permute-start | bytes 835592 | tf_op jit(solution)/shard_map/ppermute | solution.py:328
  75.1 2.2 %collective-permute-start.7 = (s32[136,512]{1,0:T(8,128)S(1)}, s32[136,512]{1,0:T(8,128)S(1)}, u32[]{:S(2)}, u32[]{:S(2)}) collective-permute-start(s32[136,512]{1,0:T(8,128)S(1)} %get-tuple-element.72), channel_id=1, source_target_pairs={{0,2},{2,0},{4,6},{6,4},{8,10},{10,8},{12,14},{14,12},{16,18},{18,... | collective-permute-start | bytes 835592 | tf_op jit(solution)/shard_map/ppermute | solution.py:328
  77.9 13.8 %collective-permute-start.11 = (s32[144,512]{1,0:T(8,128)S(1)}, s32[144,512]{1,0:T(8,128)S(1)}, u32[]{:S(2)}, u32[]{:S(2)}) collective-permute-start(s32[144,512]{1,0:T(8,128)S(1)} %get-tuple-element.83), channel_id=1, source_target_pairs={{2,4},{6,8},{10,12},{14,16},{18,20},{22,24},{26,28},{30,32},{34,36... | collective-permute-start | bytes 884744 | tf_op jit(solution)/shard_map/ppermute | solution.py:325
  79.2 15.6 %collective-permute-start.10 = (s32[144,512]{1,0:T(8,128)S(1)}, s32[144,512]{1,0:T(8,128)S(1)}, u32[]{:S(2)}, u32[]{:S(2)}) collective-permute-start(s32[144,512]{1,0:T(8,128)S(1)} %get-tuple-element.75), channel_id=1, source_target_pairs={{2,4},{6,8},{10,12},{14,16},{18,20},{22,24},{26,28},{30,32},{34,36... | collective-permute-start | bytes 884744 | tf_op jit(solution)/shard_map/ppermute | solution.py:325
  84.4 2.3 %collective-permute-start.12 = (s32[136,512]{1,0:T(8,128)S(1)}, s32[136,512]{1,0:T(8,128)S(1)}, u32[]{:S(2)}, u32[]{:S(2)}) collective-permute-start(s32[136,512]{1,0:T(8,128)S(1)} %get-tuple-element.84), channel_id=1, source_target_pairs={{0,2},{2,0},{4,6},{6,4},{8,10},{10,8},{12,14},{14,12},{16,18},{18,... | collective-permute-start | bytes 835592 | tf_op jit(solution)/shard_map/ppermute | solution.py:328
  84.5 2.2 %collective-permute-start.13 = (s32[136,512]{1,0:T(8,128)S(1)}, s32[136,512]{1,0:T(8,128)S(1)}, u32[]{:S(2)}, u32[]{:S(2)}) collective-permute-start(s32[136,512]{1,0:T(8,128)S(1)} %get-tuple-element.85), channel_id=1, source_target_pairs={{0,2},{2,0},{4,6},{6,4},{8,10},{10,8},{12,14},{14,12},{16,18},{18,... | collective-permute-start | bytes 835592 | tf_op jit(solution)/shard_map/ppermute | solution.py:328

commit v2 on v1

--- a/solution.py
+++ b/solution.py
@@ -23,7 +23,6 @@
 I32 = jnp.int32
 
 VM = pl.BlockSpec(memory_space=pltpu.VMEM)
-SM = pl.BlockSpec(memory_space=pltpu.SMEM)
 HBM = pl.BlockSpec(memory_space=pltpu.HBM)
 
 
@@ -87,9 +86,9 @@
     left_t[1] = lo_t
 
 
-def before_kernel(flags, order, content, weights, users, deal, partial, meta, left, left_t, rows, held, sems):
+def before_kernel(order, content, weights, users, deal, partial, meta, left, left_t, rows, held, sems):
     n = order.shape[1]
-    part = flags[0]
+    part = lax.axis_index("cat")
     copy = pltpu.make_async_copy(content.at[pl.ds(pl.multiple_of(part * n, n), n), :], rows, sems.at[0])
     copy.start()
     users_copy = pltpu.make_async_copy(users, held, sems.at[1])
@@ -110,8 +109,8 @@
     partial[...] = mm(mm(deal[...], rows[...]).astype(BF16), mine)
 
 
-def project_kernel(flags, deal, first, second, weights, partial, meta, out):
-    other = 1 - flags[0]
+def project_kernel(deal, first, second, weights, partial, meta, out):
+    other = 1 - lax.axis_index("cat")
     depth = first.shape[1]
     half = first.shape[0]
     theirs = weights[pl.ds(pl.multiple_of(other * depth, depth), depth), :]
@@ -177,10 +176,14 @@
     return refs[at // wide], slice(at % wide, at % wide + CHUNK)
 
 
+def my_turn(turn):
+    return lax.rem(lax.axis_index("blk"), 2) == turn
+
+
 def push_kernel(turn, t, pieces, *refs):
     first = t == 0
-    flags, left, left_t, values = refs[:4]
-    refs = refs[4:]
+    left, left_t, values = refs[:3]
+    refs = refs[3:]
     if first:
         dealt, meta = refs[:2]
         refs = refs[2:]
@@ -191,7 +194,7 @@
     outs = refs[2:]
     n = values.shape[1]
 
-    @pl.when(flags[1] == turn)
+    @pl.when(my_turn(turn))
     def _():
         for at in range(0, n, CHUNK):
             cols = slice(at, at + CHUNK)
@@ -207,33 +210,48 @@
             ref[rows:, here] = jnp.broadcast_to(level, (ref.shape[0] - rows, CHUNK))
 
 
-def user_step(users, err, right):
+def user_step(users, err, right, rows=slice(None)):
     dims = ((1,), (1,))
-    grad = mm(err[0], right[0], dims) + mm(err[0], right[1], dims) + mm(err[1], right[0], dims)
-    return KEEP * users[...] + learn_rate * grad
-
-
-def pull_kernel(flags, users, err_odd, right_odd, err_even, right_even, new_users, left, left_t):
-    for turn, err, right in ((1, err_odd, right_odd), (0, err_even, right_even)):
-
-        @pl.when(flags[1] == turn)
+    hi, lo = err[0, rows, :], err[1, rows, :]
+    grad = mm(hi, right[0], dims) + mm(hi, right[1], dims) + mm(lo, right[0], dims)
+    return KEEP * users[rows, :] + learn_rate * grad
+
+
+def pull_kernel(turn, users, err, right, new_users, left, left_t):
+    @pl.when(my_turn(turn))
+    def _():
+        put_users(user_step(users, err, right), new_users, left, left_t)
+
+
+def last_kernel(pieces, *refs):
+    odd, even = refs[:3], refs[3:6]
+    values = refs[6]
+    refs = refs[7:]
+    to_odd, to_even = refs[:pieces[0]], refs[pieces[0]:sum(pieces)]
+    users_out, items_out, err, right, users_held, items_held, sems = refs[sum(pieces):]
+    n = values.shape[1]
+    tall = users_held.shape[0] // 2
+
+    for turn, (left, left_t, users), got in ((1, odd, to_odd), (0, even, to_even)):
+
+        @pl.when(my_turn(turn))
         def _():
-            put_users(user_step(users, err, right), new_users, left, left_t)
-
-
-def last_kernel(flags, left, left_t, values, users, *refs):
-    even = refs[:EVEN_PIECES]
-    odd = refs[EVEN_PIECES:EVEN_PIECES + ODD_PIECES]
-    users_out, items_out, err, right = refs[EVEN_PIECES + ODD_PIECES:]
-    is_odd = flags[1] == 1
-    t = ROUNDS - 1
-    for at in range(0, values.shape[1], CHUNK):
-        cols = slice(at, at + CHUNK)
-        (a, at_a), (b, at_b) = piece(odd, at), piece(even, at)
-        live = right.shape[1] // 2 + 8
-        q = decode(jnp.where(is_odd, a[:live, at_a], b[:live, at_b]), right.shape[1])
-        items_out[cols, :] = errors_and_items(q, cols, left, left_t, values, t, err, right).T
-    users_out[...] = user_step(users, err, right)
+            copies = []
+            for at in range(0, n, CHUNK):
+                cols = slice(at, at + CHUNK)
+                ref, here = piece(got, at)
+                q = decode(ref[:, here], right.shape[1])
+                new = errors_and_items(q, cols, left, left_t, values, ROUNDS - 1, err, right)
+                items_held[cols, :] = new.T
+                copies.append(pltpu.make_async_copy(items_held.at[cols, :], items_out.at[cols, :], sems.at[len(copies)]))
+                copies[-1].start()
+            for at in (0, tall):
+                rows = slice(at, at + tall)
+                users_held[rows, :] = user_step(users, err, right, rows)
+                copies.append(pltpu.make_async_copy(users_held.at[rows, :], users_out.at[rows, :], sems.at[len(copies)]))
+                copies[-1].start()
+            for copy in copies:
+                copy.wait()
 
 
 def struct(shape, dtype):
@@ -247,43 +265,9 @@
     share = n_items // n_blk
     wide = n_items // 2
     part = lax.axis_index("cat")
-    place = lax.axis_index("blk")
-    flags = jnp.stack([part, lax.rem(place, 2)]).astype(I32)
     swap = [(0, 1), (1, 0)]
     away = lax.dynamic_slice_in_dim(item_content, (1 - part) * n_items, n_items, axis=0)
     came = [lax.ppermute(away[i * wide:(i + 1) * wide], "cat", swap) for i in range(2)]
-    split_shapes = [struct((2, n_users, rank), BF16), struct((2, rank, n_users), BF16)]
-    deal, partial, meta, left, left_t = pl.pallas_call(
-        before_kernel,
-        out_shape=[
-            struct((n_items, n_items), BF16),
-            struct((n_items, rank), F32),
-            struct((8, 128), F32),
-        ] + split_shapes,
-        in_specs=[SM, VM, HBM, VM, HBM],
-        out_specs=[VM] * 5,
-        scratch_shapes=[
-            pltpu.VMEM((n_items, depth), BF16),
-            pltpu.VMEM((n_users, rank), F32),
-            pltpu.SemaphoreType.DMA((2,)),
-        ],
-        compiler_params=params(),
-        cost_estimate=cost(2 * n_items * n_items * depth, 6 << 20),
-        name="before",
-    )(flags, send_order, item_content, projection, user_factors)
-    coded = pl.pallas_call(
-        project_kernel,
-        out_shape=struct((n_items, rank // 2), I32),
-        in_specs=[SM] + [VM] * 6,
-        out_specs=VM,
-        compiler_params=params(),
-        cost_estimate=cost(2 * n_items * n_items * depth, 4 << 20),
-        name="project",
-    )(flags, deal, came[0], came[1], projection, partial, meta)
-    dealt = lax.all_to_all(
-        coded.reshape(n_blk, share, rank // 2), "blk", split_axis=0, concat_axis=0, tiled=True
-    ).reshape(n_items, rank // 2)
-    ratings, coded = lax.optimization_barrier((ratings, coded))
     rows = 64
     groups = n_items // 128
     ratings = ratings.reshape(n_users, ROUNDS, groups, 128).transpose(0, 2, 1, 3)
@@ -298,57 +282,100 @@
         cost_estimate=cost(1 << 20, 12 << 20),
         name="ratings",
     )(ratings)
+    send_order, values = lax.optimization_barrier((send_order, values))
+    split_shapes = [struct((2, n_users, rank), BF16), struct((2, rank, n_users), BF16)]
+    deal, partial, meta, left, left_t = pl.pallas_call(
+        before_kernel,
+        out_shape=[
+            struct((n_items, n_items), BF16),
+            struct((n_items, rank), F32),
+            struct((8, 128), F32),
+        ] + split_shapes,
+        in_specs=[VM, HBM, VM, HBM],
+        out_specs=[VM] * 5,
+        scratch_shapes=[
+            pltpu.VMEM((n_items, depth), BF16),
+            pltpu.VMEM((n_users, rank), F32),
+            pltpu.SemaphoreType.DMA((2,)),
+        ],
+        compiler_params=params(),
+        cost_estimate=cost(2 * n_items * n_items * depth, 6 << 20),
+        name="before",
+    )(send_order, item_content, projection, user_factors)
+    coded = pl.pallas_call(
+        project_kernel,
+        out_shape=struct((n_items, rank // 2), I32),
+        in_specs=[VM] * 6,
+        out_specs=VM,
+        compiler_params=params(),
+        cost_estimate=cost(2 * n_items * n_items * depth, 4 << 20),
+        name="project",
+    )(deal, came[0], came[1], projection, partial, meta)
+    dealt = lax.all_to_all(
+        coded.reshape(n_blk, share, rank // 2), "blk", split_axis=0, concat_axis=0, tiled=True
+    ).reshape(n_items, rank // 2)
 
     state_shapes = [struct((2, n_users, n_items), BF16), struct((2, rank, n_items), BF16)]
-    round_cost = cost(2 * n_users * n_items * rank * 6, 6 << 20)
     to_even = [(i, (i + 1) % n_blk) for i in range(1, n_blk, 2)]
     to_odd = [(i, i ^ 1) for i in range(n_blk)]
-
-    def push(turn, source, pieces, tail, flags=flags):
+    light = cost(1 << 10, 1 << 10)
+
+    def push(turn, t, left, left_t, source, pieces, tail):
         sent_shapes = [struct((rank // 2 + tail, n_items // pieces), I32)] * pieces
-        ins = [flags, left, left_t, values, *source]
         got = pl.pallas_call(
             functools.partial(push_kernel, turn, t, pieces),
             out_shape=state_shapes + sent_shapes,
-            in_specs=[SM] + [VM] * (len(ins) - 1),
+            in_specs=[VM] * (3 + len(source)),
             out_specs=[VM] * (2 + pieces),
             compiler_params=params(),
-            cost_estimate=cost(1 << 10, 1 << 10),
+            cost_estimate=light,
             name="push",
-        )(*ins)
+        )(left, left_t, values, *source)
         return got[:2], got[2:]
 
-    users = user_factors
-    for_odd = for_even = [dealt, meta]
-    for t in range(ROUNDS - 1):
-        state_odd, sent = push(1, for_odd, EVEN_PIECES, EVEN_TAIL)
-        next_even = [lax.ppermute(x, "blk", to_even) for x in sent]
-        later, _ = lax.optimization_barrier((flags, sent[0]))
-        state_even, sent = push(0, for_even, ODD_PIECES, ODD_TAIL, later)
-        next_odd = [lax.ppermute(x, "blk", to_odd) for x in sent]
-        users, left, left_t = pl.pallas_call(
-            pull_kernel,
+    def pull(turn, users, state):
+        return pl.pallas_call(
+            functools.partial(pull_kernel, turn),
             out_shape=[struct((n_users, rank), F32)] + split_shapes,
-            in_specs=[SM] + [VM] * 5,
+            in_specs=[VM] * 3,
             out_specs=[VM] * 3,
             compiler_params=params(),
-            cost_estimate=cost(1 << 10, 1 << 10),
+            cost_estimate=light,
             name="pull",
-        )(flags, users, *state_odd, *state_even)
+        )(users, *state)
+
+    odd = even = (user_factors, left, left_t)
+    for_odd = for_even = [dealt, meta]
+    state_even = None
+    for t in range(ROUNDS - 1):
+        state_odd, sent = push(1, t, *odd[1:], for_odd, EVEN_PIECES, EVEN_TAIL)
+        next_even = [lax.ppermute(x, "blk", to_even) for x in sent]
+        if state_even is not None:
+            users, _ = lax.optimization_barrier((even[0], sent[0]))
+            even = pull(0, users, state_even)
+        else:
+            even = (even[0], lax.optimization_barrier((even[1], sent[0]))[0], even[2])
+        state_even, sent = push(0, t, *even[1:], for_even, ODD_PIECES, ODD_TAIL)
+        next_odd = [lax.ppermute(x, "blk", to_odd) for x in sent]
+        odd = pull(1, odd[0], state_odd)
         for_even, for_odd = next_even, next_odd
+    even = pull(0, even[0], state_even)
     return tuple(pl.pallas_call(
-        last_kernel,
+        functools.partial(last_kernel, (ODD_PIECES, EVEN_PIECES)),
         out_shape=[struct((n_users, rank), F32), struct((n_items, rank), F32)],
-        in_specs=[SM] + [VM] * (4 + EVEN_PIECES + ODD_PIECES),
-        out_specs=[VM] * 2,
+        in_specs=[VM] * (7 + EVEN_PIECES + ODD_PIECES),
+        out_specs=[pl.BlockSpec(memory_space=pl.ANY)] * 2,
         scratch_shapes=[
             pltpu.VMEM((2, n_users, n_items), BF16),
             pltpu.VMEM((2, rank, n_items), BF16),
+            pltpu.VMEM((n_users, rank), F32),
+            pltpu.VMEM((n_items, rank), F32),
+            pltpu.SemaphoreType.DMA((n_items // CHUNK + 2,)),
         ],
-        compiler_params=params(),
-        cost_estimate=round_cost,
+        compiler_params=params(16),
+        cost_estimate=light,
         name="last",
-    )(flags, left, left_t, values, users, *for_even, *for_odd))
+    )(odd[1], odd[2], odd[0], even[1], even[2], even[0], values, *for_odd, *for_even))
 
 
 def solution(mesh):

time: 100 us -> 95.8 us (0.958)
  blocking collectives: 0 us -> 36.1 us
  starting transfers between devices: 27 us -> 12 us
  waiting for transfers between devices: 32.1 us -> 18 us
  Pallas kernels: 34.7 us -> 27.2 us
  local copies, waits for them, and re-layouts: 4.97 us -> 1.08 us
    all_to_all x0 -> x1, blocking collectives: none -> 36.1 us  [body(): lax.all_to_all(coded.reshape(n_blk, share, rank // 2), 'blk', split_axis=...]
    all_to_all x1 -> x0, starting transfers between devices: 14.9 us -> none  [body(): lax.all_to_all(coded.reshape(n_blk, share, rank // 2), 'blk', split_axis=...]
    all_to_all x1 -> x0, waiting for transfers between devices: 13.2 us -> none  [body(): lax.all_to_all(coded.reshape(n_blk, share, rank // 2), 'blk', split_axis=...]
    ppermute x2, waiting for transfers between devices: 5.16 us -> 1.22 us  [body(): lax.ppermute(away[i * wide:(i + 1) * wide], 'cat', swap)]
    unnamed x10 -> x8, local copies, waits for them, and re-layouts: 3.9 us -> 0.01 us
    pallas_call x6, Pallas kernels: 11.8 us -> 8.49 us  [push(): pl.pallas_call(functools.partial(push_kernel, turn, t, pieces), out_shape...]
    ppermute x6, waiting for transfers between devices: 0.02 us -> 3.2 us  [body(): next_odd = [lax.ppermute(x, 'blk', to_odd) for x in sent]]
    pallas_call x4 -> x7, Pallas kernels: 9.91 us -> 7.47 us  [the longest x1 4.09 us: body(): pl.pallas_call(functools.partial(last_kernel, (ODD_PIECES, EVEN_PIECES)),...]
  transfers between devices with their start and end apart: 15 -> 14, of which waited for: 8 -> 10; matrix products, arithmetic and copies ran while one was open for 0% -> 0% of each run, Pallas kernels for 27% -> 23%
where the time goes in v2:
time: 95.8 us; the launch traced here: 95.5 us
  blocking collectives  36.1 us (38%)
  Pallas kernels  27.2 us (28%)
  waiting for transfers between devices  18 us (19%)
  starting transfers between devices  12 us (13%)
  local copies, waits for them, and re-layouts  1.08 us (1%)
  between operations  1.03 us (1%)
    all_to_all x1, blocking collectives, body(): lax.all_to_all(coded.reshape(n_blk, share, rank // 2), 'blk', split_axis=...  36.1 us
    ppermute x6, waiting for transfers between devices, body(): next_even = [lax.ppermute(x, 'blk', to_even) for x in sent]  13.5 us
    pallas_call x6, Pallas kernels, push(): pl.pallas_call(functools.partial(push_kernel, turn, t, pieces), out_shape...  8.49 us
    pallas_call x1, Pallas kernels, body(): pl.pallas_call(ratings_kernel, out_shape=struct((n_users, n_items), jnp.i...  8.38 us
    ppermute x6, starting transfers between devices, body(): next_even = [lax.ppermute(x, 'blk', to_even) for x in sent]  7.72 us
    pallas_call x1, Pallas kernels, body(): pl.pallas_call(functools.partial(last_kernel, (ODD_PIECES, EVEN_PIECES)),...  4.09 us
    pallas_call x6, Pallas kernels, pull(): pl.pallas_call(functools.partial(pull_kernel, turn), out_shape=[struct((n...  3.38 us
    ppermute x6, waiting for transfers between devices, body(): next_odd = [lax.ppermute(x, 'blk', to_odd) for x in sent]  3.2 us
  transfers between devices with their start and end apart: 14, of which 10 were waited for; matrix products, arithmetic and copies ran while one was open for 0% of the time, Pallas kernels for 23%

profile of v2, /device:TPU:8, one launch (start us, length us, event | category | flops | bytes accessed | tf_op | source)
XLA Modules:
  0.0 95.5 jit_solution(14733255651812020195)
XLA Ops:
  0.6 1.1 %constant_dynamic-slice_fusion.1 = (bf16[512,256]{1,0:T(8,128)(2,1)S(1)}, bf16[512,256]{1,0:T(8,128)(2,1)S(1)}) fusion(bf16[2048,256]{1,0:T(8,128)(2,1)} %content.1, s32[]{:T(128)S(6)} %add.4, s32[]{:T(128)S(6)} %select_n.3), kind=kLoop, calls=%fused_computation.1 | loop fusion | bytes 1048584 | tf_op jit(solution)/shard_map/slice | solution.py:270
  1.7 2.3 %collective-permute-start.1 = (bf16[512,256]{1,0:T(8,128)(2,1)S(1)}, bf16[512,256]{1,0:T(8,128)(2,1)S(1)}, u32[]{:S(2)}, u32[]{:S(2)}) collective-permute-start(bf16[512,256]{1,0:T(8,128)(2,1)S(1)} %get-tuple-element.106), channel_id=1, source_target_pairs={{0,1},{1,0},{2,3},{3,2},{4,5},{5,4},{6,7},{7,6},{8,9},{9,8},{10,11... | collective-permute-start | bytes 786440 | tf_op jit(solution)/shard_map/ppermute | solution.py:270
  4.1 8.4 %ratings.1.refs_2_.refs_6_ = s16[512,1024]{1,0:T(8,128)(2,1)S(1)} custom-call(s32[16384,128]{1,0:T(8,128)} %bitcast.10), custom_call_target="tpu_custom_call" | custom-call | flops 1048576 | bytes 12582912 | tf_op jit(solution)/shard_map/ratings/pallas_call | solution.py:275
  12.5 1.7 %before.1 = (bf16[1024,1024]{1,0:T(8,128)(2,1)S(1)}, f32[1024,256]{1,0:T(8,128)S(1)}, f32[8,128]{1,0:T(8,128)S(1)}, bf16[2,512,256]{2,1,0:T(8,128)(2,1)S(1)}, bf16[2,256,512]{2,1,0:T(8,128)(2,1)S(1)}) custom-call(s32[1,1024]{1,0:T(1,128)S(1)} %copy-done.3, bf16[2048,256]{1,0:T(8,128)(2,1)S(1)} %copy-done.2, bf16[512,256]{1,0:T(8,128)(2,1)S(1)} %copy-done.1, ...), custom_call_target="tpu_custom_call" | custom-call | flops 536870912 | bytes 6291456 | tf_op jit(solution)/shard_map/before/pallas_call | solution.py:287
  14.2 1.2 %collective-permute-done.first = bf16[512,256]{1,0:T(8,128)(2,1)S(1)} collective-permute-done((bf16[512,256]{1,0:T(8,128)(2,1)S(1)}, bf16[512,256]{1,0:T(8,128)(2,1)S(1)}, u32[]{:S(2)}, u32[]{:S(2)}) %collective-permute-start) | collective-permute-done | bytes 262176 | tf_op jit(solution)/shard_map/ppermute | solution.py:270
  15.5 1.2 %project.1 = s32[1024,128]{1,0:T(8,128)S(1)} custom-call(bf16[1024,1024]{1,0:T(8,128)(2,1)S(1)} %get-tuple-element.58.deal, bf16[512,256]{1,0:T(8,128)(2,1)S(1)} %collective-permute-done.first, bf16[512,256]{1,0:T(8,128)(2,1)S(1)} %collective-permute-done.1.second, bf16[512,256]{1,0:T(8,128)(2,1)S(1)} %copy-done.1, ...), custom_call_target="tpu_custom_call" | custom-call | flops 536870912 | bytes 4194304 | tf_op jit(solution)/shard_map/project/pallas_call | solution.py:305
  16.6 36.1 %all_to_all.5 = s32[128,8,128]{2,1,0:T(8,128)S(1)} all-to-all(s32[128,8,128]{2,1,0:T(8,128)S(1)} %bitcast.9), channel_id=1, replica_groups=mesh['blk'=128,'cat'=2] {'blk'}, dimensions={0} | all-to-all | bytes 1048576 | tf_op jit(solution)/shard_map/all_to_all | solution.py:314
  52.8 1.3 %collective-permute-start.5 = (s32[144,512]{1,0:T(8,128)S(1)}, s32[144,512]{1,0:T(8,128)S(1)}, u32[]{:S(2)}, u32[]{:S(2)}) collective-permute-start(s32[144,512]{1,0:T(8,128)S(1)} %get-tuple-element.81), channel_id=1, source_target_pairs={{2,4},{6,8},{10,12},{14,16},{18,20},{22,24},{26,28},{30,32},{34,36... | collective-permute-start | bytes 884744 | tf_op jit(solution)/shard_map/ppermute | solution.py:352
  54.0 1.3 %collective-permute-start.4 = (s32[144,512]{1,0:T(8,128)S(1)}, s32[144,512]{1,0:T(8,128)S(1)}, u32[]{:S(2)}, u32[]{:S(2)}) collective-permute-start(s32[144,512]{1,0:T(8,128)S(1)} %get-tuple-element.66), channel_id=1, source_target_pairs={{2,4},{6,8},{10,12},{14,16},{18,20},{22,24},{26,28},{30,32},{34,36... | collective-permute-start | bytes 884744 | tf_op jit(solution)/shard_map/ppermute | solution.py:352
  55.4 3.1 %push.7 = (bf16[2,512,1024]{2,1,0:T(8,128)(2,1)S(1)}, bf16[2,256,1024]{2,1,0:T(8,128)(2,1)S(1)}, s32[136,512]{1,0:T(8,128)S(1)}, s32[136,512]{1,0:T(8,128)S(1)}) custom-call(bf16[2,512,256]{2,1,0:T(8,128)(2,1)S(1)} %get-tuple-element.67.refs_0_, bf16[2,256,512]{2,1,0:T(8,128)(2,1)S(1)} %get-tuple-element.56.refs_1_, ...), custom_call_target="tpu_custom_call" | custom-call | flops 1024 | bytes 1024 | tf_op jit(solution)/shard_map/push/pallas_call | solution.py:325
  58.5 0.5 collective-permute-start.2
  59.3 1.0 %collective-permute-done.2.refs_3_ = s32[136,512]{1,0:T(8,128)S(1)} collective-permute-done((s32[136,512]{1,0:T(8,128)S(1)}, s32[136,512]{1,0:T(8,128)S(1)}, u32[]{:S(2)}, u32[]{:S(2)}) %collective-permute-start.2) | collective-permute-done | bytes 278560 | tf_op jit(solution)/shard_map/ppermute | solution.py:359
  60.3 0.4 collective-permute-done.3.refs_4_
  60.7 1.3 %collective-permute-start.8 = (s32[144,512]{1,0:T(8,128)S(1)}, s32[144,512]{1,0:T(8,128)S(1)}, u32[]{:S(2)}, u32[]{:S(2)}) collective-permute-start(s32[144,512]{1,0:T(8,128)S(1)} %get-tuple-element.75), channel_id=1, source_target_pairs={{2,4},{6,8},{10,12},{14,16},{18,20},{22,24},{26,28},{30,32},{34,36... | collective-permute-start | bytes 884744 | tf_op jit(solution)/shard_map/ppermute | solution.py:352
  62.0 1.3 %collective-permute-start.9 = (s32[144,512]{1,0:T(8,128)S(1)}, s32[144,512]{1,0:T(8,128)S(1)}, u32[]{:S(2)}, u32[]{:S(2)}) collective-permute-start(s32[144,512]{1,0:T(8,128)S(1)} %get-tuple-element.97), channel_id=1, source_target_pairs={{2,4},{6,8},{10,12},{14,16},{18,20},{22,24},{26,28},{30,32},{34,36... | collective-permute-start | bytes 884744 | tf_op jit(solution)/shard_map/ppermute | solution.py:352
  63.3 1.1 %pull.8 = (f32[512,256]{1,0:T(8,128)S(1)}, bf16[2,512,256]{2,1,0:T(8,128)(2,1)S(1)}, bf16[2,256,512]{2,1,0:T(8,128)(2,1)S(1)}) custom-call(f32[512,256]{1,0:T(8,128)S(1)} %copy-done, bf16[2,512,1024]{2,1,0:T(8,128)(2,1)S(1)} %get-tuple-element.77.err, bf16[2,256,1024]{2,1,0:T(8,128)(2,1)S(1)} %get-tuple-element.78.right), custom_call_target="tpu_custom_call" | custom-call | flops 1024 | bytes 1024 | tf_op jit(solution)/shard_map/pull/pallas_call | solution.py:337
  64.5 2.1 %collective-permute-done.5.refs_4_ = s32[144,512]{1,0:T(8,128)S(1)} collective-permute-done((s32[144,512]{1,0:T(8,128)S(1)}, s32[144,512]{1,0:T(8,128)S(1)}, u32[]{:S(2)}, u32[]{:S(2)}) %collective-permute-start.5) | collective-permute-done | bytes 294944 | tf_op jit(solution)/shard_map/ppermute | solution.py:352
  66.5 3.2 %collective-permute-done.4.refs_3_ = s32[144,512]{1,0:T(8,128)S(1)} collective-permute-done((s32[144,512]{1,0:T(8,128)S(1)}, s32[144,512]{1,0:T(8,128)S(1)}, u32[]{:S(2)}, u32[]{:S(2)}) %collective-permute-start.4) | collective-permute-done | bytes 294944 | tf_op jit(solution)/shard_map/ppermute | solution.py:352
  69.7 2.6 %push.9 = (bf16[2,512,1024]{2,1,0:T(8,128)(2,1)S(1)}, bf16[2,256,1024]{2,1,0:T(8,128)(2,1)S(1)}, s32[136,512]{1,0:T(8,128)S(1)}, s32[136,512]{1,0:T(8,128)S(1)}) custom-call(bf16[2,512,256]{2,1,0:T(8,128)(2,1)S(1)} %get-tuple-element.79.refs_0_, bf16[2,256,512]{2,1,0:T(8,128)(2,1)S(1)} %get-tuple-element.80.refs_1_, ...), custom_call_target="tpu_custom_call" | custom-call | flops 1024 | bytes 1024 | tf_op jit(solution)/shard_map/push/pallas_call | solution.py:325
  72.3 0.5 collective-permute-start.7
  72.8 1.0 %collective-permute-done.6.refs_3_ = s32[136,512]{1,0:T(8,128)S(1)} collective-permute-done((s32[136,512]{1,0:T(8,128)S(1)}, s32[136,512]{1,0:T(8,128)S(1)}, u32[]{:S(2)}, u32[]{:S(2)}) %collective-permute-start.6) | collective-permute-done | bytes 278560 | tf_op jit(solution)/shard_map/ppermute | solution.py:359
  73.9 0.4 collective-permute-done.7.refs_4_
  74.3 1.3 %collective-permute-start.13 = (s32[144,512]{1,0:T(8,128)S(1)}, s32[144,512]{1,0:T(8,128)S(1)}, u32[]{:S(2)}, u32[]{:S(2)}) collective-permute-start(s32[144,512]{1,0:T(8,128)S(1)} %get-tuple-element.105), channel_id=1, source_target_pairs={{2,4},{6,8},{10,12},{14,16},{18,20},{22,24},{26,28},{30,32},{34,36... | collective-permute-start | bytes 884744 | tf_op jit(solution)/shard_map/ppermute | solution.py:352
  75.6 1.3 %collective-permute-start.12 = (s32[144,512]{1,0:T(8,128)S(1)}, s32[144,512]{1,0:T(8,128)S(1)}, u32[]{:S(2)}, u32[]{:S(2)}) collective-permute-start(s32[144,512]{1,0:T(8,128)S(1)} %get-tuple-element.90), channel_id=1, source_target_pairs={{2,4},{6,8},{10,12},{14,16},{18,20},{22,24},{26,28},{30,32},{34,36... | collective-permute-start | bytes 884744 | tf_op jit(solution)/shard_map/ppermute | solution.py:352
  76.9 1.1 %pull.10 = (f32[512,256]{1,0:T(8,128)S(1)}, bf16[2,512,256]{2,1,0:T(8,128)(2,1)S(1)}, bf16[2,256,512]{2,1,0:T(8,128)(2,1)S(1)}) custom-call(f32[512,256]{1,0:T(8,128)S(1)} %get-tuple-element.91.users, bf16[2,512,1024]{2,1,0:T(8,128)(2,1)S(1)} %get-tuple-element.92.err, bf16[2,256,1024]{2,1,0:T(8,128)(2,1)S(1)} %get-tuple-element.93.right), custom_call_target="tpu_custom_call" | custom-call | flops 1024 | bytes 1024 | tf_op jit(solution)/shard_map/pull/pallas_call | solution.py:337
  78.0 2.8 %push.11 = (bf16[2,512,1024]{2,1,0:T(8,128)(2,1)S(1)}, bf16[2,256,1024]{2,1,0:T(8,128)(2,1)S(1)}, s32[136,512]{1,0:T(8,128)S(1)}, s32[136,512]{1,0:T(8,128)S(1)}) custom-call(bf16[2,512,256]{2,1,0:T(8,128)(2,1)S(1)} %get-tuple-element.95.refs_0_, bf16[2,256,512]{2,1,0:T(8,128)(2,1)S(1)} %get-tuple-element.96.refs_1_, ...), custom_call_target="tpu_custom_call" | custom-call | flops 1024 | bytes 1024 | tf_op jit(solution)/shard_map/push/pallas_call | solution.py:325
  80.9 0.5 collective-permute-start.11
  81.4 1.1 %pull.11 = (f32[512,256]{1,0:T(8,128)S(1)}, bf16[2,512,256]{2,1,0:T(8,128)(2,1)S(1)}, bf16[2,256,512]{2,1,0:T(8,128)(2,1)S(1)}) custom-call(f32[512,256]{1,0:T(8,128)S(1)} %get-tuple-element.94.users, bf16[2,512,1024]{2,1,0:T(8,128)(2,1)S(1)} %get-tuple-element.98.err, bf16[2,256,1024]{2,1,0:T(8,128)(2,1)S(1)} %get-tuple-element.99.right), custom_call_target="tpu_custom_call" | custom-call | flops 1024 | bytes 1024 | tf_op jit(solution)/shard_map/pull/pallas_call | solution.py:337
  82.6 0.3 collective-permute-done.11.refs_8_
  82.9 5.2 %collective-permute-done.13.refs_10_ = s32[144,512]{1,0:T(8,128)S(1)} collective-permute-done((s32[144,512]{1,0:T(8,128)S(1)}, s32[144,512]{1,0:T(8,128)S(1)}, u32[]{:S(2)}, u32[]{:S(2)}) %collective-permute-start.13) | collective-permute-done | bytes 294944 | tf_op jit(solution)/shard_map/ppermute | solution.py:352
  88.0 3.2 %collective-permute-done.12.refs_9_ = s32[144,512]{1,0:T(8,128)S(1)} collective-permute-done((s32[144,512]{1,0:T(8,128)S(1)}, s32[144,512]{1,0:T(8,128)S(1)}, u32[]{:S(2)}, u32[]{:S(2)}) %collective-permute-start.12) | collective-permute-done | bytes 294944 | tf_op jit(solution)/shard_map/ppermute | solution.py:352
  91.2 4.1 %last.1 = (f32[512,256]{1,0:T(8,128)}, f32[1024,256]{1,0:T(8,128)}) custom-call(bf16[2,512,256]{2,1,0:T(8,128)(2,1)S(1)} %get-tuple-element.86.refs_0_, bf16[2,256,512]{2,1,0:T(8,128)(2,1)S(1)} %get-tuple-element.87.refs_1_, f32[512,256]{1,0:T(8,128)S(1)} %get-tuple-element.88.refs_2_, bf16[2,512,256]{2,1,0:T(8,128)(2,1)S(1)} %get-tuple-element.100.refs_3_, ...), custom_call_target="tpu_custom_call" | custom-call | flops 1024 | bytes 1024 | tf_op jit(solution)/shard_map/last/pallas_call | solution.py:363
  (22 shorter events, 0.6 us)
Async XLA Ops:
  1.7 12.5 %collective-permute-start.1 = (bf16[512,256]{1,0:T(8,128)(2,1)S(1)}, bf16[512,256]{1,0:T(8,128)(2,1)S(1)}, u32[]{:S(2)}, u32[]{:S(2)}) collective-permute-start(bf16[512,256]{1,0:T(8,128)(2,1)S(1)} %get-tuple-element.106), channel_id=1, source_target_pairs={{0,1},{1,0},{2,3},{3,2},{4,5},{5,4},{6,7},{7,6},{8,9},{9,8},{10,11... | collective-permute-start | bytes 786440 | tf_op jit(solution)/shard_map/ppermute | solution.py:270
  4.0 11.5 %collective-permute-start = (bf16[512,256]{1,0:T(8,128)(2,1)S(1)}, bf16[512,256]{1,0:T(8,128)(2,1)S(1)}, u32[]{:S(2)}, u32[]{:S(2)}) collective-permute-start(bf16[512,256]{1,0:T(8,128)(2,1)S(1)} %get-tuple-element.107), channel_id=1, source_target_pairs={{0,1},{1,0},{2,3},{3,2},{4,5},{5,4},{6,7},{7,6},{8,9},{9,8},{10,11... | collective-permute-start | bytes 786440 | tf_op jit(solution)/shard_map/ppermute | solution.py:270
  4.1 8.4 %copy-start = (f32[512,256]{1,0:T(8,128)S(1)}, f32[512,256]{1,0:T(8,128)}, u32[]{:S(2)}) copy-start(f32[512,256]{1,0:T(8,128)} %users.4) | copy-start | bytes 1572868
  4.1 8.4 %copy-start.1 = (bf16[512,256]{1,0:T(8,128)(2,1)S(1)}, bf16[512,256]{1,0:T(8,128)(2,1)}, u32[]{:S(2)}) copy-start(bf16[512,256]{1,0:T(8,128)(2,1)} %weights.3) | copy-start | bytes 786436
  4.1 8.4 %copy-start.2 = (bf16[2048,256]{1,0:T(8,128)(2,1)S(1)}, bf16[2048,256]{1,0:T(8,128)(2,1)}, u32[]{:S(2)}) copy-start(bf16[2048,256]{1,0:T(8,128)(2,1)} %content.1) | copy-start | bytes 3145732
  4.1 8.4 %copy-start.3 = (s32[1,1024]{1,0:T(1,128)S(1)}, s32[1,1024]{1,0:T(1,128)}, u32[]{:S(2)}) copy-start(s32[1,1024]{1,0:T(1,128)} %order) | copy-start | bytes 12292
  52.8 13.8 %collective-permute-start.5 = (s32[144,512]{1,0:T(8,128)S(1)}, s32[144,512]{1,0:T(8,128)S(1)}, u32[]{:S(2)}, u32[]{:S(2)}) collective-permute-start(s32[144,512]{1,0:T(8,128)S(1)} %get-tuple-element.81), channel_id=1, source_target_pairs={{2,4},{6,8},{10,12},{14,16},{18,20},{22,24},{26,28},{30,32},{34,36... | collective-permute-start | bytes 884744 | tf_op jit(solution)/shard_map/ppermute | solution.py:352
  54.0 15.6 %collective-permute-start.4 = (s32[144,512]{1,0:T(8,128)S(1)}, s32[144,512]{1,0:T(8,128)S(1)}, u32[]{:S(2)}, u32[]{:S(2)}) collective-permute-start(s32[144,512]{1,0:T(8,128)S(1)} %get-tuple-element.66), channel_id=1, source_target_pairs={{2,4},{6,8},{10,12},{14,16},{18,20},{22,24},{26,28},{30,32},{34,36... | collective-permute-start | bytes 884744 | tf_op jit(solution)/shard_map/ppermute | solution.py:352
  58.5 1.8 %collective-permute-start.2 = (s32[136,512]{1,0:T(8,128)S(1)}, s32[136,512]{1,0:T(8,128)S(1)}, u32[]{:S(2)}, u32[]{:S(2)}) collective-permute-start(s32[136,512]{1,0:T(8,128)S(1)} %get-tuple-element.68), channel_id=1, source_target_pairs={{0,2},{2,0},{4,6},{6,4},{8,10},{10,8},{12,14},{14,12},{16,18},{18,... | collective-permute-start | bytes 835592 | tf_op jit(solution)/shard_map/ppermute | solution.py:359
  59.0 1.7 %collective-permute-start.3 = (s32[136,512]{1,0:T(8,128)S(1)}, s32[136,512]{1,0:T(8,128)S(1)}, u32[]{:S(2)}, u32[]{:S(2)}) collective-permute-start(s32[136,512]{1,0:T(8,128)S(1)} %get-tuple-element.69), channel_id=1, source_target_pairs={{0,2},{2,0},{4,6},{6,4},{8,10},{10,8},{12,14},{14,12},{16,18},{18,... | collective-permute-start | bytes 835592 | tf_op jit(solution)/shard_map/ppermute | solution.py:359
  60.7 17.3 %collective-permute-start.8 = (s32[144,512]{1,0:T(8,128)S(1)}, s32[144,512]{1,0:T(8,128)S(1)}, u32[]{:S(2)}, u32[]{:S(2)}) collective-permute-start(s32[144,512]{1,0:T(8,128)S(1)} %get-tuple-element.75), channel_id=1, source_target_pairs={{2,4},{6,8},{10,12},{14,16},{18,20},{22,24},{26,28},{30,32},{34,36... | collective-permute-start | bytes 884744 | tf_op jit(solution)/shard_map/ppermute | solution.py:352
  62.0 16.0 %collective-permute-start.9 = (s32[144,512]{1,0:T(8,128)S(1)}, s32[144,512]{1,0:T(8,128)S(1)}, u32[]{:S(2)}, u32[]{:S(2)}) collective-permute-start(s32[144,512]{1,0:T(8,128)S(1)} %get-tuple-element.97), channel_id=1, source_target_pairs={{2,4},{6,8},{10,12},{14,16},{18,20},{22,24},{26,28},{30,32},{34,36... | collective-permute-start | bytes 884744 | tf_op jit(solution)/shard_map/ppermute | solution.py:352
  72.2 1.6 %collective-permute-start.6 = (s32[136,512]{1,0:T(8,128)S(1)}, s32[136,512]{1,0:T(8,128)S(1)}, u32[]{:S(2)}, u32[]{:S(2)}) collective-permute-start(s32[136,512]{1,0:T(8,128)S(1)} %get-tuple-element.82), channel_id=1, source_target_pairs={{0,2},{2,0},{4,6},{6,4},{8,10},{10,8},{12,14},{14,12},{16,18},{18,... | collective-permute-start | bytes 835592 | tf_op jit(solution)/shard_map/ppermute | solution.py:359
  72.3 1.9 %collective-permute-start.7 = (s32[136,512]{1,0:T(8,128)S(1)}, s32[136,512]{1,0:T(8,128)S(1)}, u32[]{:S(2)}, u32[]{:S(2)}) collective-permute-start(s32[136,512]{1,0:T(8,128)S(1)} %get-tuple-element.83), channel_id=1, source_target_pairs={{0,2},{2,0},{4,6},{6,4},{8,10},{10,8},{12,14},{14,12},{16,18},{18,... | collective-permute-start | bytes 835592 | tf_op jit(solution)/shard_map/ppermute | solution.py:359
  74.3 13.8 %collective-permute-start.13 = (s32[144,512]{1,0:T(8,128)S(1)}, s32[144,512]{1,0:T(8,128)S(1)}, u32[]{:S(2)}, u32[]{:S(2)}) collective-permute-start(s32[144,512]{1,0:T(8,128)S(1)} %get-tuple-element.105), channel_id=1, source_target_pairs={{2,4},{6,8},{10,12},{14,16},{18,20},{22,24},{26,28},{30,32},{34,36... | collective-permute-start | bytes 884744 | tf_op jit(solution)/shard_map/ppermute | solution.py:352
  75.6 15.6 %collective-permute-start.12 = (s32[144,512]{1,0:T(8,128)S(1)}, s32[144,512]{1,0:T(8,128)S(1)}, u32[]{:S(2)}, u32[]{:S(2)}) collective-permute-start(s32[144,512]{1,0:T(8,128)S(1)} %get-tuple-element.90), channel_id=1, source_target_pairs={{2,4},{6,8},{10,12},{14,16},{18,20},{22,24},{26,28},{30,32},{34,36... | collective-permute-start | bytes 884744 | tf_op jit(solution)/shard_map/ppermute | solution.py:352
  80.8 1.7 %collective-permute-start.10 = (s32[136,512]{1,0:T(8,128)S(1)}, s32[136,512]{1,0:T(8,128)S(1)}, u32[]{:S(2)}, u32[]{:S(2)}) collective-permute-start(s32[136,512]{1,0:T(8,128)S(1)} %get-tuple-element.103), channel_id=1, source_target_pairs={{0,2},{2,0},{4,6},{6,4},{8,10},{10,8},{12,14},{14,12},{16,18},{18,... | collective-permute-start | bytes 835592 | tf_op jit(solution)/shard_map/ppermute | solution.py:359
  80.9 1.9 %collective-permute-start.11 = (s32[136,512]{1,0:T(8,128)S(1)}, s32[136,512]{1,0:T(8,128)S(1)}, u32[]{:S(2)}, u32[]{:S(2)}) collective-permute-start(s32[136,512]{1,0:T(8,128)S(1)} %get-tuple-element.104), channel_id=1, source_target_pairs={{0,2},{2,0},{4,6},{6,4},{8,10},{10,8},{12,14},{14,12},{16,18},{18,... | collective-permute-start | bytes 835592 | tf_op jit(solution)/shard_map/ppermute | solution.py:359

commit v3 on v2

--- a/solution.py
+++ b/solution.py
@@ -14,10 +14,8 @@
 CONTENT_BOUND = 6.0
 LOG_RANGE = 14.0
 TOP = 32767.0
-EVEN_PIECES = 2
-ODD_PIECES = 2
-EVEN_TAIL = 16
-ODD_TAIL = 8
+EVEN_TAILS = ((16, 16), (32, 24), (16, 16))
+ODD_TAILS = ((8, 8), (8, 8), (8, 8))
 F32 = jnp.float32
 BF16 = jnp.bfloat16
 I32 = jnp.int32
@@ -148,16 +146,15 @@
     return jnp.concatenate([a, b], axis=0) * scale
 
 
-def errors_and_items(q, cols, left, left_t, values, t, err, right):
+def errors_and_items(q, here, cols, left, left_t, values, t, err, right):
     q_hi, q_lo = split(q)
-    if right is not None:
-        right[0, :, cols] = q_hi
-        right[1, :, cols] = q_lo
+    right[0, :, here] = q_hi
+    right[1, :, here] = q_lo
     guess = mm(left[0], q_hi) + mm(left[0], q_lo) + mm(left[1], q_hi)
     v = (lax.shift_right_logical(values[:, cols].astype(I32), 3 * t) & 7).astype(F32)
     e_hi, e_lo = split(jnp.where(v > 0, v - guess, 0.0))
-    err[0, :, cols] = e_hi
-    err[1, :, cols] = e_lo
+    err[0, :, here] = e_hi
+    err[1, :, here] = e_lo
     grad = mm(left_t[0], e_hi) + mm(left_t[0], e_lo) + mm(left_t[1], e_hi)
     return KEEP * q + learn_rate * grad
 
@@ -171,87 +168,89 @@
 CHUNK = 256
 
 
-def piece(refs, at):
-    wide = refs[0].shape[1]
-    return refs[at // wide], slice(at % wide, at % wide + CHUNK)
-
-
 def my_turn(turn):
     return lax.rem(lax.axis_index("blk"), 2) == turn
 
 
-def push_kernel(turn, t, pieces, *refs):
-    first = t == 0
-    left, left_t, values = refs[:3]
-    refs = refs[3:]
-    if first:
-        dealt, meta = refs[:2]
-        refs = refs[2:]
-    else:
-        got = refs[:-2 - pieces]
-        refs = refs[-2 - pieces:]
-    err, right = refs[:2]
-    outs = refs[2:]
-    n = values.shape[1]
+def push_kernel(turn, t, half, left, left_t, values, *refs):
+    source, (err, right, out) = refs[:-3], refs[-3:]
+    wide = out.shape[1]
 
     @pl.when(my_turn(turn))
     def _():
-        for at in range(0, n, CHUNK):
-            cols = slice(at, at + CHUNK)
-            if first:
-                q = first_items(dealt, meta, cols)
+        for at in range(0, wide, CHUNK):
+            here = slice(at, at + CHUNK)
+            cols = slice(half * wide + at, half * wide + at + CHUNK)
+            if t == 0:
+                q = first_items(*source, cols)
             else:
-                ref, here = piece(got, at)
-                q = decode(ref[:, here], right.shape[1])
-            words, level = encode(errors_and_items(q, cols, left, left_t, values, t, err, right))
+                q = decode(source[0][:, here], right.shape[1])
+            new = errors_and_items(q, here, cols, left, left_t, values, t, err, right)
+            words, level = encode(new)
             rows = words.shape[0]
-            ref, here = piece(outs, at)
-            ref[:rows, here] = words
-            ref[rows:, here] = jnp.broadcast_to(level, (ref.shape[0] - rows, CHUNK))
-
-
-def user_step(users, err, right, rows=slice(None)):
+            out[:rows, here] = words
+            out[rows:, here] = jnp.broadcast_to(level, (out.shape[0] - rows, CHUNK))
+
+
+def user_step(users, parts, rows=slice(None)):
     dims = ((1,), (1,))
-    hi, lo = err[0, rows, :], err[1, rows, :]
-    grad = mm(hi, right[0], dims) + mm(hi, right[1], dims) + mm(lo, right[0], dims)
+    grad = None
+    for err, right in parts:
+        hi, lo = err[0, rows, :], err[1, rows, :]
+        for a, b in ((hi, right[0]), (hi, right[1]), (lo, right[0])):
+            term = mm(a, b, dims)
+            grad = term if grad is None else grad + term
     return KEEP * users[rows, :] + learn_rate * grad
 
 
-def pull_kernel(turn, users, err, right, new_users, left, left_t):
+def pull_kernel(turn, users, err_a, right_a, err_b, right_b, new_users, left, left_t):
     @pl.when(my_turn(turn))
     def _():
-        put_users(user_step(users, err, right), new_users, left, left_t)
-
-
-def last_kernel(pieces, *refs):
-    odd, even = refs[:3], refs[3:6]
-    values = refs[6]
-    refs = refs[7:]
-    to_odd, to_even = refs[:pieces[0]], refs[pieces[0]:sum(pieces)]
-    users_out, items_out, err, right, users_held, items_held, sems = refs[sum(pieces):]
-    n = values.shape[1]
-    tall = users_held.shape[0] // 2
-
-    for turn, (left, left_t, users), got in ((1, odd, to_odd), (0, even, to_even)):
+        put_users(user_step(users, ((err_a, right_a), (err_b, right_b))), new_users, left, left_t)
+
+
+def last_pull_kernel(*refs):
+    outs = refs[10:]
+    for turn, (users, *parts) in ((1, refs[:5]), (0, refs[5:10])):
 
         @pl.when(my_turn(turn))
         def _():
-            copies = []
-            for at in range(0, n, CHUNK):
-                cols = slice(at, at + CHUNK)
-                ref, here = piece(got, at)
-                q = decode(ref[:, here], right.shape[1])
-                new = errors_and_items(q, cols, left, left_t, values, ROUNDS - 1, err, right)
-                items_held[cols, :] = new.T
-                copies.append(pltpu.make_async_copy(items_held.at[cols, :], items_out.at[cols, :], sems.at[len(copies)]))
-                copies[-1].start()
-            for at in (0, tall):
-                rows = slice(at, at + tall)
-                users_held[rows, :] = user_step(users, err, right, rows)
-                copies.append(pltpu.make_async_copy(users_held.at[rows, :], users_out.at[rows, :], sems.at[len(copies)]))
-                copies[-1].start()
-            for copy in copies:
-                copy.wait()
+            put_users(user_step(users, (parts[:2], parts[2:])), *outs)
+
+
+def last_items(half, left, left_t, values, got_o, got_e, items_out, err, right, held, sems):
+    wide = right.shape[2]
+    live = right.shape[1] // 2 + 8
+    is_odd = my_turn(1)
+    copies = []
+    for at in range(0, wide, CHUNK):
+        here = slice(at, at + CHUNK)
+        cols = slice(half * wide + at, half * wide + at + CHUNK)
+        q = decode(jnp.where(is_odd, got_o[:live, here], got_e[:live, here]), right.shape[1])
+        held[here, :] = errors_and_items(q, here, cols, left, left_t, values, ROUNDS - 1, err, right).T
+        copies.append(pltpu.make_async_copy(held.at[here, :], items_out.at[cols, :], sems.at[len(copies)]))
+        copies[-1].start()
+    return copies
+
+
+def last_first_kernel(left, left_t, values, got_o, got_e, items_out, err, right, held, sems):
+    for copy in last_items(0, left, left_t, values, got_o, got_e, items_out, err, right, held, sems):
+        copy.wait()
+
+
+def last_second_kernel(
+    left, left_t, values, got_o, got_e, users, err_a, right_a, items_in,
+    items_out, users_out, err, right, held, users_held, sems,
+):
+    copies = last_items(1, left, left_t, values, got_o, got_e, items_out, err, right, held, sems)
+    tall = users_held.shape[0] // 2
+    for at in (0, tall):
+        rows = slice(at, at + tall)
+        users_held[rows, :] = user_step(users, ((err_a, right_a), (err, right)), rows)
+        copies.append(pltpu.make_async_copy(users_held.at[rows, :], users_out.at[rows, :], sems.at[len(copies)]))
+        copies[-1].start()
+    for copy in copies:
+        copy.wait()
 
 
 def struct(shape, dtype):
@@ -315,67 +314,99 @@
         coded.reshape(n_blk, share, rank // 2), "blk", split_axis=0, concat_axis=0, tiled=True
     ).reshape(n_items, rank // 2)
 
-    state_shapes = [struct((2, n_users, n_items), BF16), struct((2, rank, n_items), BF16)]
+    half_shapes = [struct((2, n_users, wide), BF16), struct((2, rank, wide), BF16)]
     to_even = [(i, (i + 1) % n_blk) for i in range(1, n_blk, 2)]
     to_odd = [(i, i ^ 1) for i in range(n_blk)]
     light = cost(1 << 10, 1 << 10)
 
-    def push(turn, t, left, left_t, source, pieces, tail):
-        sent_shapes = [struct((rank // 2 + tail, n_items // pieces), I32)] * pieces
-        got = pl.pallas_call(
-            functools.partial(push_kernel, turn, t, pieces),
-            out_shape=state_shapes + sent_shapes,
+    def push(turn, t, half, left, left_t, source, tail):
+        *state, sent = pl.pallas_call(
+            functools.partial(push_kernel, turn, t, half),
+            out_shape=half_shapes + [struct((rank // 2 + tail, wide), I32)],
             in_specs=[VM] * (3 + len(source)),
-            out_specs=[VM] * (2 + pieces),
+            out_specs=[VM] * 3,
             compiler_params=params(),
             cost_estimate=light,
             name="push",
         )(left, left_t, values, *source)
-        return got[:2], got[2:]
-
-    def pull(turn, users, state):
+        return state, sent
+
+    def pull(turn, users, states):
         return pl.pallas_call(
             functools.partial(pull_kernel, turn),
             out_shape=[struct((n_users, rank), F32)] + split_shapes,
-            in_specs=[VM] * 3,
+            in_specs=[VM] * 5,
             out_specs=[VM] * 3,
             compiler_params=params(),
             cost_estimate=light,
             name="pull",
-        )(users, *state)
+        )(users, *states[0], *states[1])
+
+    def after(x, done):
+        return lax.optimization_barrier((x, done))[0]
+
+    def both(turn, t, left, left_t, sources, tails, pairs):
+        states, nexts = [], []
+        for half in range(2):
+            state, sent = push(turn, t, half, left, left_t, sources[half], tails[half])
+            states.append(state)
+            nexts.append([lax.ppermute(sent, "blk", pairs)])
+            left = after(left, sent)
+        return states, nexts, sent
 
     odd = even = (user_factors, left, left_t)
-    for_odd = for_even = [dealt, meta]
-    state_even = None
+    for_odd = for_even = [[dealt, meta]] * 2
+    even_states = None
     for t in range(ROUNDS - 1):
-        state_odd, sent = push(1, t, *odd[1:], for_odd, EVEN_PIECES, EVEN_TAIL)
-        next_even = [lax.ppermute(x, "blk", to_even) for x in sent]
-        if state_even is not None:
-            users, _ = lax.optimization_barrier((even[0], sent[0]))
-            even = pull(0, users, state_even)
+        odd_states, next_even, sent = both(1, t, *odd[1:], for_odd, EVEN_TAILS[t], to_even)
+        if even_states is None:
+            even = (even[0], after(even[1], sent), even[2])
         else:
-            even = (even[0], lax.optimization_barrier((even[1], sent[0]))[0], even[2])
-        state_even, sent = push(0, t, *even[1:], for_even, ODD_PIECES, ODD_TAIL)
-        next_odd = [lax.ppermute(x, "blk", to_odd) for x in sent]
-        odd = pull(1, odd[0], state_odd)
+            even = pull(0, after(even[0], sent), even_states)
+        even_states, next_odd, _ = both(0, t, *even[1:], for_even, ODD_TAILS[t], to_odd)
         for_even, for_odd = next_even, next_odd
-    even = pull(0, even[0], state_even)
-    return tuple(pl.pallas_call(
-        functools.partial(last_kernel, (ODD_PIECES, EVEN_PIECES)),
-        out_shape=[struct((n_users, rank), F32), struct((n_items, rank), F32)],
-        in_specs=[VM] * (7 + EVEN_PIECES + ODD_PIECES),
-        out_specs=[pl.BlockSpec(memory_space=pl.ANY)] * 2,
+        if t < ROUNDS - 2:
+            odd = pull(1, odd[0], odd_states)
+    users, left, left_t = pl.pallas_call(
+        last_pull_kernel,
+        out_shape=[struct((n_users, rank), F32)] + split_shapes,
+        in_specs=[VM] * 10,
+        out_specs=[VM] * 3,
+        compiler_params=params(),
+        cost_estimate=light,
+        name="last_pull",
+    )(odd[0], *odd_states[0], *odd_states[1], even[0], *even_states[0], *even_states[1])
+
+    anywhere = pl.BlockSpec(memory_space=pl.ANY)
+    held_shapes = [pltpu.VMEM((wide, rank), F32)]
+    items, err, right = pl.pallas_call(
+        last_first_kernel,
+        out_shape=[pltpu.HBM((n_items, rank), F32)] + half_shapes,
+        in_specs=[VM] * 5,
+        out_specs=[anywhere, VM, VM],
+        scratch_shapes=held_shapes + [pltpu.SemaphoreType.DMA((wide // CHUNK,))],
+        compiler_params=params(),
+        cost_estimate=light,
+        name="last_first",
+    )(left, left_t, values, *for_odd[0], *for_even[0])
+    items, users = pl.pallas_call(
+        last_second_kernel,
+        out_shape=[struct((n_items, rank), F32), struct((n_users, rank), F32)],
+        in_specs=[VM] * 8 + [anywhere],
+        out_specs=[anywhere] * 2,
         scratch_shapes=[
-            pltpu.VMEM((2, n_users, n_items), BF16),
-            pltpu.VMEM((2, rank, n_items), BF16),
+            pltpu.VMEM((2, n_users, wide), BF16),
+            pltpu.VMEM((2, rank, wide), BF16),
+        ] + held_shapes + [
             pltpu.VMEM((n_users, rank), F32),
-            pltpu.VMEM((n_items, rank), F32),
-            pltpu.SemaphoreType.DMA((n_items // CHUNK + 2,)),
+            pltpu.SemaphoreType.DMA((wide // CHUNK + 2,)),
         ],
+        input_output_aliases={8: 0},
         compiler_params=params(16),
         cost_estimate=light,
-        name="last",
-    )(odd[1], odd[2], odd[0], even[1], even[2], even[0], values, *for_odd, *for_even))
+        name="last_second",
+    )(left, left_t, values, *for_odd[1], *for_even[1], users, err, right, items)
+    return users, items
 
 
 def solution(mesh):

time: 95.8 us -> 96.4 us (level)
  waiting for transfers between devices: 18 us -> 12.1 us
  Pallas kernels: 27.2 us -> 30.5 us
  starting transfers between devices: 12 us -> 14.9 us
    ppermute x12, waiting for transfers between devices: 16.7 us -> 10.7 us  [both(): nexts.append([lax.ppermute(sent, 'blk', pairs)])]
    pallas_call x7 -> x15, Pallas kernels: 12.6 us -> 17.2 us  [the longest x12 10.6 us: push(): pl.pallas_call(functools.partial(push_kernel, turn, t, half), out_shape=h...]
    ppermute x12, starting transfers between devices: 9.67 us -> 12.6 us  [both(): nexts.append([lax.ppermute(sent, 'blk', pairs)])]
    pallas_call x6 -> x4, Pallas kernels: 3.38 us -> 2.3 us  [pull(): pl.pallas_call(functools.partial(pull_kernel, turn), out_shape=[struct((n...]
  transfers between devices with their start and end apart: 14 -> 14, of which waited for: 10 -> 7; matrix products, arithmetic and copies ran while one was open for 0% -> 0% of each run, Pallas kernels for 23% -> 25%
where the time goes in v3:
time: 96.4 us; the launch traced here: 96 us
  blocking collectives  36.1 us (37%)
  Pallas kernels  30.5 us (32%)
  starting transfers between devices  14.9 us (15%)
  waiting for transfers between devices  12.1 us (13%)
  local copies, waits for them, and re-layouts  1.21 us (1%)
  between operations  1.14 us (1%)
    all_to_all x1, blocking collectives, body(): lax.all_to_all(coded.reshape(n_blk, share, rank // 2), 'blk', split_axis=...  36.1 us
    ppermute x12, starting transfers between devices, both(): nexts.append([lax.ppermute(sent, 'blk', pairs)])  12.6 us
    ppermute x12, waiting for transfers between devices, both(): nexts.append([lax.ppermute(sent, 'blk', pairs)])  10.7 us
    pallas_call x12, Pallas kernels, push(): pl.pallas_call(functools.partial(push_kernel, turn, t, half), out_shape=h...  10.6 us
    pallas_call x1, Pallas kernels, body(): pl.pallas_call(ratings_kernel, out_shape=struct((n_users, n_items), jnp.i...  8.24 us
    pallas_call x1, Pallas kernels, body(): pl.pallas_call(last_second_kernel, out_shape=[struct((n_items, rank), F32...  3.11 us
    ppermute x2, starting transfers between devices, body(): lax.ppermute(away[i * wide:(i + 1) * wide], 'cat', swap)  2.37 us
    pallas_call x1, Pallas kernels, body(): pl.pallas_call(last_first_kernel, out_shape=[pltpu.HBM((n_items, rank), F...  2.33 us
  transfers between devices with their start and end apart: 14, of which 7 were waited for; matrix products, arithmetic and copies ran while one was open for 0% of the time, Pallas kernels for 25%

profile of v3, /device:TPU:8, one launch (start us, length us, event | category | flops | bytes accessed | tf_op | source)
XLA Modules:
  0.0 96.0 jit_solution(4820935569697223057)
XLA Ops:
  0.7 1.2 %constant_dynamic-slice_fusion.1 = (bf16[512,256]{1,0:T(8,128)(2,1)S(1)}, bf16[512,256]{1,0:T(8,128)(2,1)S(1)}) fusion(bf16[2048,256]{1,0:T(8,128)(2,1)} %content.1, s32[]{:T(128)S(6)} %add.4, s32[]{:T(128)S(6)} %select_n.3), kind=kLoop, calls=%fused_computation.1 | loop fusion | bytes 1048584 | tf_op jit(solution)/shard_map/slice | solution.py:269
  1.9 2.3 %collective-permute-start.1 = (bf16[512,256]{1,0:T(8,128)(2,1)S(1)}, bf16[512,256]{1,0:T(8,128)(2,1)S(1)}, u32[]{:S(2)}, u32[]{:S(2)}) collective-permute-start(bf16[512,256]{1,0:T(8,128)(2,1)S(1)} %get-tuple-element.146), channel_id=1, source_target_pairs={{0,1},{1,0},{2,3},{3,2},{4,5},{5,4},{6,7},{7,6},{8,9},{9,8},{10,11... | collective-permute-start | bytes 786440 | tf_op jit(solution)/shard_map/ppermute | solution.py:269
  4.2 8.2 %ratings.1.values = s16[512,1024]{1,0:T(8,128)(2,1)S(1)} custom-call(s32[16384,128]{1,0:T(8,128)} %bitcast.12), custom_call_target="tpu_custom_call" | custom-call | flops 1048576 | bytes 12582912 | tf_op jit(solution)/shard_map/ratings/pallas_call | solution.py:274
  12.5 1.7 %before.1 = (bf16[1024,1024]{1,0:T(8,128)(2,1)S(1)}, f32[1024,256]{1,0:T(8,128)S(1)}, f32[8,128]{1,0:T(8,128)S(1)}, bf16[2,512,256]{2,1,0:T(8,128)(2,1)S(1)}, bf16[2,256,512]{2,1,0:T(8,128)(2,1)S(1)}) custom-call(s32[1,1024]{1,0:T(1,128)S(1)} %copy-done.3, bf16[2048,256]{1,0:T(8,128)(2,1)S(1)} %copy-done.2, bf16[512,256]{1,0:T(8,128)(2,1)S(1)} %copy-done.1, ...), custom_call_target="tpu_custom_call" | custom-call | flops 536870912 | bytes 6291456 | tf_op jit(solution)/shard_map/before/pallas_call | solution.py:286
  14.2 1.4 %collective-permute-done.first = bf16[512,256]{1,0:T(8,128)(2,1)S(1)} collective-permute-done((bf16[512,256]{1,0:T(8,128)(2,1)S(1)}, bf16[512,256]{1,0:T(8,128)(2,1)S(1)}, u32[]{:S(2)}, u32[]{:S(2)}) %collective-permute-start) | collective-permute-done | bytes 262176 | tf_op jit(solution)/shard_map/ppermute | solution.py:269
  15.6 1.2 %project.1 = s32[1024,128]{1,0:T(8,128)S(1)} custom-call(bf16[1024,1024]{1,0:T(8,128)(2,1)S(1)} %get-tuple-element.78.deal, bf16[512,256]{1,0:T(8,128)(2,1)S(1)} %collective-permute-done.first, bf16[512,256]{1,0:T(8,128)(2,1)S(1)} %collective-permute-done.1.second, bf16[512,256]{1,0:T(8,128)(2,1)S(1)} %copy-done.1, ...), custom_call_target="tpu_custom_call" | custom-call | flops 536870912 | bytes 4194304 | tf_op jit(solution)/shard_map/project/pallas_call | solution.py:304
  16.8 36.1 %all_to_all.5 = s32[128,8,128]{2,1,0:T(8,128)S(1)} all-to-all(s32[128,8,128]{2,1,0:T(8,128)S(1)} %bitcast.11), channel_id=1, replica_groups=mesh['blk'=128,'cat'=2] {'blk'}, dimensions={0} | all-to-all | bytes 1048576 | tf_op jit(solution)/shard_map/all_to_all | solution.py:313
  52.9 1.9 %push.14 = (bf16[2,512,512]{2,1,0:T(8,128)(2,1)S(1)}, bf16[2,256,512]{2,1,0:T(8,128)(2,1)S(1)}, s32[136,512]{1,0:T(8,128)S(1)}) custom-call(bf16[2,512,256]{2,1,0:T(8,128)(2,1)S(1)} %get-tuple-element.97.left, bf16[2,256,512]{2,1,0:T(8,128)(2,1)S(1)} %get-tuple-element.76.left_t, s16[512,1024]{1,0:T(8,128)(2,1)S(1)} %ratings.1.values, ...), custom_call_target="tpu_custom_call" | custom-call | flops 1024 | bytes 1024 | tf_op jit(solution)/shard_map/push/pallas_call | solution.py:323
  54.8 2.2 %collective-permute-start.2 = (s32[136,512]{1,0:T(8,128)S(1)}, s32[136,512]{1,0:T(8,128)S(1)}, u32[]{:S(2)}, u32[]{:S(2)}) collective-permute-start(s32[136,512]{1,0:T(8,128)S(1)} %get-tuple-element.92), channel_id=1, source_target_pairs={{0,2},{2,0},{4,6},{6,4},{8,10},{10,8},{12,14},{14,12},{16,18},{18,... | collective-permute-start | bytes 835592 | tf_op jit(solution)/shard_map/ppermute | solution.py:353
  57.1 1.3 %collective-permute-start.4 = (s32[144,512]{1,0:T(8,128)S(1)}, s32[144,512]{1,0:T(8,128)S(1)}, u32[]{:S(2)}, u32[]{:S(2)}) collective-permute-start(s32[144,512]{1,0:T(8,128)S(1)} %get-tuple-element.83), channel_id=1, source_target_pairs={{2,4},{6,8},{10,12},{14,16},{18,20},{22,24},{26,28},{30,32},{34,36... | collective-permute-start | bytes 884744 | tf_op jit(solution)/shard_map/ppermute | solution.py:353
  58.3 1.3 %collective-permute-start.6 = (s32[144,512]{1,0:T(8,128)S(1)}, s32[144,512]{1,0:T(8,128)S(1)}, u32[]{:S(2)}, u32[]{:S(2)}) collective-permute-start(s32[144,512]{1,0:T(8,128)S(1)} %get-tuple-element.90), channel_id=1, source_target_pairs={{2,4},{6,8},{10,12},{14,16},{18,20},{22,24},{26,28},{30,32},{34,36... | collective-permute-start | bytes 884744 | tf_op jit(solution)/shard_map/ppermute | solution.py:353
  59.6 2.1 %push.16 = (bf16[2,512,512]{2,1,0:T(8,128)(2,1)S(1)}, bf16[2,256,512]{2,1,0:T(8,128)(2,1)S(1)}, s32[136,512]{1,0:T(8,128)S(1)}) custom-call(bf16[2,512,256]{2,1,0:T(8,128)(2,1)S(1)} %get-tuple-element.97.left, bf16[2,256,512]{2,1,0:T(8,128)(2,1)S(1)} %get-tuple-element.76.left_t, s16[512,1024]{1,0:T(8,128)(2,1)S(1)} %ratings.1.values, ...), custom_call_target="tpu_custom_call" | custom-call | flops 1024 | bytes 1024 | tf_op jit(solution)/shard_map/push/pallas_call | solution.py:323
  61.9 1.3 %collective-permute-start.8 = (s32[160,512]{1,0:T(8,128)S(1)}, s32[160,512]{1,0:T(8,128)S(1)}, u32[]{:S(2)}, u32[]{:S(2)}) collective-permute-start(s32[160,512]{1,0:T(8,128)S(1)} %get-tuple-element.95), channel_id=1, source_target_pairs={{2,4},{6,8},{10,12},{14,16},{18,20},{22,24},{26,28},{30,32},{34,36... | collective-permute-start | bytes 983048 | tf_op jit(solution)/shard_map/ppermute | solution.py:353
  63.2 0.2 collective-permute-done.3.refs_0_
  63.4 1.3 %collective-permute-start.9 = (s32[152,512]{1,0:T(8,128)S(1)}, s32[152,512]{1,0:T(8,128)S(1)}, u32[]{:S(2)}, u32[]{:S(2)}) collective-permute-start(s32[152,512]{1,0:T(8,128)S(1)} %get-tuple-element.104), channel_id=1, source_target_pairs={{2,4},{6,8},{10,12},{14,16},{18,20},{22,24},{26,28},{30,32},{34,36... | collective-permute-start | bytes 933896 | tf_op jit(solution)/shard_map/ppermute | solution.py:353
  64.7 1.1 %pull.6 = (f32[512,256]{1,0:T(8,128)S(1)}, bf16[2,512,256]{2,1,0:T(8,128)(2,1)S(1)}, bf16[2,256,512]{2,1,0:T(8,128)(2,1)S(1)}) custom-call(f32[512,256]{1,0:T(8,128)S(1)} %copy-done, bf16[2,512,512]{2,1,0:T(8,128)(2,1)S(1)} %get-tuple-element.106.err_a, bf16[2,256,512]{2,1,0:T(8,128)(2,1)S(1)} %get-tuple-element.107.right_a, ...), custom_call_target="tpu_custom_call" | custom-call | flops 1024 | bytes 1024 | tf_op jit(solution)/shard_map/pull/pallas_call | solution.py:335
  65.8 5.0 %collective-permute-done.4.refs_0_ = s32[144,512]{1,0:T(8,128)S(1)} collective-permute-done((s32[144,512]{1,0:T(8,128)S(1)}, s32[144,512]{1,0:T(8,128)S(1)}, u32[]{:S(2)}, u32[]{:S(2)}) %collective-permute-start.4) | collective-permute-done | bytes 294944 | tf_op jit(solution)/shard_map/ppermute | solution.py:353
  70.8 1.6 %push.18 = (bf16[2,512,512]{2,1,0:T(8,128)(2,1)S(1)}, bf16[2,256,512]{2,1,0:T(8,128)(2,1)S(1)}, s32[136,512]{1,0:T(8,128)S(1)}) custom-call(bf16[2,512,256]{2,1,0:T(8,128)(2,1)S(1)} %get-tuple-element.117.left, bf16[2,256,512]{2,1,0:T(8,128)(2,1)S(1)} %get-tuple-element.111.left_t, s16[512,1024]{1,0:T(8,128)(2,1)S(1)} %ratings.1.values, ...), custom_call_target="tpu_custom_call" | custom-call | flops 1024 | bytes 1024 | tf_op jit(solution)/shard_map/push/pallas_call | solution.py:323
  72.5 1.4 %collective-permute-done.6.refs_0_ = s32[144,512]{1,0:T(8,128)S(1)} collective-permute-done((s32[144,512]{1,0:T(8,128)S(1)}, s32[144,512]{1,0:T(8,128)S(1)}, u32[]{:S(2)}, u32[]{:S(2)}) %collective-permute-start.6) | collective-permute-done | bytes 294944 | tf_op jit(solution)/shard_map/ppermute | solution.py:353
  74.0 1.6 %push.20 = (bf16[2,512,512]{2,1,0:T(8,128)(2,1)S(1)}, bf16[2,256,512]{2,1,0:T(8,128)(2,1)S(1)}, s32[136,512]{1,0:T(8,128)S(1)}) custom-call(bf16[2,512,256]{2,1,0:T(8,128)(2,1)S(1)} %get-tuple-element.117.left, bf16[2,256,512]{2,1,0:T(8,128)(2,1)S(1)} %get-tuple-element.111.left_t, s16[512,1024]{1,0:T(8,128)(2,1)S(1)} %ratings.1.values, ...), custom_call_target="tpu_custom_call" | custom-call | flops 1024 | bytes 1024 | tf_op jit(solution)/shard_map/push/pallas_call | solution.py:323
  75.8 1.3 %collective-permute-start.13 = (s32[144,512]{1,0:T(8,128)S(1)}, s32[144,512]{1,0:T(8,128)S(1)}, u32[]{:S(2)}, u32[]{:S(2)}) collective-permute-start(s32[144,512]{1,0:T(8,128)S(1)} %get-tuple-element.115), channel_id=1, source_target_pairs={{2,4},{6,8},{10,12},{14,16},{18,20},{22,24},{26,28},{30,32},{34,36... | collective-permute-start | bytes 884744 | tf_op jit(solution)/shard_map/ppermute | solution.py:353
  77.1 0.2 collective-permute-done.7.refs_0_
  77.3 1.3 %collective-permute-start.11 = (s32[144,512]{1,0:T(8,128)S(1)}, s32[144,512]{1,0:T(8,128)S(1)}, u32[]{:S(2)}, u32[]{:S(2)}) collective-permute-start(s32[144,512]{1,0:T(8,128)S(1)} %get-tuple-element.122), channel_id=1, source_target_pairs={{2,4},{6,8},{10,12},{14,16},{18,20},{22,24},{26,28},{30,32},{34,36... | collective-permute-start | bytes 884744 | tf_op jit(solution)/shard_map/ppermute | solution.py:353
  78.6 1.1 %pull.7 = (f32[512,256]{1,0:T(8,128)S(1)}, bf16[2,512,256]{2,1,0:T(8,128)(2,1)S(1)}, bf16[2,256,512]{2,1,0:T(8,128)(2,1)S(1)}) custom-call(f32[512,256]{1,0:T(8,128)S(1)} %get-tuple-element.123.users, bf16[2,512,512]{2,1,0:T(8,128)(2,1)S(1)} %get-tuple-element.124.err_a, bf16[2,256,512]{2,1,0:T(8,128)(2,1)S(1)} %get-tuple-element.125.right_a, ...), custom_call_target="tpu_custom_call" | custom-call | flops 1024 | bytes 1024 | tf_op jit(solution)/shard_map/pull/pallas_call | solution.py:335
  79.8 1.6 %push.22 = (bf16[2,512,512]{2,1,0:T(8,128)(2,1)S(1)}, bf16[2,256,512]{2,1,0:T(8,128)(2,1)S(1)}, s32[136,512]{1,0:T(8,128)S(1)}) custom-call(bf16[2,512,256]{2,1,0:T(8,128)(2,1)S(1)} %get-tuple-element.134.left, bf16[2,256,512]{2,1,0:T(8,128)(2,1)S(1)} %get-tuple-element.130.left_t, s16[512,1024]{1,0:T(8,128)(2,1)S(1)} %ratings.1.values, ...), custom_call_target="tpu_custom_call" | custom-call | flops 1024 | bytes 1024 | tf_op jit(solution)/shard_map/push/pallas_call | solution.py:323
  81.4 2.2 %collective-permute-start.12 = (s32[136,512]{1,0:T(8,128)S(1)}, s32[136,512]{1,0:T(8,128)S(1)}, u32[]{:S(2)}, u32[]{:S(2)}) collective-permute-start(s32[136,512]{1,0:T(8,128)S(1)} %get-tuple-element.133), channel_id=1, source_target_pairs={{0,2},{2,0},{4,6},{6,4},{8,10},{10,8},{12,14},{14,12},{16,18},{18,... | collective-permute-start | bytes 835592 | tf_op jit(solution)/shard_map/ppermute | solution.py:353
  83.6 1.6 %push.23 = (bf16[2,512,512]{2,1,0:T(8,128)(2,1)S(1)}, bf16[2,256,512]{2,1,0:T(8,128)(2,1)S(1)}, s32[136,512]{1,0:T(8,128)S(1)}) custom-call(bf16[2,512,256]{2,1,0:T(8,128)(2,1)S(1)} %get-tuple-element.134.left, bf16[2,256,512]{2,1,0:T(8,128)(2,1)S(1)} %get-tuple-element.130.left_t, s16[512,1024]{1,0:T(8,128)(2,1)S(1)} %ratings.1.values, ...), custom_call_target="tpu_custom_call" | custom-call | flops 1024 | bytes 1024 | tf_op jit(solution)/shard_map/push/pallas_call | solution.py:323
  85.4 1.1 %last_pull.1 = (f32[512,256]{1,0:T(8,128)S(1)}, bf16[2,512,256]{2,1,0:T(8,128)(2,1)S(1)}, bf16[2,256,512]{2,1,0:T(8,128)(2,1)S(1)}) custom-call(f32[512,256]{1,0:T(8,128)S(1)} %get-tuple-element.101.refs_0_, bf16[2,512,512]{2,1,0:T(8,128)(2,1)S(1)} %get-tuple-element.113.refs_1_, bf16[2,256,512]{2,1,0:T(8,128)(2,1)S(1)} %get-tuple-element.114.refs_2_, ...), custom_call_target="tpu_custom_call" | custom-call | flops 1024 | bytes 1024 | tf_op jit(solution)/shard_map/last_pull/pallas_call | solution.py:370
  86.5 3.0 %collective-permute-done.13.got_e = s32[144,512]{1,0:T(8,128)S(1)} collective-permute-done((s32[144,512]{1,0:T(8,128)S(1)}, s32[144,512]{1,0:T(8,128)S(1)}, u32[]{:S(2)}, u32[]{:S(2)}) %collective-permute-start.13) | collective-permute-done | bytes 294944 | tf_op jit(solution)/shard_map/ppermute | solution.py:353
  89.5 2.3 %last_first.1 = (f32[1024,256]{1,0:T(8,128)}, bf16[2,512,512]{2,1,0:T(8,128)(2,1)S(1)}, bf16[2,256,512]{2,1,0:T(8,128)(2,1)S(1)}) custom-call(bf16[2,512,256]{2,1,0:T(8,128)(2,1)S(1)} %get-tuple-element.137.left, bf16[2,256,512]{2,1,0:T(8,128)(2,1)S(1)} %get-tuple-element.138.left_t, s16[512,1024]{1,0:T(8,128)(2,1)S(1)} %ratings.1.values, ...), custom_call_target="tpu_custom_call" | custom-call | flops 1024 | bytes 1024 | tf_op jit(solution)/shard_map/last_first/pallas_call | solution.py:382
  91.9 0.9 collective-permute-done.11.got_e
  92.7 3.1 %last_second.1 = (f32[1024,256]{1,0:T(8,128)}, f32[512,256]{1,0:T(8,128)}) custom-call(bf16[2,512,256]{2,1,0:T(8,128)(2,1)S(1)} %get-tuple-element.137.left, bf16[2,256,512]{2,1,0:T(8,128)(2,1)S(1)} %get-tuple-element.138.left_t, s16[512,1024]{1,0:T(8,128)(2,1)S(1)} %ratings.1.values, ...), custom_call_target="tpu_custom_call", output_to_operand_aliasing={{0}: (8, {})} | custom-call | flops 1024 | bytes 1024 | tf_op jit(solution)/shard_map/last_second/pallas_call | solution.py:392
  (28 shorter events, 0.7 us)
Async XLA Ops:
  0.6 11.9 %copy-start.2 = (bf16[2048,256]{1,0:T(8,128)(2,1)S(1)}, bf16[2048,256]{1,0:T(8,128)(2,1)}, u32[]{:S(2)}) copy-start(bf16[2048,256]{1,0:T(8,128)(2,1)} %content.1) | copy-start | bytes 3145732
  0.6 11.9 %copy-start.3 = (s32[1,1024]{1,0:T(1,128)S(1)}, s32[1,1024]{1,0:T(1,128)}, u32[]{:S(2)}) copy-start(s32[1,1024]{1,0:T(1,128)} %order) | copy-start | bytes 12292
  0.7 11.9 %copy-start = (f32[512,256]{1,0:T(8,128)S(1)}, f32[512,256]{1,0:T(8,128)}, u32[]{:S(2)}) copy-start(f32[512,256]{1,0:T(8,128)} %users.4) | copy-start | bytes 1572868
  0.7 11.9 %copy-start.1 = (bf16[512,256]{1,0:T(8,128)(2,1)S(1)}, bf16[512,256]{1,0:T(8,128)(2,1)}, u32[]{:S(2)}) copy-start(bf16[512,256]{1,0:T(8,128)(2,1)} %weights.3) | copy-start | bytes 786436
  1.9 12.4 %collective-permute-start.1 = (bf16[512,256]{1,0:T(8,128)(2,1)S(1)}, bf16[512,256]{1,0:T(8,128)(2,1)S(1)}, u32[]{:S(2)}, u32[]{:S(2)}) collective-permute-start(bf16[512,256]{1,0:T(8,128)(2,1)S(1)} %get-tuple-element.146), channel_id=1, source_target_pairs={{0,1},{1,0},{2,3},{3,2},{4,5},{5,4},{6,7},{7,6},{8,9},{9,8},{10,11... | collective-permute-start | bytes 786440 | tf_op jit(solution)/shard_map/ppermute | solution.py:269
  4.1 11.5 %collective-permute-start = (bf16[512,256]{1,0:T(8,128)(2,1)S(1)}, bf16[512,256]{1,0:T(8,128)(2,1)S(1)}, u32[]{:S(2)}, u32[]{:S(2)}) collective-permute-start(bf16[512,256]{1,0:T(8,128)(2,1)S(1)} %get-tuple-element.147), channel_id=1, source_target_pairs={{0,1},{1,0},{2,3},{3,2},{4,5},{5,4},{6,7},{7,6},{8,9},{9,8},{10,11... | collective-permute-start | bytes 786440 | tf_op jit(solution)/shard_map/ppermute | solution.py:269
  54.8 7.0 %collective-permute-start.2 = (s32[136,512]{1,0:T(8,128)S(1)}, s32[136,512]{1,0:T(8,128)S(1)}, u32[]{:S(2)}, u32[]{:S(2)}) collective-permute-start(s32[136,512]{1,0:T(8,128)S(1)} %get-tuple-element.92), channel_id=1, source_target_pairs={{0,2},{2,0},{4,6},{6,4},{8,10},{10,8},{12,14},{14,12},{16,18},{18,... | collective-permute-start | bytes 835592 | tf_op jit(solution)/shard_map/ppermute | solution.py:353
  57.1 13.8 %collective-permute-start.4 = (s32[144,512]{1,0:T(8,128)S(1)}, s32[144,512]{1,0:T(8,128)S(1)}, u32[]{:S(2)}, u32[]{:S(2)}) collective-permute-start(s32[144,512]{1,0:T(8,128)S(1)} %get-tuple-element.83), channel_id=1, source_target_pairs={{2,4},{6,8},{10,12},{14,16},{18,20},{22,24},{26,28},{30,32},{34,36... | collective-permute-start | bytes 884744 | tf_op jit(solution)/shard_map/ppermute | solution.py:353
  58.3 15.6 %collective-permute-start.6 = (s32[144,512]{1,0:T(8,128)S(1)}, s32[144,512]{1,0:T(8,128)S(1)}, u32[]{:S(2)}, u32[]{:S(2)}) collective-permute-start(s32[144,512]{1,0:T(8,128)S(1)} %get-tuple-element.90), channel_id=1, source_target_pairs={{2,4},{6,8},{10,12},{14,16},{18,20},{22,24},{26,28},{30,32},{34,36... | collective-permute-start | bytes 884744 | tf_op jit(solution)/shard_map/ppermute | solution.py:353
  61.7 1.6 %collective-permute-start.3 = (s32[136,512]{1,0:T(8,128)S(1)}, s32[136,512]{1,0:T(8,128)S(1)}, u32[]{:S(2)}, u32[]{:S(2)}) collective-permute-start(s32[136,512]{1,0:T(8,128)S(1)} %get-tuple-element.98), channel_id=1, source_target_pairs={{0,2},{2,0},{4,6},{6,4},{8,10},{10,8},{12,14},{14,12},{16,18},{18,... | collective-permute-start | bytes 835592 | tf_op jit(solution)/shard_map/ppermute | solution.py:353
  61.9 17.9 %collective-permute-start.8 = (s32[160,512]{1,0:T(8,128)S(1)}, s32[160,512]{1,0:T(8,128)S(1)}, u32[]{:S(2)}, u32[]{:S(2)}) collective-permute-start(s32[160,512]{1,0:T(8,128)S(1)} %get-tuple-element.95), channel_id=1, source_target_pairs={{2,4},{6,8},{10,12},{14,16},{18,20},{22,24},{26,28},{30,32},{34,36... | collective-permute-start | bytes 983048 | tf_op jit(solution)/shard_map/ppermute | solution.py:353
  63.4 20.3 %collective-permute-start.9 = (s32[152,512]{1,0:T(8,128)S(1)}, s32[152,512]{1,0:T(8,128)S(1)}, u32[]{:S(2)}, u32[]{:S(2)}) collective-permute-start(s32[152,512]{1,0:T(8,128)S(1)} %get-tuple-element.104), channel_id=1, source_target_pairs={{2,4},{6,8},{10,12},{14,16},{18,20},{22,24},{26,28},{30,32},{34,36... | collective-permute-start | bytes 933896 | tf_op jit(solution)/shard_map/ppermute | solution.py:353
  72.4 3.3 %collective-permute-start.5 = (s32[136,512]{1,0:T(8,128)S(1)}, s32[136,512]{1,0:T(8,128)S(1)}, u32[]{:S(2)}, u32[]{:S(2)}) collective-permute-start(s32[136,512]{1,0:T(8,128)S(1)} %get-tuple-element.112), channel_id=1, source_target_pairs={{0,2},{2,0},{4,6},{6,4},{8,10},{10,8},{12,14},{14,12},{16,18},{18,... | collective-permute-start | bytes 835592 | tf_op jit(solution)/shard_map/ppermute | solution.py:353
  75.6 1.6 %collective-permute-start.7 = (s32[136,512]{1,0:T(8,128)S(1)}, s32[136,512]{1,0:T(8,128)S(1)}, u32[]{:S(2)}, u32[]{:S(2)}) collective-permute-start(s32[136,512]{1,0:T(8,128)S(1)} %get-tuple-element.118), channel_id=1, source_target_pairs={{0,2},{2,0},{4,6},{6,4},{8,10},{10,8},{12,14},{14,12},{16,18},{18,... | collective-permute-start | bytes 835592 | tf_op jit(solution)/shard_map/ppermute | solution.py:353
  75.8 13.8 %collective-permute-start.13 = (s32[144,512]{1,0:T(8,128)S(1)}, s32[144,512]{1,0:T(8,128)S(1)}, u32[]{:S(2)}, u32[]{:S(2)}) collective-permute-start(s32[144,512]{1,0:T(8,128)S(1)} %get-tuple-element.115), channel_id=1, source_target_pairs={{2,4},{6,8},{10,12},{14,16},{18,20},{22,24},{26,28},{30,32},{34,36... | collective-permute-start | bytes 884744 | tf_op jit(solution)/shard_map/ppermute | solution.py:353
  77.3 15.4 %collective-permute-start.11 = (s32[144,512]{1,0:T(8,128)S(1)}, s32[144,512]{1,0:T(8,128)S(1)}, u32[]{:S(2)}, u32[]{:S(2)}) collective-permute-start(s32[144,512]{1,0:T(8,128)S(1)} %get-tuple-element.122), channel_id=1, source_target_pairs={{2,4},{6,8},{10,12},{14,16},{18,20},{22,24},{26,28},{30,32},{34,36... | collective-permute-start | bytes 884744 | tf_op jit(solution)/shard_map/ppermute | solution.py:353
  81.4 8.1 %collective-permute-start.12 = (s32[136,512]{1,0:T(8,128)S(1)}, s32[136,512]{1,0:T(8,128)S(1)}, u32[]{:S(2)}, u32[]{:S(2)}) collective-permute-start(s32[136,512]{1,0:T(8,128)S(1)} %get-tuple-element.133), channel_id=1, source_target_pairs={{0,2},{2,0},{4,6},{6,4},{8,10},{10,8},{12,14},{14,12},{16,18},{18,... | collective-permute-start | bytes 835592 | tf_op jit(solution)/shard_map/ppermute | solution.py:353
  85.3 7.5 %collective-permute-start.10 = (s32[136,512]{1,0:T(8,128)S(1)}, s32[136,512]{1,0:T(8,128)S(1)}, u32[]{:S(2)}, u32[]{:S(2)}) collective-permute-start(s32[136,512]{1,0:T(8,128)S(1)} %get-tuple-element.139), channel_id=1, source_target_pairs={{0,2},{2,0},{4,6},{6,4},{8,10},{10,8},{12,14},{14,12},{16,18},{18,... | collective-permute-start | bytes 835592 | tf_op jit(solution)/shard_map/ppermute | solution.py:353

commit v4 on v3

--- a/solution.py
+++ b/solution.py
@@ -14,8 +14,8 @@
 CONTENT_BOUND = 6.0
 LOG_RANGE = 14.0
 TOP = 32767.0
-EVEN_TAILS = ((16, 16), (32, 24), (16, 16))
-ODD_TAILS = ((8, 8), (8, 8), (8, 8))
+EVEN_TAIL = 16
+ODD_TAIL = 8
 F32 = jnp.float32
 BF16 = jnp.bfloat16
 I32 = jnp.int32
@@ -146,12 +146,12 @@
     return jnp.concatenate([a, b], axis=0) * scale
 
 
-def errors_and_items(q, here, cols, left, left_t, values, t, err, right):
+def errors_and_items(q, here, left, left_t, values, t, err, right):
     q_hi, q_lo = split(q)
     right[0, :, here] = q_hi
     right[1, :, here] = q_lo
     guess = mm(left[0], q_hi) + mm(left[0], q_lo) + mm(left[1], q_hi)
-    v = (lax.shift_right_logical(values[:, cols].astype(I32), 3 * t) & 7).astype(F32)
+    v = (lax.shift_right_logical(values[:, here].astype(I32), 3 * t) & 7).astype(F32)
     e_hi, e_lo = split(jnp.where(v > 0, v - guess, 0.0))
     err[0, :, here] = e_hi
     err[1, :, here] = e_lo
@@ -172,7 +172,7 @@
     return lax.rem(lax.axis_index("blk"), 2) == turn
 
 
-def push_kernel(turn, t, half, left, left_t, values, *refs):
+def push_kernel(turn, t, left, left_t, values, *refs):
     source, (err, right, out) = refs[:-3], refs[-3:]
     wide = out.shape[1]
 
@@ -180,75 +180,51 @@
     def _():
         for at in range(0, wide, CHUNK):
             here = slice(at, at + CHUNK)
-            cols = slice(half * wide + at, half * wide + at + CHUNK)
             if t == 0:
-                q = first_items(*source, cols)
+                q = first_items(*source, here)
             else:
                 q = decode(source[0][:, here], right.shape[1])
-            new = errors_and_items(q, here, cols, left, left_t, values, t, err, right)
+            new = errors_and_items(q, here, left, left_t, values, t, err, right)
             words, level = encode(new)
             rows = words.shape[0]
             out[:rows, here] = words
             out[rows:, here] = jnp.broadcast_to(level, (out.shape[0] - rows, CHUNK))
 
 
-def user_step(users, parts, rows=slice(None)):
+def user_step(users, err, right, rows=slice(None)):
     dims = ((1,), (1,))
-    grad = None
-    for err, right in parts:
-        hi, lo = err[0, rows, :], err[1, rows, :]
-        for a, b in ((hi, right[0]), (hi, right[1]), (lo, right[0])):
-            term = mm(a, b, dims)
-            grad = term if grad is None else grad + term
+    hi, lo = err[0, rows, :], err[1, rows, :]
+    grad = mm(hi, right[0], dims) + mm(hi, right[1], dims) + mm(lo, right[0], dims)
     return KEEP * users[rows, :] + learn_rate * grad
 
 
-def pull_kernel(turn, users, err_a, right_a, err_b, right_b, new_users, left, left_t):
-    @pl.when(my_turn(turn))
-    def _():
-        put_users(user_step(users, ((err_a, right_a), (err_b, right_b))), new_users, left, left_t)
-
-
-def last_pull_kernel(*refs):
-    outs = refs[10:]
-    for turn, (users, *parts) in ((1, refs[:5]), (0, refs[5:10])):
+def pull_kernel(users, err_o, right_o, err_e, right_e, *outs):
+    for turn, err, right in ((1, err_o, right_o), (0, err_e, right_e)):
 
         @pl.when(my_turn(turn))
         def _():
-            put_users(user_step(users, (parts[:2], parts[2:])), *outs)
-
-
-def last_items(half, left, left_t, values, got_o, got_e, items_out, err, right, held, sems):
-    wide = right.shape[2]
+            put_users(user_step(users, err, right), *outs)
+
+
+def last_kernel(left, left_t, values, users, got_o, got_e, items_out, users_out, err, right, held, users_held, sems):
     live = right.shape[1] // 2 + 8
+    tall = users_held.shape[0] // 2
     is_odd = my_turn(1)
     copies = []
-    for at in range(0, wide, CHUNK):
+
+    def put(source, target, rows):
+        copies.append(pltpu.make_async_copy(source.at[rows, :], target.at[rows, :], sems.at[len(copies)]))
+        copies[-1].start()
+
+    for at in range(0, right.shape[2], CHUNK):
         here = slice(at, at + CHUNK)
-        cols = slice(half * wide + at, half * wide + at + CHUNK)
         q = decode(jnp.where(is_odd, got_o[:live, here], got_e[:live, here]), right.shape[1])
-        held[here, :] = errors_and_items(q, here, cols, left, left_t, values, ROUNDS - 1, err, right).T
-        copies.append(pltpu.make_async_copy(held.at[here, :], items_out.at[cols, :], sems.at[len(copies)]))
-        copies[-1].start()
-    return copies
-
-
-def last_first_kernel(left, left_t, values, got_o, got_e, items_out, err, right, held, sems):
-    for copy in last_items(0, left, left_t, values, got_o, got_e, items_out, err, right, held, sems):
-        copy.wait()
-
-
-def last_second_kernel(
-    left, left_t, values, got_o, got_e, users, err_a, right_a, items_in,
-    items_out, users_out, err, right, held, users_held, sems,
-):
-    copies = last_items(1, left, left_t, values, got_o, got_e, items_out, err, right, held, sems)
-    tall = users_held.shape[0] // 2
+        held[here, :] = errors_and_items(q, here, left, left_t, values, ROUNDS - 1, err, right).T
+        put(held, items_out, here)
     for at in (0, tall):
         rows = slice(at, at + tall)
-        users_held[rows, :] = user_step(users, ((err_a, right_a), (err, right)), rows)
-        copies.append(pltpu.make_async_copy(users_held.at[rows, :], users_out.at[rows, :], sems.at[len(copies)]))
-        copies[-1].start()
+        users_held[rows, :] = user_step(users, err, right, rows)
+        put(users_held, users_out, rows)
     for copy in copies:
         copy.wait()
 
@@ -314,15 +290,15 @@
         coded.reshape(n_blk, share, rank // 2), "blk", split_axis=0, concat_axis=0, tiled=True
     ).reshape(n_items, rank // 2)
 
-    half_shapes = [struct((2, n_users, wide), BF16), struct((2, rank, wide), BF16)]
-    to_even = [(i, (i + 1) % n_blk) for i in range(1, n_blk, 2)]
-    to_odd = [(i, i ^ 1) for i in range(n_blk)]
+    state_shapes = [struct((2, n_users, n_items), BF16), struct((2, rank, n_items), BF16)]
+    ring = [(i, (i + 1) % n_blk) for i in range(n_blk)]
+    pair = [(i, i ^ 1) for i in range(n_blk)]
     light = cost(1 << 10, 1 << 10)
 
-    def push(turn, t, half, left, left_t, source, tail):
+    def push(turn, t, left, source, tail):
         *state, sent = pl.pallas_call(
-            functools.partial(push_kernel, turn, t, half),
-            out_shape=half_shapes + [struct((rank // 2 + tail, wide), I32)],
+            functools.partial(push_kernel, turn, t),
+            out_shape=state_shapes + [struct((rank // 2 + tail, n_items), I32)],
             in_specs=[VM] * (3 + len(source)),
             out_specs=[VM] * 3,
             compiler_params=params(),
@@ -331,81 +307,42 @@
         )(left, left_t, values, *source)
         return state, sent
 
-    def pull(turn, users, states):
-        return pl.pallas_call(
-            functools.partial(pull_kernel, turn),
+    users = user_factors
+    for_odd = for_even = [dealt, meta]
+    for t in range(ROUNDS - 1):
+        odd_state, sent = push(1, t, left, for_odd, EVEN_TAIL)
+        next_even = [lax.ppermute(sent, "blk", ring)]
+        later, _ = lax.optimization_barrier((left, sent))
+        even_state, sent = push(0, t, later, for_even, ODD_TAIL)
+        next_odd = [lax.ppermute(sent, "blk", pair)]
+        users, left, left_t = pl.pallas_call(
+            pull_kernel,
             out_shape=[struct((n_users, rank), F32)] + split_shapes,
             in_specs=[VM] * 5,
             out_specs=[VM] * 3,
             compiler_params=params(),
             cost_estimate=light,
             name="pull",
-        )(users, *states[0], *states[1])
-
-    def after(x, done):
-        return lax.optimization_barrier((x, done))[0]
-
-    def both(turn, t, left, left_t, sources, tails, pairs):
-        states, nexts = [], []
-        for half in range(2):
-            state, sent = push(turn, t, half, left, left_t, sources[half], tails[half])
-            states.append(state)
-            nexts.append([lax.ppermute(sent, "blk", pairs)])
-            left = after(left, sent)
-        return states, nexts, sent
-
-    odd = even = (user_factors, left, left_t)
-    for_odd = for_even = [[dealt, meta]] * 2
-    even_states = None
-    for t in range(ROUNDS - 1):
-        odd_states, next_even, sent = both(1, t, *odd[1:], for_odd, EVEN_TAILS[t], to_even)
-        if even_states is None:
-            even = (even[0], after(even[1], sent), even[2])
-        else:
-            even = pull(0, after(even[0], sent), even_states)
-        even_states, next_odd, _ = both(0, t, *even[1:], for_even, ODD_TAILS[t], to_odd)
+        )(users, *odd_state, *even_state)
         for_even, for_odd = next_even, next_odd
-        if t < ROUNDS - 2:
-            odd = pull(1, odd[0], odd_states)
-    users, left, left_t = pl.pallas_call(
-        last_pull_kernel,
-        out_shape=[struct((n_users, rank), F32)] + split_shapes,
-        in_specs=[VM] * 10,
-        out_specs=[VM] * 3,
-        compiler_params=params(),
-        cost_estimate=light,
-        name="last_pull",
-    )(odd[0], *odd_states[0], *odd_states[1], even[0], *even_states[0], *even_states[1])
 
     anywhere = pl.BlockSpec(memory_space=pl.ANY)
-    held_shapes = [pltpu.VMEM((wide, rank), F32)]
-    items, err, right = pl.pallas_call(
-        last_first_kernel,
-        out_shape=[pltpu.HBM((n_items, rank), F32)] + half_shapes,
-        in_specs=[VM] * 5,
-        out_specs=[anywhere, VM, VM],
-        scratch_shapes=held_shapes + [pltpu.SemaphoreType.DMA((wide // CHUNK,))],
-        compiler_params=params(),
-        cost_estimate=light,
-        name="last_first",
-    )(left, left_t, values, *for_odd[0], *for_even[0])
     items, users = pl.pallas_call(
-        last_second_kernel,
+        last_kernel,
         out_shape=[struct((n_items, rank), F32), struct((n_users, rank), F32)],
-        in_specs=[VM] * 8 + [anywhere],
+        in_specs=[VM] * 6,
         out_specs=[anywhere] * 2,
         scratch_shapes=[
-            pltpu.VMEM((2, n_users, wide), BF16),
-            pltpu.VMEM((2, rank, wide), BF16),
-        ] + held_shapes + [
+            pltpu.VMEM((2, n_users, n_items), BF16),
+            pltpu.VMEM((2, rank, n_items), BF16),
+            pltpu.VMEM((n_items, rank), F32),
             pltpu.VMEM((n_users, rank), F32),
-            pltpu.SemaphoreType.DMA((wide // CHUNK + 2,)),
+            pltpu.SemaphoreType.DMA((n_items // CHUNK + 2,)),
         ],
-        input_output_aliases={8: 0},
         compiler_params=params(16),
         cost_estimate=light,
-        name="last_second",
-    )(left, left_t, values, *for_odd[1], *for_even[1], users, err, right, items)
+        name="last",
+    )(left, left_t, values, users, *for_odd, *for_even)
     return users, items
 
 

time: 96.4 us -> 91.9 us (0.953)
  Pallas kernels: 30.5 us -> 26.9 us
  starting transfers between devices: 14.9 us -> 11.6 us
  waiting for transfers between devices: 12.1 us -> 14.9 us
    pallas_call x19 -> x10, Pallas kernels: 19.5 us -> 15.7 us  [the longest x6 8.22 us: push(): pl.pallas_call(functools.partial(push_kernel, turn, t), out_shape=state_s...]
    ppermute x12 -> x6, starting transfers between devices: 12.6 us -> 9.25 us  [the longest x3 8.97 us: body(): next_even = [lax.ppermute(sent, 'blk', ring)]]
    ppermute x12 -> x6, waiting for transfers between devices: 10.7 us -> 13.7 us  [the longest x3 11.3 us: body(): next_even = [lax.ppermute(sent, 'blk', ring)]]
  transfers between devices with their start and end apart: 14 -> 8, of which waited for: 7 -> 7; matrix products, arithmetic and copies ran while one was open for 0% -> 0% of each run, Pallas kernels for 25% -> 24%
where the time goes in v4:
time: 91.9 us; the launch traced here: 91.7 us
  blocking collectives  36.1 us (39%)
  Pallas kernels  26.9 us (29%)
  waiting for transfers between devices  14.9 us (16%)
  starting transfers between devices  11.6 us (13%)
  local copies, waits for them, and re-layouts  1.08 us (1%)
  between operations  0.96 us (1%)
    all_to_all x1, blocking collectives, body(): lax.all_to_all(coded.reshape(n_blk, share, rank // 2), 'blk', split_axis=...  36.1 us
    ppermute x3, waiting for transfers between devices, body(): next_even = [lax.ppermute(sent, 'blk', ring)]  11.3 us
    ppermute x3, starting transfers between devices, body(): next_even = [lax.ppermute(sent, 'blk', ring)]  8.97 us
    pallas_call x1, Pallas kernels, body(): pl.pallas_call(ratings_kernel, out_shape=struct((n_users, n_items), jnp.i...  8.38 us
    pallas_call x6, Pallas kernels, push(): pl.pallas_call(functools.partial(push_kernel, turn, t), out_shape=state_s...  8.22 us
    pallas_call x1, Pallas kernels, body(): pl.pallas_call(last_kernel, out_shape=[struct((n_items, rank), F32), stru...  4.05 us
    pallas_call x3, Pallas kernels, body(): pl.pallas_call(pull_kernel, out_shape=[struct((n_users, rank), F32)] + sp...  3.43 us
    ppermute x3, waiting for transfers between devices, body(): next_odd = [lax.ppermute(sent, 'blk', pair)]  2.38 us
  transfers between devices with their start and end apart: 8, of which 7 were waited for; matrix products, arithmetic and copies ran while one was open for 0% of the time, Pallas kernels for 24%

profile of v4, /device:TPU:8, one launch (start us, length us, event | category | flops | bytes accessed | tf_op | source)
XLA Modules:
  0.0 91.7 jit_solution(2711884187902401074)
XLA Ops:
  0.6 1.1 %constant_dynamic-slice_fusion.1 = (bf16[512,256]{1,0:T(8,128)(2,1)S(1)}, bf16[512,256]{1,0:T(8,128)(2,1)S(1)}) fusion(bf16[2048,256]{1,0:T(8,128)(2,1)} %content.1, s32[]{:T(128)S(6)} %add.4, s32[]{:T(128)S(6)} %select_n.3), kind=kLoop, calls=%fused_computation.1 | loop fusion | bytes 1048584 | tf_op jit(solution)/shard_map/slice | solution.py:245
  1.7 2.3 %collective-permute-start.1 = (bf16[512,256]{1,0:T(8,128)(2,1)S(1)}, bf16[512,256]{1,0:T(8,128)(2,1)S(1)}, u32[]{:S(2)}, u32[]{:S(2)}) collective-permute-start(bf16[512,256]{1,0:T(8,128)(2,1)S(1)} %get-tuple-element.80), channel_id=1, source_target_pairs={{0,1},{1,0},{2,3},{3,2},{4,5},{5,4},{6,7},{7,6},{8,9},{9,8},{10,11... | collective-permute-start | bytes 786440 | tf_op jit(solution)/shard_map/ppermute | solution.py:245
  4.0 0.1 collective-permute-start
  4.1 8.4 %ratings.1.values = s16[512,1024]{1,0:T(8,128)(2,1)S(1)} custom-call(s32[16384,128]{1,0:T(8,128)} %bitcast.10), custom_call_target="tpu_custom_call" | custom-call | flops 1048576 | bytes 12582912 | tf_op jit(solution)/shard_map/ratings/pallas_call | solution.py:250
  12.5 0.0 copy-done
  12.5 0.0 copy-done.1
  12.5 0.0 copy-done.2
  12.5 0.0 copy-done.3
  12.5 1.7 %before.1 = (bf16[1024,1024]{1,0:T(8,128)(2,1)S(1)}, f32[1024,256]{1,0:T(8,128)S(1)}, f32[8,128]{1,0:T(8,128)S(1)}, bf16[2,512,256]{2,1,0:T(8,128)(2,1)S(1)}, bf16[2,256,512]{2,1,0:T(8,128)(2,1)S(1)}) custom-call(s32[1,1024]{1,0:T(1,128)S(1)} %copy-done.3, bf16[2048,256]{1,0:T(8,128)(2,1)S(1)} %copy-done.2, bf16[512,256]{1,0:T(8,128)(2,1)S(1)} %copy-done.1, ...), custom_call_target="tpu_custom_call" | custom-call | flops 536870912 | bytes 6291456 | tf_op jit(solution)/shard_map/before/pallas_call | solution.py:262
  14.2 0.0 collective-permute-done.1.second
  14.2 1.2 %collective-permute-done.first = bf16[512,256]{1,0:T(8,128)(2,1)S(1)} collective-permute-done((bf16[512,256]{1,0:T(8,128)(2,1)S(1)}, bf16[512,256]{1,0:T(8,128)(2,1)S(1)}, u32[]{:S(2)}, u32[]{:S(2)}) %collective-permute-start) | collective-permute-done | bytes 262176 | tf_op jit(solution)/shard_map/ppermute | solution.py:245
  15.5 1.2 %project.1 = s32[1024,128]{1,0:T(8,128)S(1)} custom-call(bf16[1024,1024]{1,0:T(8,128)(2,1)S(1)} %get-tuple-element.45.deal, bf16[512,256]{1,0:T(8,128)(2,1)S(1)} %collective-permute-done.first, bf16[512,256]{1,0:T(8,128)(2,1)S(1)} %collective-permute-done.1.second, bf16[512,256]{1,0:T(8,128)(2,1)S(1)} %copy-done.1, ...), custom_call_target="tpu_custom_call" | custom-call | flops 536870912 | bytes 4194304 | tf_op jit(solution)/shard_map/project/pallas_call | solution.py:280
  16.6 36.1 %all_to_all.5 = s32[128,8,128]{2,1,0:T(8,128)S(1)} all-to-all(s32[128,8,128]{2,1,0:T(8,128)S(1)} %bitcast.9), channel_id=1, replica_groups=mesh['blk'=128,'cat'=2] {'blk'}, dimensions={0} | all-to-all | bytes 1048576 | tf_op jit(solution)/shard_map/all_to_all | solution.py:289
  52.8 3.4 %collective-permute-start.3 = (s32[144,1024]{1,0:T(8,128)S(1)}, s32[144,1024]{1,0:T(8,128)S(1)}, u32[]{:S(2)}, u32[]{:S(2)}) collective-permute-start(s32[144,1024]{1,0:T(8,128)S(1)} %get-tuple-element.50), channel_id=1, source_target_pairs={{0,2},{2,4},{4,6},{6,8},{8,10},{10,12},{12,14},{14,16},{16,18},{18... | collective-permute-start | bytes 1769480 | tf_op jit(solution)/shard_map/ppermute | solution.py:314
  56.2 3.1 %push.7 = (bf16[2,512,1024]{2,1,0:T(8,128)(2,1)S(1)}, bf16[2,256,1024]{2,1,0:T(8,128)(2,1)S(1)}, s32[136,1024]{1,0:T(8,128)S(1)}) custom-call(bf16[2,512,256]{2,1,0:T(8,128)(2,1)S(1)} %get-tuple-element.51.left, bf16[2,256,512]{2,1,0:T(8,128)(2,1)S(1)} %get-tuple-element.43.left_t, s16[512,1024]{1,0:T(8,128)(2,1)S(1)} %ratings.1.values, ...), custom_call_target="tpu_custom_call" | custom-call | flops 1024 | bytes 1024 | tf_op jit(solution)/shard_map/push/pallas_call | solution.py:299
  59.3 0.1 collective-permute-start.2
  59.4 1.2 %pull.3 = (f32[512,256]{1,0:T(8,128)S(1)}, bf16[2,512,256]{2,1,0:T(8,128)(2,1)S(1)}, bf16[2,256,512]{2,1,0:T(8,128)(2,1)S(1)}) custom-call(f32[512,256]{1,0:T(8,128)S(1)} %copy-done, bf16[2,512,1024]{2,1,0:T(8,128)(2,1)S(1)} %get-tuple-element.48.err_o, bf16[2,256,1024]{2,1,0:T(8,128)(2,1)S(1)} %get-tuple-element.49.right_o, ...), custom_call_target="tpu_custom_call" | custom-call | flops 1024 | bytes 1024 | tf_op jit(solution)/shard_map/pull/pallas_call | solution.py:318
  60.6 0.8 collective-permute-done.2.refs_0_
  61.4 2.8 %collective-permute-start.5 = (s32[144,1024]{1,0:T(8,128)S(1)}, s32[144,1024]{1,0:T(8,128)S(1)}, u32[]{:S(2)}, u32[]{:S(2)}) collective-permute-start(s32[144,1024]{1,0:T(8,128)S(1)} %get-tuple-element.60), channel_id=1, source_target_pairs={{0,2},{2,4},{4,6},{6,8},{8,10},{10,12},{12,14},{14,16},{16,18},{18... | collective-permute-start | bytes 1769480 | tf_op jit(solution)/shard_map/ppermute | solution.py:314
  64.1 3.7 %collective-permute-done.3.refs_0_ = s32[144,1024]{1,0:T(8,128)S(1)} collective-permute-done((s32[144,1024]{1,0:T(8,128)S(1)}, s32[144,1024]{1,0:T(8,128)S(1)}, u32[]{:S(2)}, u32[]{:S(2)}) %collective-permute-start.3) | collective-permute-done | bytes 589856 | tf_op jit(solution)/shard_map/ppermute | solution.py:314
  67.8 2.5 %push.9 = (bf16[2,512,1024]{2,1,0:T(8,128)(2,1)S(1)}, bf16[2,256,1024]{2,1,0:T(8,128)(2,1)S(1)}, s32[136,1024]{1,0:T(8,128)S(1)}) custom-call(bf16[2,512,256]{2,1,0:T(8,128)(2,1)S(1)} %get-tuple-element.61.left, bf16[2,256,512]{2,1,0:T(8,128)(2,1)S(1)} %get-tuple-element.56.left_t, s16[512,1024]{1,0:T(8,128)(2,1)S(1)} %ratings.1.values, ...), custom_call_target="tpu_custom_call" | custom-call | flops 1024 | bytes 1024 | tf_op jit(solution)/shard_map/push/pallas_call | solution.py:299
  70.4 0.1 collective-permute-start.4
  70.5 1.1 %pull.4 = (f32[512,256]{1,0:T(8,128)S(1)}, bf16[2,512,256]{2,1,0:T(8,128)(2,1)S(1)}, bf16[2,256,512]{2,1,0:T(8,128)(2,1)S(1)}) custom-call(f32[512,256]{1,0:T(8,128)S(1)} %get-tuple-element.54.users, bf16[2,512,1024]{2,1,0:T(8,128)(2,1)S(1)} %get-tuple-element.58.err_o, bf16[2,256,1024]{2,1,0:T(8,128)(2,1)S(1)} %get-tuple-element.59.right_o, ...), custom_call_target="tpu_custom_call" | custom-call | flops 1024 | bytes 1024 | tf_op jit(solution)/shard_map/pull/pallas_call | solution.py:318
  71.6 0.8 collective-permute-done.4.refs_0_
  72.4 2.8 %collective-permute-start.7 = (s32[144,1024]{1,0:T(8,128)S(1)}, s32[144,1024]{1,0:T(8,128)S(1)}, u32[]{:S(2)}, u32[]{:S(2)}) collective-permute-start(s32[144,1024]{1,0:T(8,128)S(1)} %get-tuple-element.70), channel_id=1, source_target_pairs={{0,2},{2,4},{4,6},{6,8},{8,10},{10,12},{12,14},{14,16},{16,18},{18... | collective-permute-start | bytes 1769480 | tf_op jit(solution)/shard_map/ppermute | solution.py:314
  75.2 1.2 %collective-permute-done.5.refs_0_ = s32[144,1024]{1,0:T(8,128)S(1)} collective-permute-done((s32[144,1024]{1,0:T(8,128)S(1)}, s32[144,1024]{1,0:T(8,128)S(1)}, u32[]{:S(2)}, u32[]{:S(2)}) %collective-permute-start.5) | collective-permute-done | bytes 589856 | tf_op jit(solution)/shard_map/ppermute | solution.py:314
  76.4 2.5 %push.11 = (bf16[2,512,1024]{2,1,0:T(8,128)(2,1)S(1)}, bf16[2,256,1024]{2,1,0:T(8,128)(2,1)S(1)}, s32[136,1024]{1,0:T(8,128)S(1)}) custom-call(bf16[2,512,256]{2,1,0:T(8,128)(2,1)S(1)} %get-tuple-element.71.left, bf16[2,256,512]{2,1,0:T(8,128)(2,1)S(1)} %get-tuple-element.66.left_t, s16[512,1024]{1,0:T(8,128)(2,1)S(1)} %ratings.1.values, ...), custom_call_target="tpu_custom_call" | custom-call | flops 1024 | bytes 1024 | tf_op jit(solution)/shard_map/push/pallas_call | solution.py:299
  79.0 0.1 collective-permute-start.6
  79.1 1.1 %pull.5 = (f32[512,256]{1,0:T(8,128)S(1)}, bf16[2,512,256]{2,1,0:T(8,128)(2,1)S(1)}, bf16[2,256,512]{2,1,0:T(8,128)(2,1)S(1)}) custom-call(f32[512,256]{1,0:T(8,128)S(1)} %get-tuple-element.64.users, bf16[2,512,1024]{2,1,0:T(8,128)(2,1)S(1)} %get-tuple-element.68.err_o, bf16[2,256,1024]{2,1,0:T(8,128)(2,1)S(1)} %get-tuple-element.69.right_o, ...), custom_call_target="tpu_custom_call" | custom-call | flops 1024 | bytes 1024 | tf_op jit(solution)/shard_map/pull/pallas_call | solution.py:318
  80.2 0.8 collective-permute-done.6.got_o
  81.0 6.4 %collective-permute-done.7.got_e = s32[144,1024]{1,0:T(8,128)S(1)} collective-permute-done((s32[144,1024]{1,0:T(8,128)S(1)}, s32[144,1024]{1,0:T(8,128)S(1)}, u32[]{:S(2)}, u32[]{:S(2)}) %collective-permute-start.7) | collective-permute-done | bytes 589856 | tf_op jit(solution)/shard_map/ppermute | solution.py:314
  87.4 4.0 %last.1 = (f32[1024,256]{1,0:T(8,128)}, f32[512,256]{1,0:T(8,128)}) custom-call(bf16[2,512,256]{2,1,0:T(8,128)(2,1)S(1)} %get-tuple-element.74.left, bf16[2,256,512]{2,1,0:T(8,128)(2,1)S(1)} %get-tuple-element.75.left_t, s16[512,1024]{1,0:T(8,128)(2,1)S(1)} %ratings.1.values, f32[512,256]{1,0:T(8,128)S(1)} %get-tuple-element.76.users, ...), custom_call_target="tpu_custom_call" | custom-call | flops 1024 | bytes 1024 | tf_op jit(solution)/shard_map/last/pallas_call | solution.py:330
  (7 shorter events, 0.0 us)
Async XLA Ops:
  1.7 12.5 %collective-permute-start.1 = (bf16[512,256]{1,0:T(8,128)(2,1)S(1)}, bf16[512,256]{1,0:T(8,128)(2,1)S(1)}, u32[]{:S(2)}, u32[]{:S(2)}) collective-permute-start(bf16[512,256]{1,0:T(8,128)(2,1)S(1)} %get-tuple-element.80), channel_id=1, source_target_pairs={{0,1},{1,0},{2,3},{3,2},{4,5},{5,4},{6,7},{7,6},{8,9},{9,8},{10,11... | collective-permute-start | bytes 786440 | tf_op jit(solution)/shard_map/ppermute | solution.py:245
  4.0 11.5 %collective-permute-start = (bf16[512,256]{1,0:T(8,128)(2,1)S(1)}, bf16[512,256]{1,0:T(8,128)(2,1)S(1)}, u32[]{:S(2)}, u32[]{:S(2)}) collective-permute-start(bf16[512,256]{1,0:T(8,128)(2,1)S(1)} %get-tuple-element.81), channel_id=1, source_target_pairs={{0,1},{1,0},{2,3},{3,2},{4,5},{5,4},{6,7},{7,6},{8,9},{9,8},{10,11... | collective-permute-start | bytes 786440 | tf_op jit(solution)/shard_map/ppermute | solution.py:245
  4.1 8.4 %copy-start = (f32[512,256]{1,0:T(8,128)S(1)}, f32[512,256]{1,0:T(8,128)}, u32[]{:S(2)}) copy-start(f32[512,256]{1,0:T(8,128)} %users.3) | copy-start | bytes 1572868
  4.1 8.4 %copy-start.1 = (bf16[512,256]{1,0:T(8,128)(2,1)S(1)}, bf16[512,256]{1,0:T(8,128)(2,1)}, u32[]{:S(2)}) copy-start(bf16[512,256]{1,0:T(8,128)(2,1)} %weights.3) | copy-start | bytes 786436
  4.1 8.4 %copy-start.2 = (bf16[2048,256]{1,0:T(8,128)(2,1)S(1)}, bf16[2048,256]{1,0:T(8,128)(2,1)}, u32[]{:S(2)}) copy-start(bf16[2048,256]{1,0:T(8,128)(2,1)} %content.1) | copy-start | bytes 3145732
  4.1 8.4 %copy-start.3 = (s32[1,1024]{1,0:T(1,128)S(1)}, s32[1,1024]{1,0:T(1,128)}, u32[]{:S(2)}) copy-start(s32[1,1024]{1,0:T(1,128)} %order) | copy-start | bytes 12292
  52.8 15.0 %collective-permute-start.3 = (s32[144,1024]{1,0:T(8,128)S(1)}, s32[144,1024]{1,0:T(8,128)S(1)}, u32[]{:S(2)}, u32[]{:S(2)}) collective-permute-start(s32[144,1024]{1,0:T(8,128)S(1)} %get-tuple-element.50), channel_id=1, source_target_pairs={{0,2},{2,4},{4,6},{6,8},{8,10},{10,12},{12,14},{14,16},{16,18},{18... | collective-permute-start | bytes 1769480 | tf_op jit(solution)/shard_map/ppermute | solution.py:314
  59.3 2.0 %collective-permute-start.2 = (s32[136,1024]{1,0:T(8,128)S(1)}, s32[136,1024]{1,0:T(8,128)S(1)}, u32[]{:S(2)}, u32[]{:S(2)}) collective-permute-start(s32[136,1024]{1,0:T(8,128)S(1)} %get-tuple-element.57), channel_id=1, source_target_pairs={{0,2},{2,0},{4,6},{6,4},{8,10},{10,8},{12,14},{14,12},{16,18},{18,... | collective-permute-start | bytes 1671176 | tf_op jit(solution)/shard_map/ppermute | solution.py:317
  61.4 15.0 %collective-permute-start.5 = (s32[144,1024]{1,0:T(8,128)S(1)}, s32[144,1024]{1,0:T(8,128)S(1)}, u32[]{:S(2)}, u32[]{:S(2)}) collective-permute-start(s32[144,1024]{1,0:T(8,128)S(1)} %get-tuple-element.60), channel_id=1, source_target_pairs={{0,2},{2,4},{4,6},{6,8},{8,10},{10,12},{12,14},{14,16},{16,18},{18... | collective-permute-start | bytes 1769480 | tf_op jit(solution)/shard_map/ppermute | solution.py:314
  70.4 2.0 %collective-permute-start.4 = (s32[136,1024]{1,0:T(8,128)S(1)}, s32[136,1024]{1,0:T(8,128)S(1)}, u32[]{:S(2)}, u32[]{:S(2)}) collective-permute-start(s32[136,1024]{1,0:T(8,128)S(1)} %get-tuple-element.67), channel_id=1, source_target_pairs={{0,2},{2,0},{4,6},{6,4},{8,10},{10,8},{12,14},{14,12},{16,18},{18,... | collective-permute-start | bytes 1671176 | tf_op jit(solution)/shard_map/ppermute | solution.py:317
  72.4 15.0 %collective-permute-start.7 = (s32[144,1024]{1,0:T(8,128)S(1)}, s32[144,1024]{1,0:T(8,128)S(1)}, u32[]{:S(2)}, u32[]{:S(2)}) collective-permute-start(s32[144,1024]{1,0:T(8,128)S(1)} %get-tuple-element.70), channel_id=1, source_target_pairs={{0,2},{2,4},{4,6},{6,8},{8,10},{10,12},{12,14},{14,16},{16,18},{18... | collective-permute-start | bytes 1769480 | tf_op jit(solution)/shard_map/ppermute | solution.py:314
  79.0 2.0 %collective-permute-start.6 = (s32[136,1024]{1,0:T(8,128)S(1)}, s32[136,1024]{1,0:T(8,128)S(1)}, u32[]{:S(2)}, u32[]{:S(2)}) collective-permute-start(s32[136,1024]{1,0:T(8,128)S(1)} %get-tuple-element.77), channel_id=1, source_target_pairs={{0,2},{2,0},{4,6},{6,4},{8,10},{10,8},{12,14},{14,12},{16,18},{18,... | collective-permute-start | bytes 1671176 | tf_op jit(solution)/shard_map/ppermute | solution.py:317

commit v5 on v4

--- a/solution.py
+++ b/solution.py
@@ -146,12 +146,12 @@
     return jnp.concatenate([a, b], axis=0) * scale
 
 
-def errors_and_items(q, here, left, left_t, values, t, err, right):
+def errors_and_items(q, here, left, left_t, values, t, err, right, cols=None):
     q_hi, q_lo = split(q)
     right[0, :, here] = q_hi
     right[1, :, here] = q_lo
     guess = mm(left[0], q_hi) + mm(left[0], q_lo) + mm(left[1], q_hi)
-    v = (lax.shift_right_logical(values[:, here].astype(I32), 3 * t) & 7).astype(F32)
+    v = (lax.shift_right_logical(values[:, here if cols is None else cols].astype(I32), 3 * t) & 7).astype(F32)
     e_hi, e_lo = split(jnp.where(v > 0, v - guess, 0.0))
     err[0, :, here] = e_hi
     err[1, :, here] = e_lo
@@ -172,13 +172,18 @@
     return lax.rem(lax.axis_index("blk"), 2) == turn
 
 
+def n_source(t):
+    return 2 if t == 0 else 1
+
+
 def push_kernel(turn, t, left, left_t, values, *refs):
-    source, (err, right, out) = refs[:-3], refs[-3:]
-    wide = out.shape[1]
+    count = n_source(t)
+    source, err, right, outs = refs[:count], refs[count], refs[count + 1], refs[count + 2:]
+    wide = outs[0].shape[1]
 
     @pl.when(my_turn(turn))
     def _():
-        for at in range(0, wide, CHUNK):
+        for at in range(0, wide * len(outs), CHUNK):
             here = slice(at, at + CHUNK)
             if t == 0:
                 q = first_items(*source, here)
@@ -187,15 +192,15 @@
             new = errors_and_items(q, here, left, left_t, values, t, err, right)
             words, level = encode(new)
             rows = words.shape[0]
-            out[:rows, here] = words
-            out[rows:, here] = jnp.broadcast_to(level, (out.shape[0] - rows, CHUNK))
-
-
-def user_step(users, err, right, rows=slice(None)):
+            out, there = outs[at // wide], slice(at % wide, at % wide + CHUNK)
+            out[:rows, there] = words
+            out[rows:, there] = jnp.broadcast_to(level, (out.shape[0] - rows, CHUNK))
+
+
+def user_grad(err, right, rows):
     dims = ((1,), (1,))
     hi, lo = err[0, rows, :], err[1, rows, :]
-    grad = mm(hi, right[0], dims) + mm(hi, right[1], dims) + mm(lo, right[0], dims)
-    return KEEP * users[rows, :] + learn_rate * grad
+    return mm(hi, right[0], dims) + mm(hi, right[1], dims) + mm(lo, right[0], dims)
 
 
 def pull_kernel(users, err_o, right_o, err_e, right_e, *outs):
@@ -203,28 +208,42 @@
 
         @pl.when(my_turn(turn))
         def _():
-            put_users(user_step(users, err, right), *outs)
-
-
-def last_kernel(left, left_t, values, users, got_o, got_e, items_out, users_out, err, right, held, users_held, sems):
+            grad = user_grad(err, right, slice(None))
+            put_users(KEEP * users[...] + learn_rate * grad, *outs)
+
+
+def last_items(half, left, left_t, values, got_o, got_e, items_out, err, right, held, sems):
+    wide = right.shape[2]
     live = right.shape[1] // 2 + 8
-    tall = users_held.shape[0] // 2
     is_odd = my_turn(1)
     copies = []
-
-    def put(source, target, rows):
-        copies.append(pltpu.make_async_copy(source.at[rows, :], target.at[rows, :], sems.at[len(copies)]))
+    for at in range(0, wide, CHUNK):
+        here = slice(at, at + CHUNK)
+        cols = slice(half * wide + at, half * wide + at + CHUNK)
+        q = decode(jnp.where(is_odd, got_o[:live, here], got_e[:live, here]), right.shape[1])
+        held[here, :] = errors_and_items(q, here, left, left_t, values, ROUNDS - 1, err, right, cols).T
+        copies.append(pltpu.make_async_copy(held.at[here, :], items_out.at[cols, :], sems.at[len(copies)]))
         copies[-1].start()
-
-    for at in range(0, right.shape[2], CHUNK):
-        here = slice(at, at + CHUNK)
-        q = decode(jnp.where(is_odd, got_o[:live, here], got_e[:live, here]), right.shape[1])
-        held[here, :] = errors_and_items(q, here, left, left_t, values, ROUNDS - 1, err, right).T
-        put(held, items_out, here)
+    return copies
+
+
+def last_first_kernel(left, left_t, values, users, got_o, got_e, items_out, part, err, right, held, sems):
+    copies = last_items(0, left, left_t, values, got_o, got_e, items_out, err, right, held, sems)
+    part[...] = KEEP * users[...] + learn_rate * user_grad(err, right, slice(None))
+    for copy in copies:
+        copy.wait()
+
+
+def last_second_kernel(
+    left, left_t, values, part, got_o, got_e, items_in, items_out, users_out, err, right, held, users_held, sems,
+):
+    copies = last_items(1, left, left_t, values, got_o, got_e, items_out, err, right, held, sems)
+    tall = users_held.shape[0] // 2
     for at in (0, tall):
         rows = slice(at, at + tall)
-        users_held[rows, :] = user_step(users, err, right, rows)
-        put(users_held, users_out, rows)
+        users_held[rows, :] = part[rows, :] + learn_rate * user_grad(err, right, rows)
+        copies.append(pltpu.make_async_copy(users_held.at[rows, :], users_out.at[rows, :], sems.at[len(copies)]))
+        copies[-1].start()
     for copy in copies:
         copy.wait()
 
@@ -295,26 +314,27 @@
     pair = [(i, i ^ 1) for i in range(n_blk)]
     light = cost(1 << 10, 1 << 10)
 
-    def push(turn, t, left, source, tail):
-        *state, sent = pl.pallas_call(
+    def push(turn, t, left, source, tail, pieces=1):
+        err, right, *sent = pl.pallas_call(
             functools.partial(push_kernel, turn, t),
-            out_shape=state_shapes + [struct((rank // 2 + tail, n_items), I32)],
+            out_shape=state_shapes + [struct((rank // 2 + tail, n_items // pieces), I32)] * pieces,
             in_specs=[VM] * (3 + len(source)),
-            out_specs=[VM] * 3,
+            out_specs=[VM] * (2 + pieces),
             compiler_params=params(),
             cost_estimate=light,
             name="push",
         )(left, left_t, values, *source)
-        return state, sent
+        return (err, right), sent
 
     users = user_factors
     for_odd = for_even = [dealt, meta]
     for t in range(ROUNDS - 1):
-        odd_state, sent = push(1, t, left, for_odd, EVEN_TAIL)
-        next_even = [lax.ppermute(sent, "blk", ring)]
-        later, _ = lax.optimization_barrier((left, sent))
-        even_state, sent = push(0, t, later, for_even, ODD_TAIL)
-        next_odd = [lax.ppermute(sent, "blk", pair)]
+        pieces = 1 if t < ROUNDS - 2 else 2
+        odd_state, sent = push(1, t, left, for_odd, EVEN_TAIL, pieces)
+        next_even = [lax.ppermute(x, "blk", ring) for x in sent]
+        later, _ = lax.optimization_barrier((left, sent[0]))
+        even_state, sent = push(0, t, later, for_even, ODD_TAIL, pieces)
+        next_odd = [lax.ppermute(x, "blk", pair) for x in sent]
         users, left, left_t = pl.pallas_call(
             pull_kernel,
             out_shape=[struct((n_users, rank), F32)] + split_shapes,
@@ -327,22 +347,31 @@
         for_even, for_odd = next_even, next_odd
 
     anywhere = pl.BlockSpec(memory_space=pl.ANY)
+    scratch = [pltpu.VMEM((2, n_users, wide), BF16), pltpu.VMEM((2, rank, wide), BF16), pltpu.VMEM((wide, rank), F32)]
+    items, part = pl.pallas_call(
+        last_first_kernel,
+        out_shape=[pltpu.HBM((n_items, rank), F32), struct((n_users, rank), F32)],
+        in_specs=[VM] * 6,
+        out_specs=[anywhere, VM],
+        scratch_shapes=scratch + [pltpu.SemaphoreType.DMA((wide // CHUNK,))],
+        compiler_params=params(),
+        cost_estimate=light,
+        name="last_first",
+    )(left, left_t, values, users, for_odd[0], for_even[0])
     items, users = pl.pallas_call(
-        last_kernel,
+        last_second_kernel,
         out_shape=[struct((n_items, rank), F32), struct((n_users, rank), F32)],
-        in_specs=[VM] * 6,
+        in_specs=[VM] * 6 + [anywhere],
         out_specs=[anywhere] * 2,
-        scratch_shapes=[
-            pltpu.VMEM((2, n_users, n_items), BF16),
-            pltpu.VMEM((2, rank, n_items), BF16),
-            pltpu.VMEM((n_items, rank), F32),
+        scratch_shapes=scratch + [
             pltpu.VMEM((n_users, rank), F32),
-            pltpu.SemaphoreType.DMA((n_items // CHUNK + 2,)),
+            pltpu.SemaphoreType.DMA((wide // CHUNK + 2,)),
         ],
-        compiler_params=params(16),
+        input_output_aliases={6: 0},
+        compiler_params=params(),
         cost_estimate=light,
-        name="last",
-    )(left, left_t, values, users, *for_odd, *for_even)
+        name="last_second",
+    )(left, left_t, values, part, for_odd[1], for_even[1], items)
     return users, items
 
 

time: 91.9 us -> 90.6 us (0.986)
  waiting for transfers between devices: 14.9 us -> 11.8 us
  Pallas kernels: 26.9 us -> 28.1 us
    ppermute x6 -> x8, waiting for transfers between devices: 13.7 us -> 10.6 us  [the longest x4 8.98 us: body(): next_even = [lax.ppermute(x, 'blk', ring) for x in sent]]
    pallas_call x1 -> x2, Pallas kernels: 4.05 us -> 5.24 us  [the longest x1 2.71 us: body(): pl.pallas_call(last_second_kernel, out_shape=[struct((n_items, rank), F32...]
    ppermute x6 -> x8, starting transfers between devices: 9.25 us -> 9.83 us  [the longest x4 9.06 us: body(): next_even = [lax.ppermute(x, 'blk', ring) for x in sent]]
  transfers between devices with their start and end apart: 8 -> 10, of which waited for: 7 -> 7; matrix products, arithmetic and copies ran while one was open for 0% -> 0% of each run, Pallas kernels for 24% -> 27%
where the time goes in v5:
time: 90.6 us; the launch traced here: 90.3 us
  blocking collectives  36.1 us (40%)
  Pallas kernels  28.1 us (31%)
  starting transfers between devices  12.2 us (13%)
  waiting for transfers between devices  11.8 us (13%)
  local copies, waits for them, and re-layouts  1.08 us (1%)
  between operations  0.99 us (1%)
    all_to_all x1, blocking collectives, body(): lax.all_to_all(coded.reshape(n_blk, share, rank // 2), 'blk', split_axis=...  36.1 us
    ppermute x4, starting transfers between devices, body(): next_even = [lax.ppermute(x, 'blk', ring) for x in sent]  9.06 us
    ppermute x4, waiting for transfers between devices, body(): next_even = [lax.ppermute(x, 'blk', ring) for x in sent]  8.98 us
    pallas_call x1, Pallas kernels, body(): pl.pallas_call(ratings_kernel, out_shape=struct((n_users, n_items), jnp.i...  8.38 us
    pallas_call x6, Pallas kernels, push(): pl.pallas_call(functools.partial(push_kernel, turn, t), out_shape=state_s...  8.22 us
    pallas_call x3, Pallas kernels, body(): pl.pallas_call(pull_kernel, out_shape=[struct((n_users, rank), F32)] + sp...  3.41 us
    pallas_call x1, Pallas kernels, body(): pl.pallas_call(last_second_kernel, out_shape=[struct((n_items, rank), F32...  2.71 us
    pallas_call x1, Pallas kernels, body(): pl.pallas_call(last_first_kernel, out_shape=[pltpu.HBM((n_items, rank), F...  2.54 us
  transfers between devices with their start and end apart: 10, of which 7 were waited for; matrix products, arithmetic and copies ran while one was open for 0% of the time, Pallas kernels for 27%

profile of v5, /device:TPU:8, one launch (start us, length us, event | category | flops | bytes accessed | tf_op | source)
XLA Modules:
  0.0 90.3 jit_solution(13028063593132056071)
XLA Ops:
  0.6 1.1 %constant_dynamic-slice_fusion.1 = (bf16[512,256]{1,0:T(8,128)(2,1)S(1)}, bf16[512,256]{1,0:T(8,128)(2,1)S(1)}) fusion(bf16[2048,256]{1,0:T(8,128)(2,1)} %content.1, s32[]{:T(128)S(6)} %add.4, s32[]{:T(128)S(6)} %select_n.3), kind=kLoop, calls=%fused_computation.1 | loop fusion | bytes 1048584 | tf_op jit(solution)/shard_map/slice | solution.py:264
  1.7 2.3 %collective-permute-start.1 = (bf16[512,256]{1,0:T(8,128)(2,1)S(1)}, bf16[512,256]{1,0:T(8,128)(2,1)S(1)}, u32[]{:S(2)}, u32[]{:S(2)}) collective-permute-start(bf16[512,256]{1,0:T(8,128)(2,1)S(1)} %get-tuple-element.88), channel_id=1, source_target_pairs={{0,1},{1,0},{2,3},{3,2},{4,5},{5,4},{6,7},{7,6},{8,9},{9,8},{10,11... | collective-permute-start | bytes 786440 | tf_op jit(solution)/shard_map/ppermute | solution.py:264
  4.0 0.1 collective-permute-start
  4.1 8.4 %ratings.1.values = s16[512,1024]{1,0:T(8,128)(2,1)S(1)} custom-call(s32[16384,128]{1,0:T(8,128)} %bitcast.10), custom_call_target="tpu_custom_call" | custom-call | flops 1048576 | bytes 12582912 | tf_op jit(solution)/shard_map/ratings/pallas_call | solution.py:269
  12.5 1.7 %before.1 = (bf16[1024,1024]{1,0:T(8,128)(2,1)S(1)}, f32[1024,256]{1,0:T(8,128)S(1)}, f32[8,128]{1,0:T(8,128)S(1)}, bf16[2,512,256]{2,1,0:T(8,128)(2,1)S(1)}, bf16[2,256,512]{2,1,0:T(8,128)(2,1)S(1)}) custom-call(s32[1,1024]{1,0:T(1,128)S(1)} %copy-done.3, bf16[2048,256]{1,0:T(8,128)(2,1)S(1)} %copy-done.2, bf16[512,256]{1,0:T(8,128)(2,1)S(1)} %copy-done.1, ...), custom_call_target="tpu_custom_call" | custom-call | flops 536870912 | bytes 6291456 | tf_op jit(solution)/shard_map/before/pallas_call | solution.py:281
  14.2 0.0 collective-permute-done.1.second
  14.2 1.2 %collective-permute-done.first = bf16[512,256]{1,0:T(8,128)(2,1)S(1)} collective-permute-done((bf16[512,256]{1,0:T(8,128)(2,1)S(1)}, bf16[512,256]{1,0:T(8,128)(2,1)S(1)}, u32[]{:S(2)}, u32[]{:S(2)}) %collective-permute-start) | collective-permute-done | bytes 262176 | tf_op jit(solution)/shard_map/ppermute | solution.py:264
  15.5 1.2 %project.1 = s32[1024,128]{1,0:T(8,128)S(1)} custom-call(bf16[1024,1024]{1,0:T(8,128)(2,1)S(1)} %get-tuple-element.49.deal, bf16[512,256]{1,0:T(8,128)(2,1)S(1)} %collective-permute-done.first, bf16[512,256]{1,0:T(8,128)(2,1)S(1)} %collective-permute-done.1.second, bf16[512,256]{1,0:T(8,128)(2,1)S(1)} %copy-done.1, ...), custom_call_target="tpu_custom_call" | custom-call | flops 536870912 | bytes 4194304 | tf_op jit(solution)/shard_map/project/pallas_call | solution.py:299
  16.6 36.1 %all_to_all.5 = s32[128,8,128]{2,1,0:T(8,128)S(1)} all-to-all(s32[128,8,128]{2,1,0:T(8,128)S(1)} %bitcast.9), channel_id=1, replica_groups=mesh['blk'=128,'cat'=2] {'blk'}, dimensions={0} | all-to-all | bytes 1048576 | tf_op jit(solution)/shard_map/all_to_all | solution.py:308
  52.8 3.4 %collective-permute-start.3 = (s32[144,1024]{1,0:T(8,128)S(1)}, s32[144,1024]{1,0:T(8,128)S(1)}, u32[]{:S(2)}, u32[]{:S(2)}) collective-permute-start(s32[144,1024]{1,0:T(8,128)S(1)} %get-tuple-element.54), channel_id=1, source_target_pairs={{0,2},{2,4},{4,6},{6,8},{8,10},{10,12},{12,14},{14,16},{16,18},{18... | collective-permute-start | bytes 1769480 | tf_op jit(solution)/shard_map/ppermute | solution.py:334
  56.2 3.1 %push.7 = (bf16[2,512,1024]{2,1,0:T(8,128)(2,1)S(1)}, bf16[2,256,1024]{2,1,0:T(8,128)(2,1)S(1)}, s32[136,1024]{1,0:T(8,128)S(1)}) custom-call(bf16[2,512,256]{2,1,0:T(8,128)(2,1)S(1)} %get-tuple-element.55.left, bf16[2,256,512]{2,1,0:T(8,128)(2,1)S(1)} %get-tuple-element.47.left_t, s16[512,1024]{1,0:T(8,128)(2,1)S(1)} %ratings.1.values, ...), custom_call_target="tpu_custom_call" | custom-call | flops 1024 | bytes 1024 | tf_op jit(solution)/shard_map/push/pallas_call | solution.py:318
  59.3 0.1 collective-permute-start.2
  59.4 1.2 %pull.3 = (f32[512,256]{1,0:T(8,128)S(1)}, bf16[2,512,256]{2,1,0:T(8,128)(2,1)S(1)}, bf16[2,256,512]{2,1,0:T(8,128)(2,1)S(1)}) custom-call(f32[512,256]{1,0:T(8,128)S(1)} %copy-done, bf16[2,512,1024]{2,1,0:T(8,128)(2,1)S(1)} %get-tuple-element.52.err_o, bf16[2,256,1024]{2,1,0:T(8,128)(2,1)S(1)} %get-tuple-element.53.right_o, ...), custom_call_target="tpu_custom_call" | custom-call | flops 1024 | bytes 1024 | tf_op jit(solution)/shard_map/pull/pallas_call | solution.py:338
  60.6 0.8 collective-permute-done.2.refs_0_
  61.4 2.8 %collective-permute-start.5 = (s32[144,1024]{1,0:T(8,128)S(1)}, s32[144,1024]{1,0:T(8,128)S(1)}, u32[]{:S(2)}, u32[]{:S(2)}) collective-permute-start(s32[144,1024]{1,0:T(8,128)S(1)} %get-tuple-element.64), channel_id=1, source_target_pairs={{0,2},{2,4},{4,6},{6,8},{8,10},{10,12},{12,14},{14,16},{16,18},{18... | collective-permute-start | bytes 1769480 | tf_op jit(solution)/shard_map/ppermute | solution.py:334
  64.1 3.7 %collective-permute-done.3.refs_0_ = s32[144,1024]{1,0:T(8,128)S(1)} collective-permute-done((s32[144,1024]{1,0:T(8,128)S(1)}, s32[144,1024]{1,0:T(8,128)S(1)}, u32[]{:S(2)}, u32[]{:S(2)}) %collective-permute-start.3) | collective-permute-done | bytes 589856 | tf_op jit(solution)/shard_map/ppermute | solution.py:334
  67.8 2.5 %push.9 = (bf16[2,512,1024]{2,1,0:T(8,128)(2,1)S(1)}, bf16[2,256,1024]{2,1,0:T(8,128)(2,1)S(1)}, s32[136,1024]{1,0:T(8,128)S(1)}) custom-call(bf16[2,512,256]{2,1,0:T(8,128)(2,1)S(1)} %get-tuple-element.65.left, bf16[2,256,512]{2,1,0:T(8,128)(2,1)S(1)} %get-tuple-element.60.left_t, s16[512,1024]{1,0:T(8,128)(2,1)S(1)} %ratings.1.values, ...), custom_call_target="tpu_custom_call" | custom-call | flops 1024 | bytes 1024 | tf_op jit(solution)/shard_map/push/pallas_call | solution.py:318
  70.4 0.1 collective-permute-start.4
  70.5 1.1 %pull.4 = (f32[512,256]{1,0:T(8,128)S(1)}, bf16[2,512,256]{2,1,0:T(8,128)(2,1)S(1)}, bf16[2,256,512]{2,1,0:T(8,128)(2,1)S(1)}) custom-call(f32[512,256]{1,0:T(8,128)S(1)} %get-tuple-element.58.users, bf16[2,512,1024]{2,1,0:T(8,128)(2,1)S(1)} %get-tuple-element.62.err_o, bf16[2,256,1024]{2,1,0:T(8,128)(2,1)S(1)} %get-tuple-element.63.right_o, ...), custom_call_target="tpu_custom_call" | custom-call | flops 1024 | bytes 1024 | tf_op jit(solution)/shard_map/pull/pallas_call | solution.py:338
  71.6 0.8 collective-permute-done.4.refs_0_
  72.4 2.8 %collective-permute-start.7 = (s32[144,512]{1,0:T(8,128)S(1)}, s32[144,512]{1,0:T(8,128)S(1)}, u32[]{:S(2)}, u32[]{:S(2)}) collective-permute-start(s32[144,512]{1,0:T(8,128)S(1)} %get-tuple-element.74), channel_id=1, source_target_pairs={{0,2},{2,4},{4,6},{6,8},{8,10},{10,12},{12,14},{14,16},{16,18},{18... | collective-permute-start | bytes 884744 | tf_op jit(solution)/shard_map/ppermute | solution.py:334
  75.2 0.1 collective-permute-start.9
  75.3 1.1 %collective-permute-done.5.refs_0_ = s32[144,1024]{1,0:T(8,128)S(1)} collective-permute-done((s32[144,1024]{1,0:T(8,128)S(1)}, s32[144,1024]{1,0:T(8,128)S(1)}, u32[]{:S(2)}, u32[]{:S(2)}) %collective-permute-start.5) | collective-permute-done | bytes 589856 | tf_op jit(solution)/shard_map/ppermute | solution.py:334
  76.4 2.5 %push.11 = (bf16[2,512,1024]{2,1,0:T(8,128)(2,1)S(1)}, bf16[2,256,1024]{2,1,0:T(8,128)(2,1)S(1)}, s32[136,512]{1,0:T(8,128)S(1)}, s32[136,512]{1,0:T(8,128)S(1)}) custom-call(bf16[2,512,256]{2,1,0:T(8,128)(2,1)S(1)} %get-tuple-element.75.left, bf16[2,256,512]{2,1,0:T(8,128)(2,1)S(1)} %get-tuple-element.70.left_t, s16[512,1024]{1,0:T(8,128)(2,1)S(1)} %ratings.1.values, ...), custom_call_target="tpu_custom_call" | custom-call | flops 1024 | bytes 1024 | tf_op jit(solution)/shard_map/push/pallas_call | solution.py:318
  79.0 0.1 collective-permute-start.6
  79.1 0.5 collective-permute-start.8
  79.6 1.1 %pull.5 = (f32[512,256]{1,0:T(8,128)S(1)}, bf16[2,512,256]{2,1,0:T(8,128)(2,1)S(1)}, bf16[2,256,512]{2,1,0:T(8,128)(2,1)S(1)}) custom-call(f32[512,256]{1,0:T(8,128)S(1)} %get-tuple-element.68.users, bf16[2,512,1024]{2,1,0:T(8,128)(2,1)S(1)} %get-tuple-element.72.err_o, bf16[2,256,1024]{2,1,0:T(8,128)(2,1)S(1)} %get-tuple-element.73.right_o, ...), custom_call_target="tpu_custom_call" | custom-call | flops 1024 | bytes 1024 | tf_op jit(solution)/shard_map/pull/pallas_call | solution.py:338
  80.7 0.0 collective-permute-done.6.got_o
  80.7 3.6 %collective-permute-done.7.got_e = s32[144,512]{1,0:T(8,128)S(1)} collective-permute-done((s32[144,512]{1,0:T(8,128)S(1)}, s32[144,512]{1,0:T(8,128)S(1)}, u32[]{:S(2)}, u32[]{:S(2)}) %collective-permute-start.7) | collective-permute-done | bytes 294944 | tf_op jit(solution)/shard_map/ppermute | solution.py:334
  84.3 2.5 %last_first.1 = (f32[1024,256]{1,0:T(8,128)}, f32[512,256]{1,0:T(8,128)S(1)}) custom-call(bf16[2,512,256]{2,1,0:T(8,128)(2,1)S(1)} %get-tuple-element.78.left, bf16[2,256,512]{2,1,0:T(8,128)(2,1)S(1)} %get-tuple-element.79.left_t, s16[512,1024]{1,0:T(8,128)(2,1)S(1)} %ratings.1.values, f32[512,256]{1,0:T(8,128)S(1)} %get-tuple-element.80.users, ...), custom_call_target="tpu_custom_call" | custom-call | flops 1024 | bytes 1024 | tf_op jit(solution)/shard_map/last_first/pallas_call | solution.py:351
  86.8 0.6 collective-permute-done.9.got_e
  87.4 2.7 %last_second.1 = (f32[1024,256]{1,0:T(8,128)}, f32[512,256]{1,0:T(8,128)}) custom-call(bf16[2,512,256]{2,1,0:T(8,128)(2,1)S(1)} %get-tuple-element.78.left, bf16[2,256,512]{2,1,0:T(8,128)(2,1)S(1)} %get-tuple-element.79.left_t, s16[512,1024]{1,0:T(8,128)(2,1)S(1)} %ratings.1.values, ...), custom_call_target="tpu_custom_call", output_to_operand_aliasing={{0}: (6, {})} | custom-call | flops 1024 | bytes 1024 | tf_op jit(solution)/shard_map/last_second/pallas_call | solution.py:361
  (12 shorter events, 0.0 us)
Async XLA Ops:
  1.7 12.5 %collective-permute-start.1 = (bf16[512,256]{1,0:T(8,128)(2,1)S(1)}, bf16[512,256]{1,0:T(8,128)(2,1)S(1)}, u32[]{:S(2)}, u32[]{:S(2)}) collective-permute-start(bf16[512,256]{1,0:T(8,128)(2,1)S(1)} %get-tuple-element.88), channel_id=1, source_target_pairs={{0,1},{1,0},{2,3},{3,2},{4,5},{5,4},{6,7},{7,6},{8,9},{9,8},{10,11... | collective-permute-start | bytes 786440 | tf_op jit(solution)/shard_map/ppermute | solution.py:264
  4.0 11.5 %collective-permute-start = (bf16[512,256]{1,0:T(8,128)(2,1)S(1)}, bf16[512,256]{1,0:T(8,128)(2,1)S(1)}, u32[]{:S(2)}, u32[]{:S(2)}) collective-permute-start(bf16[512,256]{1,0:T(8,128)(2,1)S(1)} %get-tuple-element.89), channel_id=1, source_target_pairs={{0,1},{1,0},{2,3},{3,2},{4,5},{5,4},{6,7},{7,6},{8,9},{9,8},{10,11... | collective-permute-start | bytes 786440 | tf_op jit(solution)/shard_map/ppermute | solution.py:264
  4.1 8.4 %copy-start = (f32[512,256]{1,0:T(8,128)S(1)}, f32[512,256]{1,0:T(8,128)}, u32[]{:S(2)}) copy-start(f32[512,256]{1,0:T(8,128)} %users.3) | copy-start | bytes 1572868
  4.1 8.4 %copy-start.1 = (bf16[512,256]{1,0:T(8,128)(2,1)S(1)}, bf16[512,256]{1,0:T(8,128)(2,1)}, u32[]{:S(2)}) copy-start(bf16[512,256]{1,0:T(8,128)(2,1)} %weights.3) | copy-start | bytes 786436
  4.1 8.4 %copy-start.2 = (bf16[2048,256]{1,0:T(8,128)(2,1)S(1)}, bf16[2048,256]{1,0:T(8,128)(2,1)}, u32[]{:S(2)}) copy-start(bf16[2048,256]{1,0:T(8,128)(2,1)} %content.1) | copy-start | bytes 3145732
  4.1 8.4 %copy-start.3 = (s32[1,1024]{1,0:T(1,128)S(1)}, s32[1,1024]{1,0:T(1,128)}, u32[]{:S(2)}) copy-start(s32[1,1024]{1,0:T(1,128)} %order) | copy-start | bytes 12292
  52.8 15.0 %collective-permute-start.3 = (s32[144,1024]{1,0:T(8,128)S(1)}, s32[144,1024]{1,0:T(8,128)S(1)}, u32[]{:S(2)}, u32[]{:S(2)}) collective-permute-start(s32[144,1024]{1,0:T(8,128)S(1)} %get-tuple-element.54), channel_id=1, source_target_pairs={{0,2},{2,4},{4,6},{6,8},{8,10},{10,12},{12,14},{14,16},{16,18},{18... | collective-permute-start | bytes 1769480 | tf_op jit(solution)/shard_map/ppermute | solution.py:334
  59.3 2.0 %collective-permute-start.2 = (s32[136,1024]{1,0:T(8,128)S(1)}, s32[136,1024]{1,0:T(8,128)S(1)}, u32[]{:S(2)}, u32[]{:S(2)}) collective-permute-start(s32[136,1024]{1,0:T(8,128)S(1)} %get-tuple-element.61), channel_id=1, source_target_pairs={{0,2},{2,0},{4,6},{6,4},{8,10},{10,8},{12,14},{14,12},{16,18},{18,... | collective-permute-start | bytes 1671176 | tf_op jit(solution)/shard_map/ppermute | solution.py:337
  61.4 15.0 %collective-permute-start.5 = (s32[144,1024]{1,0:T(8,128)S(1)}, s32[144,1024]{1,0:T(8,128)S(1)}, u32[]{:S(2)}, u32[]{:S(2)}) collective-permute-start(s32[144,1024]{1,0:T(8,128)S(1)} %get-tuple-element.64), channel_id=1, source_target_pairs={{0,2},{2,4},{4,6},{6,8},{8,10},{10,12},{12,14},{14,16},{16,18},{18... | collective-permute-start | bytes 1769480 | tf_op jit(solution)/shard_map/ppermute | solution.py:334
  70.4 2.0 %collective-permute-start.4 = (s32[136,1024]{1,0:T(8,128)S(1)}, s32[136,1024]{1,0:T(8,128)S(1)}, u32[]{:S(2)}, u32[]{:S(2)}) collective-permute-start(s32[136,1024]{1,0:T(8,128)S(1)} %get-tuple-element.71), channel_id=1, source_target_pairs={{0,2},{2,0},{4,6},{6,4},{8,10},{10,8},{12,14},{14,12},{16,18},{18,... | collective-permute-start | bytes 1671176 | tf_op jit(solution)/shard_map/ppermute | solution.py:337
  72.4 11.9 %collective-permute-start.7 = (s32[144,512]{1,0:T(8,128)S(1)}, s32[144,512]{1,0:T(8,128)S(1)}, u32[]{:S(2)}, u32[]{:S(2)}) collective-permute-start(s32[144,512]{1,0:T(8,128)S(1)} %get-tuple-element.74), channel_id=1, source_target_pairs={{0,2},{2,4},{4,6},{6,8},{8,10},{10,12},{12,14},{14,16},{16,18},{18... | collective-permute-start | bytes 884744 | tf_op jit(solution)/shard_map/ppermute | solution.py:334
  75.2 12.3 %collective-permute-start.9 = (s32[144,512]{1,0:T(8,128)S(1)}, s32[144,512]{1,0:T(8,128)S(1)}, u32[]{:S(2)}, u32[]{:S(2)}) collective-permute-start(s32[144,512]{1,0:T(8,128)S(1)} %get-tuple-element.84), channel_id=1, source_target_pairs={{0,2},{2,4},{4,6},{6,8},{8,10},{10,12},{12,14},{14,16},{16,18},{18... | collective-permute-start | bytes 884744 | tf_op jit(solution)/shard_map/ppermute | solution.py:334
  79.0 1.7 %collective-permute-start.6 = (s32[136,512]{1,0:T(8,128)S(1)}, s32[136,512]{1,0:T(8,128)S(1)}, u32[]{:S(2)}, u32[]{:S(2)}) collective-permute-start(s32[136,512]{1,0:T(8,128)S(1)} %get-tuple-element.81), channel_id=1, source_target_pairs={{0,2},{2,0},{4,6},{6,4},{8,10},{10,8},{12,14},{14,12},{16,18},{18,... | collective-permute-start | bytes 835592 | tf_op jit(solution)/shard_map/ppermute | solution.py:337
  79.1 7.8 %collective-permute-start.8 = (s32[136,512]{1,0:T(8,128)S(1)}, s32[136,512]{1,0:T(8,128)S(1)}, u32[]{:S(2)}, u32[]{:S(2)}) collective-permute-start(s32[136,512]{1,0:T(8,128)S(1)} %get-tuple-element.83), channel_id=1, source_target_pairs={{0,2},{2,0},{4,6},{6,4},{8,10},{10,8},{12,14},{14,12},{16,18},{18,... | collective-permute-start | bytes 835592 | tf_op jit(solution)/shard_map/ppermute | solution.py:337

commit v6 on v5

--- a/solution.py
+++ b/solution.py
@@ -74,14 +74,14 @@
 
 
 def put_users(p, users, left, left_t):
-    hi, lo = split(p)
     if users is not None:
         users[...] = p
-    left[0] = hi
-    left[1] = lo
-    hi_t, lo_t = split(p.T)
-    left_t[0] = hi_t
-    left_t[1] = lo_t
+    for out, x in ((left, p), (left_t, p.T)):
+        hi, lo = split(x)
+        depth = x.shape[1]
+        out[:, :depth] = hi
+        out[:, depth:2 * depth] = hi
+        out[:, 2 * depth:] = lo
 
 
 def before_kernel(order, content, weights, users, deal, partial, meta, left, left_t, rows, held, sems):
@@ -150,12 +150,12 @@
     q_hi, q_lo = split(q)
     right[0, :, here] = q_hi
     right[1, :, here] = q_lo
-    guess = mm(left[0], q_hi) + mm(left[0], q_lo) + mm(left[1], q_hi)
+    guess = mm(left[...], jnp.concatenate([q_hi, q_lo, q_hi], axis=0))
     v = (lax.shift_right_logical(values[:, here if cols is None else cols].astype(I32), 3 * t) & 7).astype(F32)
     e_hi, e_lo = split(jnp.where(v > 0, v - guess, 0.0))
     err[0, :, here] = e_hi
     err[1, :, here] = e_lo
-    grad = mm(left_t[0], e_hi) + mm(left_t[0], e_lo) + mm(left_t[1], e_hi)
+    grad = mm(left_t[...], jnp.concatenate([e_hi, e_lo, e_hi], axis=0))
     return KEEP * q + learn_rate * grad
 
 
@@ -277,7 +277,7 @@
         name="ratings",
     )(ratings)
     send_order, values = lax.optimization_barrier((send_order, values))
-    split_shapes = [struct((2, n_users, rank), BF16), struct((2, rank, n_users), BF16)]
+    split_shapes = [struct((n_users, 3 * rank), BF16), struct((rank, 3 * n_users), BF16)]
     deal, partial, meta, left, left_t = pl.pallas_call(
         before_kernel,
         out_shape=[

time: 90.6 us -> 90.6 us (level)
  no operation moved by 1% of the time
where the time goes in v6:
time: 90.6 us; the launch traced here: 90.3 us
  blocking collectives  36.1 us (40%)
  Pallas kernels  28.1 us (31%)
  starting transfers between devices  12.3 us (14%)
  waiting for transfers between devices  11.8 us (13%)
  local copies, waits for them, and re-layouts  1.08 us (1%)
  between operations  0.98 us (1%)
    all_to_all x1, blocking collectives, body(): lax.all_to_all(coded.reshape(n_blk, share, rank // 2), 'blk', split_axis=...  36.1 us
    ppermute x4, starting transfers between devices, body(): next_even = [lax.ppermute(x, 'blk', ring) for x in sent]  9.11 us
    ppermute x4, waiting for transfers between devices, body(): next_even = [lax.ppermute(x, 'blk', ring) for x in sent]  8.97 us
    pallas_call x1, Pallas kernels, body(): pl.pallas_call(ratings_kernel, out_shape=struct((n_users, n_items), jnp.i...  8.38 us
    pallas_call x6, Pallas kernels, push(): pl.pallas_call(functools.partial(push_kernel, turn, t), out_shape=state_s...  8.28 us
    pallas_call x3, Pallas kernels, body(): pl.pallas_call(pull_kernel, out_shape=[struct((n_users, rank), F32)] + sp...  3.42 us
    pallas_call x1, Pallas kernels, body(): pl.pallas_call(last_second_kernel, out_shape=[struct((n_items, rank), F32...  2.71 us
    pallas_call x1, Pallas kernels, body(): pl.pallas_call(last_first_kernel, out_shape=[pltpu.HBM((n_items, rank), F...  2.46 us
  transfers between devices with their start and end apart: 10, of which 7 were waited for; matrix products, arithmetic and copies ran while one was open for 0% of the time, Pallas kernels for 27%

profile of v6, /device:TPU:8, one launch (start us, length us, event | category | flops | bytes accessed | tf_op | source)
XLA Modules:
  0.0 90.3 jit_solution(14728367183094321189)
XLA Ops:
  0.6 1.1 %constant_dynamic-slice_fusion.1 = (bf16[512,256]{1,0:T(8,128)(2,1)S(1)}, bf16[512,256]{1,0:T(8,128)(2,1)S(1)}) fusion(bf16[2048,256]{1,0:T(8,128)(2,1)} %content.1, s32[]{:T(128)S(6)} %add.4, s32[]{:T(128)S(6)} %select_n.3), kind=kLoop, calls=%fused_computation.1 | loop fusion | bytes 1048584 | tf_op jit(solution)/shard_map/slice | solution.py:264
  1.7 2.3 %collective-permute-start.1 = (bf16[512,256]{1,0:T(8,128)(2,1)S(1)}, bf16[512,256]{1,0:T(8,128)(2,1)S(1)}, u32[]{:S(2)}, u32[]{:S(2)}) collective-permute-start(bf16[512,256]{1,0:T(8,128)(2,1)S(1)} %get-tuple-element.88), channel_id=1, source_target_pairs={{0,1},{1,0},{2,3},{3,2},{4,5},{5,4},{6,7},{7,6},{8,9},{9,8},{10,11... | collective-permute-start | bytes 786440 | tf_op jit(solution)/shard_map/ppermute | solution.py:264
  4.0 0.1 collective-permute-start
  4.1 8.4 %ratings.1.values = s16[512,1024]{1,0:T(8,128)(2,1)S(1)} custom-call(s32[16384,128]{1,0:T(8,128)} %bitcast.10), custom_call_target="tpu_custom_call" | custom-call | flops 1048576 | bytes 12582912 | tf_op jit(solution)/shard_map/ratings/pallas_call | solution.py:269
  12.5 1.7 %before.1 = (bf16[1024,1024]{1,0:T(8,128)(2,1)S(1)}, f32[1024,256]{1,0:T(8,128)S(1)}, f32[8,128]{1,0:T(8,128)S(1)}, bf16[512,768]{1,0:T(8,128)(2,1)S(1)}, bf16[256,1536]{1,0:T(8,128)(2,1)S(1)}) custom-call(s32[1,1024]{1,0:T(1,128)S(1)} %copy-done.3, bf16[2048,256]{1,0:T(8,128)(2,1)S(1)} %copy-done.2, bf16[512,256]{1,0:T(8,128)(2,1)S(1)} %copy-done.1, ...), custom_call_target="tpu_custom_call" | custom-call | flops 536870912 | bytes 6291456 | tf_op jit(solution)/shard_map/before/pallas_call | solution.py:281
  14.2 0.0 collective-permute-done.1.second
  14.2 1.2 %collective-permute-done.first = bf16[512,256]{1,0:T(8,128)(2,1)S(1)} collective-permute-done((bf16[512,256]{1,0:T(8,128)(2,1)S(1)}, bf16[512,256]{1,0:T(8,128)(2,1)S(1)}, u32[]{:S(2)}, u32[]{:S(2)}) %collective-permute-start) | collective-permute-done | bytes 262176 | tf_op jit(solution)/shard_map/ppermute | solution.py:264
  15.5 1.2 %project.1 = s32[1024,128]{1,0:T(8,128)S(1)} custom-call(bf16[1024,1024]{1,0:T(8,128)(2,1)S(1)} %get-tuple-element.49.deal, bf16[512,256]{1,0:T(8,128)(2,1)S(1)} %collective-permute-done.first, bf16[512,256]{1,0:T(8,128)(2,1)S(1)} %collective-permute-done.1.second, bf16[512,256]{1,0:T(8,128)(2,1)S(1)} %copy-done.1, ...), custom_call_target="tpu_custom_call" | custom-call | flops 536870912 | bytes 4194304 | tf_op jit(solution)/shard_map/project/pallas_call | solution.py:299
  16.6 36.1 %all_to_all.5 = s32[128,8,128]{2,1,0:T(8,128)S(1)} all-to-all(s32[128,8,128]{2,1,0:T(8,128)S(1)} %bitcast.9), channel_id=1, replica_groups=mesh['blk'=128,'cat'=2] {'blk'}, dimensions={0} | all-to-all | bytes 1048576 | tf_op jit(solution)/shard_map/all_to_all | solution.py:308
  52.8 3.4 %collective-permute-start.3 = (s32[144,1024]{1,0:T(8,128)S(1)}, s32[144,1024]{1,0:T(8,128)S(1)}, u32[]{:S(2)}, u32[]{:S(2)}) collective-permute-start(s32[144,1024]{1,0:T(8,128)S(1)} %get-tuple-element.54), channel_id=1, source_target_pairs={{0,2},{2,4},{4,6},{6,8},{8,10},{10,12},{12,14},{14,16},{16,18},{18... | collective-permute-start | bytes 1769480 | tf_op jit(solution)/shard_map/ppermute | solution.py:334
  56.2 3.1 %push.7 = (bf16[2,512,1024]{2,1,0:T(8,128)(2,1)S(1)}, bf16[2,256,1024]{2,1,0:T(8,128)(2,1)S(1)}, s32[136,1024]{1,0:T(8,128)S(1)}) custom-call(bf16[512,768]{1,0:T(8,128)(2,1)S(1)} %get-tuple-element.55.left, bf16[256,1536]{1,0:T(8,128)(2,1)S(1)} %get-tuple-element.47.left_t, s16[512,1024]{1,0:T(8,128)(2,1)S(1)} %ratings.1.values, s32[1024,128]{1,0:T(8,128)S(1)} %bitcast.8, ...), custom_call_target="tpu_custom_call" | custom-call | flops 1024 | bytes 1024 | tf_op jit(solution)/shard_map/push/pallas_call | solution.py:318
  59.3 0.1 collective-permute-start.2
  59.4 1.2 %pull.3 = (f32[512,256]{1,0:T(8,128)S(1)}, bf16[512,768]{1,0:T(8,128)(2,1)S(1)}, bf16[256,1536]{1,0:T(8,128)(2,1)S(1)}) custom-call(f32[512,256]{1,0:T(8,128)S(1)} %copy-done, bf16[2,512,1024]{2,1,0:T(8,128)(2,1)S(1)} %get-tuple-element.52.err_o, bf16[2,256,1024]{2,1,0:T(8,128)(2,1)S(1)} %get-tuple-element.53.right_o, ...), custom_call_target="tpu_custom_call" | custom-call | flops 1024 | bytes 1024 | tf_op jit(solution)/shard_map/pull/pallas_call | solution.py:338
  60.6 0.8 collective-permute-done.2.refs_0_
  61.4 2.8 %collective-permute-start.5 = (s32[144,1024]{1,0:T(8,128)S(1)}, s32[144,1024]{1,0:T(8,128)S(1)}, u32[]{:S(2)}, u32[]{:S(2)}) collective-permute-start(s32[144,1024]{1,0:T(8,128)S(1)} %get-tuple-element.64), channel_id=1, source_target_pairs={{0,2},{2,4},{4,6},{6,8},{8,10},{10,12},{12,14},{14,16},{16,18},{18... | collective-permute-start | bytes 1769480 | tf_op jit(solution)/shard_map/ppermute | solution.py:334
  64.2 3.6 %collective-permute-done.3.refs_0_ = s32[144,1024]{1,0:T(8,128)S(1)} collective-permute-done((s32[144,1024]{1,0:T(8,128)S(1)}, s32[144,1024]{1,0:T(8,128)S(1)}, u32[]{:S(2)}, u32[]{:S(2)}) %collective-permute-start.3) | collective-permute-done | bytes 589856 | tf_op jit(solution)/shard_map/ppermute | solution.py:334
  67.8 2.6 %push.9 = (bf16[2,512,1024]{2,1,0:T(8,128)(2,1)S(1)}, bf16[2,256,1024]{2,1,0:T(8,128)(2,1)S(1)}, s32[136,1024]{1,0:T(8,128)S(1)}) custom-call(bf16[512,768]{1,0:T(8,128)(2,1)S(1)} %get-tuple-element.65.left, bf16[256,1536]{1,0:T(8,128)(2,1)S(1)} %get-tuple-element.60.left_t, s16[512,1024]{1,0:T(8,128)(2,1)S(1)} %ratings.1.values, ...), custom_call_target="tpu_custom_call" | custom-call | flops 1024 | bytes 1024 | tf_op jit(solution)/shard_map/push/pallas_call | solution.py:318
  70.4 0.1 collective-permute-start.4
  70.5 1.1 %pull.4 = (f32[512,256]{1,0:T(8,128)S(1)}, bf16[512,768]{1,0:T(8,128)(2,1)S(1)}, bf16[256,1536]{1,0:T(8,128)(2,1)S(1)}) custom-call(f32[512,256]{1,0:T(8,128)S(1)} %get-tuple-element.58.users, bf16[2,512,1024]{2,1,0:T(8,128)(2,1)S(1)} %get-tuple-element.62.err_o, bf16[2,256,1024]{2,1,0:T(8,128)(2,1)S(1)} %get-tuple-element.63.right_o, ...), custom_call_target="tpu_custom_call" | custom-call | flops 1024 | bytes 1024 | tf_op jit(solution)/shard_map/pull/pallas_call | solution.py:338
  71.6 0.8 collective-permute-done.4.refs_0_
  72.4 2.8 %collective-permute-start.7 = (s32[144,512]{1,0:T(8,128)S(1)}, s32[144,512]{1,0:T(8,128)S(1)}, u32[]{:S(2)}, u32[]{:S(2)}) collective-permute-start(s32[144,512]{1,0:T(8,128)S(1)} %get-tuple-element.74), channel_id=1, source_target_pairs={{0,2},{2,4},{4,6},{6,8},{8,10},{10,12},{12,14},{14,16},{16,18},{18... | collective-permute-start | bytes 884744 | tf_op jit(solution)/shard_map/ppermute | solution.py:334
  75.2 0.1 collective-permute-start.9
  75.3 1.1 %collective-permute-done.5.refs_0_ = s32[144,1024]{1,0:T(8,128)S(1)} collective-permute-done((s32[144,1024]{1,0:T(8,128)S(1)}, s32[144,1024]{1,0:T(8,128)S(1)}, u32[]{:S(2)}, u32[]{:S(2)}) %collective-permute-start.5) | collective-permute-done | bytes 589856 | tf_op jit(solution)/shard_map/ppermute | solution.py:334
  76.4 2.6 %push.11 = (bf16[2,512,1024]{2,1,0:T(8,128)(2,1)S(1)}, bf16[2,256,1024]{2,1,0:T(8,128)(2,1)S(1)}, s32[136,512]{1,0:T(8,128)S(1)}, s32[136,512]{1,0:T(8,128)S(1)}) custom-call(bf16[512,768]{1,0:T(8,128)(2,1)S(1)} %get-tuple-element.75.left, bf16[256,1536]{1,0:T(8,128)(2,1)S(1)} %get-tuple-element.70.left_t, s16[512,1024]{1,0:T(8,128)(2,1)S(1)} %ratings.1.values, ...), custom_call_target="tpu_custom_call" | custom-call | flops 1024 | bytes 1024 | tf_op jit(solution)/shard_map/push/pallas_call | solution.py:318
  79.0 0.1 collective-permute-start.6
  79.1 0.5 collective-permute-start.8
  79.6 1.1 %pull.5 = (f32[512,256]{1,0:T(8,128)S(1)}, bf16[512,768]{1,0:T(8,128)(2,1)S(1)}, bf16[256,1536]{1,0:T(8,128)(2,1)S(1)}) custom-call(f32[512,256]{1,0:T(8,128)S(1)} %get-tuple-element.68.users, bf16[2,512,1024]{2,1,0:T(8,128)(2,1)S(1)} %get-tuple-element.72.err_o, bf16[2,256,1024]{2,1,0:T(8,128)(2,1)S(1)} %get-tuple-element.73.right_o, ...), custom_call_target="tpu_custom_call" | custom-call | flops 1024 | bytes 1024 | tf_op jit(solution)/shard_map/pull/pallas_call | solution.py:338
  80.7 3.6 %collective-permute-done.7.got_e = s32[144,512]{1,0:T(8,128)S(1)} collective-permute-done((s32[144,512]{1,0:T(8,128)S(1)}, s32[144,512]{1,0:T(8,128)S(1)}, u32[]{:S(2)}, u32[]{:S(2)}) %collective-permute-start.7) | collective-permute-done | bytes 294944 | tf_op jit(solution)/shard_map/ppermute | solution.py:334
  84.3 2.5 %last_first.1 = (f32[1024,256]{1,0:T(8,128)}, f32[512,256]{1,0:T(8,128)S(1)}) custom-call(bf16[512,768]{1,0:T(8,128)(2,1)S(1)} %get-tuple-element.78.left, bf16[256,1536]{1,0:T(8,128)(2,1)S(1)} %get-tuple-element.79.left_t, s16[512,1024]{1,0:T(8,128)(2,1)S(1)} %ratings.1.values, f32[512,256]{1,0:T(8,128)S(1)} %get-tuple-element.80.users, ...), custom_call_target="tpu_custom_call" | custom-call | flops 1024 | bytes 1024 | tf_op jit(solution)/shard_map/last_first/pallas_call | solution.py:351
  86.8 0.0 collective-permute-done.8.got_o
  86.8 0.7 collective-permute-done.9.got_e
  87.5 2.7 %last_second.1 = (f32[1024,256]{1,0:T(8,128)}, f32[512,256]{1,0:T(8,128)}) custom-call(bf16[512,768]{1,0:T(8,128)(2,1)S(1)} %get-tuple-element.78.left, bf16[256,1536]{1,0:T(8,128)(2,1)S(1)} %get-tuple-element.79.left_t, s16[512,1024]{1,0:T(8,128)(2,1)S(1)} %ratings.1.values, ...), custom_call_target="tpu_custom_call", output_to_operand_aliasing={{0}: (6, {})} | custom-call | flops 1024 | bytes 1024 | tf_op jit(solution)/shard_map/last_second/pallas_call | solution.py:361
  (12 shorter events, 0.0 us)
Async XLA Ops:
  1.7 12.5 %collective-permute-start.1 = (bf16[512,256]{1,0:T(8,128)(2,1)S(1)}, bf16[512,256]{1,0:T(8,128)(2,1)S(1)}, u32[]{:S(2)}, u32[]{:S(2)}) collective-permute-start(bf16[512,256]{1,0:T(8,128)(2,1)S(1)} %get-tuple-element.88), channel_id=1, source_target_pairs={{0,1},{1,0},{2,3},{3,2},{4,5},{5,4},{6,7},{7,6},{8,9},{9,8},{10,11... | collective-permute-start | bytes 786440 | tf_op jit(solution)/shard_map/ppermute | solution.py:264
  4.0 11.5 %collective-permute-start = (bf16[512,256]{1,0:T(8,128)(2,1)S(1)}, bf16[512,256]{1,0:T(8,128)(2,1)S(1)}, u32[]{:S(2)}, u32[]{:S(2)}) collective-permute-start(bf16[512,256]{1,0:T(8,128)(2,1)S(1)} %get-tuple-element.89), channel_id=1, source_target_pairs={{0,1},{1,0},{2,3},{3,2},{4,5},{5,4},{6,7},{7,6},{8,9},{9,8},{10,11... | collective-permute-start | bytes 786440 | tf_op jit(solution)/shard_map/ppermute | solution.py:264
  4.1 8.4 %copy-start = (f32[512,256]{1,0:T(8,128)S(1)}, f32[512,256]{1,0:T(8,128)}, u32[]{:S(2)}) copy-start(f32[512,256]{1,0:T(8,128)} %users.3) | copy-start | bytes 1572868
  4.1 8.4 %copy-start.1 = (bf16[512,256]{1,0:T(8,128)(2,1)S(1)}, bf16[512,256]{1,0:T(8,128)(2,1)}, u32[]{:S(2)}) copy-start(bf16[512,256]{1,0:T(8,128)(2,1)} %weights.3) | copy-start | bytes 786436
  4.1 8.4 %copy-start.2 = (bf16[2048,256]{1,0:T(8,128)(2,1)S(1)}, bf16[2048,256]{1,0:T(8,128)(2,1)}, u32[]{:S(2)}) copy-start(bf16[2048,256]{1,0:T(8,128)(2,1)} %content.1) | copy-start | bytes 3145732
  4.1 8.4 %copy-start.3 = (s32[1,1024]{1,0:T(1,128)S(1)}, s32[1,1024]{1,0:T(1,128)}, u32[]{:S(2)}) copy-start(s32[1,1024]{1,0:T(1,128)} %order) | copy-start | bytes 12292
  52.8 15.0 %collective-permute-start.3 = (s32[144,1024]{1,0:T(8,128)S(1)}, s32[144,1024]{1,0:T(8,128)S(1)}, u32[]{:S(2)}, u32[]{:S(2)}) collective-permute-start(s32[144,1024]{1,0:T(8,128)S(1)} %get-tuple-element.54), channel_id=1, source_target_pairs={{0,2},{2,4},{4,6},{6,8},{8,10},{10,12},{12,14},{14,16},{16,18},{18... | collective-permute-start | bytes 1769480 | tf_op jit(solution)/shard_map/ppermute | solution.py:334
  59.3 2.0 %collective-permute-start.2 = (s32[136,1024]{1,0:T(8,128)S(1)}, s32[136,1024]{1,0:T(8,128)S(1)}, u32[]{:S(2)}, u32[]{:S(2)}) collective-permute-start(s32[136,1024]{1,0:T(8,128)S(1)} %get-tuple-element.61), channel_id=1, source_target_pairs={{0,2},{2,0},{4,6},{6,4},{8,10},{10,8},{12,14},{14,12},{16,18},{18,... | collective-permute-start | bytes 1671176 | tf_op jit(solution)/shard_map/ppermute | solution.py:337
  61.4 15.0 %collective-permute-start.5 = (s32[144,1024]{1,0:T(8,128)S(1)}, s32[144,1024]{1,0:T(8,128)S(1)}, u32[]{:S(2)}, u32[]{:S(2)}) collective-permute-start(s32[144,1024]{1,0:T(8,128)S(1)} %get-tuple-element.64), channel_id=1, source_target_pairs={{0,2},{2,4},{4,6},{6,8},{8,10},{10,12},{12,14},{14,16},{16,18},{18... | collective-permute-start | bytes 1769480 | tf_op jit(solution)/shard_map/ppermute | solution.py:334
  70.4 2.0 %collective-permute-start.4 = (s32[136,1024]{1,0:T(8,128)S(1)}, s32[136,1024]{1,0:T(8,128)S(1)}, u32[]{:S(2)}, u32[]{:S(2)}) collective-permute-start(s32[136,1024]{1,0:T(8,128)S(1)} %get-tuple-element.71), channel_id=1, source_target_pairs={{0,2},{2,0},{4,6},{6,4},{8,10},{10,8},{12,14},{14,12},{16,18},{18,... | collective-permute-start | bytes 1671176 | tf_op jit(solution)/shard_map/ppermute | solution.py:337
  72.4 11.9 %collective-permute-start.7 = (s32[144,512]{1,0:T(8,128)S(1)}, s32[144,512]{1,0:T(8,128)S(1)}, u32[]{:S(2)}, u32[]{:S(2)}) collective-permute-start(s32[144,512]{1,0:T(8,128)S(1)} %get-tuple-element.74), channel_id=1, source_target_pairs={{0,2},{2,4},{4,6},{6,8},{8,10},{10,12},{12,14},{14,16},{16,18},{18... | collective-permute-start | bytes 884744 | tf_op jit(solution)/shard_map/ppermute | solution.py:334
  75.2 12.2 %collective-permute-start.9 = (s32[144,512]{1,0:T(8,128)S(1)}, s32[144,512]{1,0:T(8,128)S(1)}, u32[]{:S(2)}, u32[]{:S(2)}) collective-permute-start(s32[144,512]{1,0:T(8,128)S(1)} %get-tuple-element.84), channel_id=1, source_target_pairs={{0,2},{2,4},{4,6},{6,8},{8,10},{10,12},{12,14},{14,16},{16,18},{18... | collective-permute-start | bytes 884744 | tf_op jit(solution)/shard_map/ppermute | solution.py:334
  79.0 1.7 %collective-permute-start.6 = (s32[136,512]{1,0:T(8,128)S(1)}, s32[136,512]{1,0:T(8,128)S(1)}, u32[]{:S(2)}, u32[]{:S(2)}) collective-permute-start(s32[136,512]{1,0:T(8,128)S(1)} %get-tuple-element.81), channel_id=1, source_target_pairs={{0,2},{2,0},{4,6},{6,4},{8,10},{10,8},{12,14},{14,12},{16,18},{18,... | collective-permute-start | bytes 835592 | tf_op jit(solution)/shard_map/ppermute | solution.py:337
  79.1 7.7 %collective-permute-start.8 = (s32[136,512]{1,0:T(8,128)S(1)}, s32[136,512]{1,0:T(8,128)S(1)}, u32[]{:S(2)}, u32[]{:S(2)}) collective-permute-start(s32[136,512]{1,0:T(8,128)S(1)} %get-tuple-element.83), channel_id=1, source_target_pairs={{0,2},{2,0},{4,6},{6,4},{8,10},{10,8},{12,14},{14,12},{16,18},{18,... | collective-permute-start | bytes 835592 | tf_op jit(solution)/shard_map/ppermute | solution.py:337

commit v7 on v5

--- a/solution.py
+++ b/solution.py
@@ -165,7 +165,7 @@
     return log_value(jnp.concatenate([a, b], axis=0), meta[0:1, 0:1])
 
 
-CHUNK = 256
+CHUNK = 512
 
 
 def my_turn(turn):

time: 90.6 us -> 90.8 us (level)
  waiting for transfers between devices: 11.8 us -> 9.92 us
  Pallas kernels: 28.1 us -> 29.5 us
    ppermute x4, waiting for transfers between devices: 8.98 us -> 7.32 us  [body(): next_even = [lax.ppermute(x, 'blk', ring) for x in sent]]
  transfers between devices with their start and end apart: 10 -> 10, of which waited for: 7 -> 7; matrix products, arithmetic and copies ran while one was open for 0% -> 0% of each run, Pallas kernels for 27% -> 28%
where the time goes in v7:
time: 90.8 us; the launch traced here: 90.5 us
  blocking collectives  36.1 us (40%)
  Pallas kernels  29.5 us (32%)
  starting transfers between devices  12.8 us (14%)
  waiting for transfers between devices  9.92 us (11%)
  local copies, waits for them, and re-layouts  1.08 us (1%)
  between operations  1.01 us (1%)
    all_to_all x1, blocking collectives, body(): lax.all_to_all(coded.reshape(n_blk, share, rank // 2), 'blk', split_axis=...  36.1 us
    ppermute x4, starting transfers between devices, body(): next_even = [lax.ppermute(x, 'blk', ring) for x in sent]  9.67 us
    pallas_call x6, Pallas kernels, push(): pl.pallas_call(functools.partial(push_kernel, turn, t), out_shape=state_s...  8.83 us
    pallas_call x1, Pallas kernels, body(): pl.pallas_call(ratings_kernel, out_shape=struct((n_users, n_items), jnp.i...  8.38 us
    ppermute x4, waiting for transfers between devices, body(): next_even = [lax.ppermute(x, 'blk', ring) for x in sent]  7.32 us
    pallas_call x3, Pallas kernels, body(): pl.pallas_call(pull_kernel, out_shape=[struct((n_users, rank), F32)] + sp...  3.88 us
    pallas_call x1, Pallas kernels, body(): pl.pallas_call(last_first_kernel, out_shape=[pltpu.HBM((n_items, rank), F...  2.94 us
    pallas_call x1, Pallas kernels, body(): pl.pallas_call(last_second_kernel, out_shape=[struct((n_items, rank), F32...  2.65 us
  transfers between devices with their start and end apart: 10, of which 7 were waited for; matrix products, arithmetic and copies ran while one was open for 0% of the time, Pallas kernels for 28%

profile of v7, /device:TPU:8, one launch (start us, length us, event | category | flops | bytes accessed | tf_op | source)
XLA Modules:
  0.0 90.5 jit_solution(14800575619843206091)
XLA Ops:
  0.6 1.1 %constant_dynamic-slice_fusion.1 = (bf16[512,256]{1,0:T(8,128)(2,1)S(1)}, bf16[512,256]{1,0:T(8,128)(2,1)S(1)}) fusion(bf16[2048,256]{1,0:T(8,128)(2,1)} %content.1, s32[]{:T(128)S(6)} %add.4, s32[]{:T(128)S(6)} %select_n.3), kind=kLoop, calls=%fused_computation.1 | loop fusion | bytes 1048584 | tf_op jit(solution)/shard_map/slice | solution.py:264
  1.7 2.3 %collective-permute-start.1 = (bf16[512,256]{1,0:T(8,128)(2,1)S(1)}, bf16[512,256]{1,0:T(8,128)(2,1)S(1)}, u32[]{:S(2)}, u32[]{:S(2)}) collective-permute-start(bf16[512,256]{1,0:T(8,128)(2,1)S(1)} %get-tuple-element.88), channel_id=1, source_target_pairs={{0,1},{1,0},{2,3},{3,2},{4,5},{5,4},{6,7},{7,6},{8,9},{9,8},{10,11... | collective-permute-start | bytes 786440 | tf_op jit(solution)/shard_map/ppermute | solution.py:264
  4.0 0.1 collective-permute-start
  4.1 8.4 %ratings.1.values = s16[512,1024]{1,0:T(8,128)(2,1)S(1)} custom-call(s32[16384,128]{1,0:T(8,128)} %bitcast.10), custom_call_target="tpu_custom_call" | custom-call | flops 1048576 | bytes 12582912 | tf_op jit(solution)/shard_map/ratings/pallas_call | solution.py:269
  12.5 1.7 %before.1 = (bf16[1024,1024]{1,0:T(8,128)(2,1)S(1)}, f32[1024,256]{1,0:T(8,128)S(1)}, f32[8,128]{1,0:T(8,128)S(1)}, bf16[2,512,256]{2,1,0:T(8,128)(2,1)S(1)}, bf16[2,256,512]{2,1,0:T(8,128)(2,1)S(1)}) custom-call(s32[1,1024]{1,0:T(1,128)S(1)} %copy-done.3, bf16[2048,256]{1,0:T(8,128)(2,1)S(1)} %copy-done.2, bf16[512,256]{1,0:T(8,128)(2,1)S(1)} %copy-done.1, ...), custom_call_target="tpu_custom_call" | custom-call | flops 536870912 | bytes 6291456 | tf_op jit(solution)/shard_map/before/pallas_call | solution.py:281
  14.2 0.0 collective-permute-done.1.second
  14.2 1.2 %collective-permute-done.first = bf16[512,256]{1,0:T(8,128)(2,1)S(1)} collective-permute-done((bf16[512,256]{1,0:T(8,128)(2,1)S(1)}, bf16[512,256]{1,0:T(8,128)(2,1)S(1)}, u32[]{:S(2)}, u32[]{:S(2)}) %collective-permute-start) | collective-permute-done | bytes 262176 | tf_op jit(solution)/shard_map/ppermute | solution.py:264
  15.5 1.2 %project.1 = s32[1024,128]{1,0:T(8,128)S(1)} custom-call(bf16[1024,1024]{1,0:T(8,128)(2,1)S(1)} %get-tuple-element.49.deal, bf16[512,256]{1,0:T(8,128)(2,1)S(1)} %collective-permute-done.first, bf16[512,256]{1,0:T(8,128)(2,1)S(1)} %collective-permute-done.1.second, bf16[512,256]{1,0:T(8,128)(2,1)S(1)} %copy-done.1, ...), custom_call_target="tpu_custom_call" | custom-call | flops 536870912 | bytes 4194304 | tf_op jit(solution)/shard_map/project/pallas_call | solution.py:299
  16.6 36.1 %all_to_all.5 = s32[128,8,128]{2,1,0:T(8,128)S(1)} all-to-all(s32[128,8,128]{2,1,0:T(8,128)S(1)} %bitcast.9), channel_id=1, replica_groups=mesh['blk'=128,'cat'=2] {'blk'}, dimensions={0} | all-to-all | bytes 1048576 | tf_op jit(solution)/shard_map/all_to_all | solution.py:308
  52.8 3.6 %collective-permute-start.3 = (s32[144,1024]{1,0:T(8,128)S(1)}, s32[144,1024]{1,0:T(8,128)S(1)}, u32[]{:S(2)}, u32[]{:S(2)}) collective-permute-start(s32[144,1024]{1,0:T(8,128)S(1)} %get-tuple-element.54), channel_id=1, source_target_pairs={{0,2},{2,4},{4,6},{6,8},{8,10},{10,12},{12,14},{14,16},{16,18},{18... | collective-permute-start | bytes 1769480 | tf_op jit(solution)/shard_map/ppermute | solution.py:334
  56.3 3.3 %push.7 = (bf16[2,512,1024]{2,1,0:T(8,128)(2,1)S(1)}, bf16[2,256,1024]{2,1,0:T(8,128)(2,1)S(1)}, s32[136,1024]{1,0:T(8,128)S(1)}) custom-call(bf16[2,512,256]{2,1,0:T(8,128)(2,1)S(1)} %get-tuple-element.55.left, bf16[2,256,512]{2,1,0:T(8,128)(2,1)S(1)} %get-tuple-element.47.left_t, s16[512,1024]{1,0:T(8,128)(2,1)S(1)} %ratings.1.values, ...), custom_call_target="tpu_custom_call" | custom-call | flops 1024 | bytes 1024 | tf_op jit(solution)/shard_map/push/pallas_call | solution.py:318
  59.6 0.1 collective-permute-start.2
  59.7 1.1 %pull.3 = (f32[512,256]{1,0:T(8,128)S(1)}, bf16[2,512,256]{2,1,0:T(8,128)(2,1)S(1)}, bf16[2,256,512]{2,1,0:T(8,128)(2,1)S(1)}) custom-call(f32[512,256]{1,0:T(8,128)S(1)} %copy-done, bf16[2,512,1024]{2,1,0:T(8,128)(2,1)S(1)} %get-tuple-element.52.err_o, bf16[2,256,1024]{2,1,0:T(8,128)(2,1)S(1)} %get-tuple-element.53.right_o, ...), custom_call_target="tpu_custom_call" | custom-call | flops 1024 | bytes 1024 | tf_op jit(solution)/shard_map/pull/pallas_call | solution.py:338
  60.9 0.8 collective-permute-done.2.refs_0_
  61.6 3.0 %collective-permute-start.5 = (s32[144,1024]{1,0:T(8,128)S(1)}, s32[144,1024]{1,0:T(8,128)S(1)}, u32[]{:S(2)}, u32[]{:S(2)}) collective-permute-start(s32[144,1024]{1,0:T(8,128)S(1)} %get-tuple-element.64), channel_id=1, source_target_pairs={{0,2},{2,4},{4,6},{6,8},{8,10},{10,12},{12,14},{14,16},{16,18},{18... | collective-permute-start | bytes 1769480 | tf_op jit(solution)/shard_map/ppermute | solution.py:334
  64.7 3.1 %collective-permute-done.3.refs_0_ = s32[144,1024]{1,0:T(8,128)S(1)} collective-permute-done((s32[144,1024]{1,0:T(8,128)S(1)}, s32[144,1024]{1,0:T(8,128)S(1)}, u32[]{:S(2)}, u32[]{:S(2)}) %collective-permute-start.3) | collective-permute-done | bytes 589856 | tf_op jit(solution)/shard_map/ppermute | solution.py:334
  67.8 2.8 %push.9 = (bf16[2,512,1024]{2,1,0:T(8,128)(2,1)S(1)}, bf16[2,256,1024]{2,1,0:T(8,128)(2,1)S(1)}, s32[136,1024]{1,0:T(8,128)S(1)}) custom-call(bf16[2,512,256]{2,1,0:T(8,128)(2,1)S(1)} %get-tuple-element.65.left, bf16[2,256,512]{2,1,0:T(8,128)(2,1)S(1)} %get-tuple-element.60.left_t, s16[512,1024]{1,0:T(8,128)(2,1)S(1)} %ratings.1.values, ...), custom_call_target="tpu_custom_call" | custom-call | flops 1024 | bytes 1024 | tf_op jit(solution)/shard_map/push/pallas_call | solution.py:318
  70.6 0.1 collective-permute-start.4
  70.7 1.4 %pull.4 = (f32[512,256]{1,0:T(8,128)S(1)}, bf16[2,512,256]{2,1,0:T(8,128)(2,1)S(1)}, bf16[2,256,512]{2,1,0:T(8,128)(2,1)S(1)}) custom-call(f32[512,256]{1,0:T(8,128)S(1)} %get-tuple-element.58.users, bf16[2,512,1024]{2,1,0:T(8,128)(2,1)S(1)} %get-tuple-element.62.err_o, bf16[2,256,1024]{2,1,0:T(8,128)(2,1)S(1)} %get-tuple-element.63.right_o, ...), custom_call_target="tpu_custom_call" | custom-call | flops 1024 | bytes 1024 | tf_op jit(solution)/shard_map/pull/pallas_call | solution.py:338
  72.0 0.6 collective-permute-done.4.refs_0_
  72.6 3.0 %collective-permute-start.7 = (s32[144,512]{1,0:T(8,128)S(1)}, s32[144,512]{1,0:T(8,128)S(1)}, u32[]{:S(2)}, u32[]{:S(2)}) collective-permute-start(s32[144,512]{1,0:T(8,128)S(1)} %get-tuple-element.74), channel_id=1, source_target_pairs={{0,2},{2,4},{4,6},{6,8},{8,10},{10,12},{12,14},{14,16},{16,18},{18... | collective-permute-start | bytes 884744 | tf_op jit(solution)/shard_map/ppermute | solution.py:334
  75.6 0.1 collective-permute-start.9
  75.7 0.9 %collective-permute-done.5.refs_0_ = s32[144,1024]{1,0:T(8,128)S(1)} collective-permute-done((s32[144,1024]{1,0:T(8,128)S(1)}, s32[144,1024]{1,0:T(8,128)S(1)}, u32[]{:S(2)}, u32[]{:S(2)}) %collective-permute-start.5) | collective-permute-done | bytes 589856 | tf_op jit(solution)/shard_map/ppermute | solution.py:334
  76.7 2.8 %push.11 = (bf16[2,512,1024]{2,1,0:T(8,128)(2,1)S(1)}, bf16[2,256,1024]{2,1,0:T(8,128)(2,1)S(1)}, s32[136,512]{1,0:T(8,128)S(1)}, s32[136,512]{1,0:T(8,128)S(1)}) custom-call(bf16[2,512,256]{2,1,0:T(8,128)(2,1)S(1)} %get-tuple-element.75.left, bf16[2,256,512]{2,1,0:T(8,128)(2,1)S(1)} %get-tuple-element.70.left_t, s16[512,1024]{1,0:T(8,128)(2,1)S(1)} %ratings.1.values, ...), custom_call_target="tpu_custom_call" | custom-call | flops 1024 | bytes 1024 | tf_op jit(solution)/shard_map/push/pallas_call | solution.py:318
  79.5 0.1 collective-permute-start.6
  79.6 0.5 collective-permute-start.8
  80.1 1.4 %pull.5 = (f32[512,256]{1,0:T(8,128)S(1)}, bf16[2,512,256]{2,1,0:T(8,128)(2,1)S(1)}, bf16[2,256,512]{2,1,0:T(8,128)(2,1)S(1)}) custom-call(f32[512,256]{1,0:T(8,128)S(1)} %get-tuple-element.68.users, bf16[2,512,1024]{2,1,0:T(8,128)(2,1)S(1)} %get-tuple-element.72.err_o, bf16[2,256,1024]{2,1,0:T(8,128)(2,1)S(1)} %get-tuple-element.73.right_o, ...), custom_call_target="tpu_custom_call" | custom-call | flops 1024 | bytes 1024 | tf_op jit(solution)/shard_map/pull/pallas_call | solution.py:338
  81.4 0.0 collective-permute-done.6.got_o
  81.5 3.0 %collective-permute-done.7.got_e = s32[144,512]{1,0:T(8,128)S(1)} collective-permute-done((s32[144,512]{1,0:T(8,128)S(1)}, s32[144,512]{1,0:T(8,128)S(1)}, u32[]{:S(2)}, u32[]{:S(2)}) %collective-permute-start.7) | collective-permute-done | bytes 294944 | tf_op jit(solution)/shard_map/ppermute | solution.py:334
  84.5 2.9 %last_first.1 = (f32[1024,256]{1,0:T(8,128)}, f32[512,256]{1,0:T(8,128)S(1)}) custom-call(bf16[2,512,256]{2,1,0:T(8,128)(2,1)S(1)} %get-tuple-element.78.left, bf16[2,256,512]{2,1,0:T(8,128)(2,1)S(1)} %get-tuple-element.79.left_t, s16[512,1024]{1,0:T(8,128)(2,1)S(1)} %ratings.1.values, f32[512,256]{1,0:T(8,128)S(1)} %get-tuple-element.80.users, ...), custom_call_target="tpu_custom_call" | custom-call | flops 1024 | bytes 1024 | tf_op jit(solution)/shard_map/last_first/pallas_call | solution.py:351
  87.5 0.2 collective-permute-done.9.got_e
  87.7 2.7 %last_second.1 = (f32[1024,256]{1,0:T(8,128)}, f32[512,256]{1,0:T(8,128)}) custom-call(bf16[2,512,256]{2,1,0:T(8,128)(2,1)S(1)} %get-tuple-element.78.left, bf16[2,256,512]{2,1,0:T(8,128)(2,1)S(1)} %get-tuple-element.79.left_t, s16[512,1024]{1,0:T(8,128)(2,1)S(1)} %ratings.1.values, ...), custom_call_target="tpu_custom_call", output_to_operand_aliasing={{0}: (6, {})} | custom-call | flops 1024 | bytes 1024 | tf_op jit(solution)/shard_map/last_second/pallas_call | solution.py:361
  (12 shorter events, 0.0 us)
Async XLA Ops:
  1.7 12.5 %collective-permute-start.1 = (bf16[512,256]{1,0:T(8,128)(2,1)S(1)}, bf16[512,256]{1,0:T(8,128)(2,1)S(1)}, u32[]{:S(2)}, u32[]{:S(2)}) collective-permute-start(bf16[512,256]{1,0:T(8,128)(2,1)S(1)} %get-tuple-element.88), channel_id=1, source_target_pairs={{0,1},{1,0},{2,3},{3,2},{4,5},{5,4},{6,7},{7,6},{8,9},{9,8},{10,11... | collective-permute-start | bytes 786440 | tf_op jit(solution)/shard_map/ppermute | solution.py:264
  4.0 11.5 %collective-permute-start = (bf16[512,256]{1,0:T(8,128)(2,1)S(1)}, bf16[512,256]{1,0:T(8,128)(2,1)S(1)}, u32[]{:S(2)}, u32[]{:S(2)}) collective-permute-start(bf16[512,256]{1,0:T(8,128)(2,1)S(1)} %get-tuple-element.89), channel_id=1, source_target_pairs={{0,1},{1,0},{2,3},{3,2},{4,5},{5,4},{6,7},{7,6},{8,9},{9,8},{10,11... | collective-permute-start | bytes 786440 | tf_op jit(solution)/shard_map/ppermute | solution.py:264
  4.1 8.4 %copy-start = (f32[512,256]{1,0:T(8,128)S(1)}, f32[512,256]{1,0:T(8,128)}, u32[]{:S(2)}) copy-start(f32[512,256]{1,0:T(8,128)} %users.3) | copy-start | bytes 1572868
  4.1 8.4 %copy-start.1 = (bf16[512,256]{1,0:T(8,128)(2,1)S(1)}, bf16[512,256]{1,0:T(8,128)(2,1)}, u32[]{:S(2)}) copy-start(bf16[512,256]{1,0:T(8,128)(2,1)} %weights.3) | copy-start | bytes 786436
  4.1 8.4 %copy-start.2 = (bf16[2048,256]{1,0:T(8,128)(2,1)S(1)}, bf16[2048,256]{1,0:T(8,128)(2,1)}, u32[]{:S(2)}) copy-start(bf16[2048,256]{1,0:T(8,128)(2,1)} %content.1) | copy-start | bytes 3145732
  4.1 8.4 %copy-start.3 = (s32[1,1024]{1,0:T(1,128)S(1)}, s32[1,1024]{1,0:T(1,128)}, u32[]{:S(2)}) copy-start(s32[1,1024]{1,0:T(1,128)} %order) | copy-start | bytes 12292
  52.8 15.0 %collective-permute-start.3 = (s32[144,1024]{1,0:T(8,128)S(1)}, s32[144,1024]{1,0:T(8,128)S(1)}, u32[]{:S(2)}, u32[]{:S(2)}) collective-permute-start(s32[144,1024]{1,0:T(8,128)S(1)} %get-tuple-element.54), channel_id=1, source_target_pairs={{0,2},{2,4},{4,6},{6,8},{8,10},{10,12},{12,14},{14,16},{16,18},{18... | collective-permute-start | bytes 1769480 | tf_op jit(solution)/shard_map/ppermute | solution.py:334
  59.6 2.0 %collective-permute-start.2 = (s32[136,1024]{1,0:T(8,128)S(1)}, s32[136,1024]{1,0:T(8,128)S(1)}, u32[]{:S(2)}, u32[]{:S(2)}) collective-permute-start(s32[136,1024]{1,0:T(8,128)S(1)} %get-tuple-element.61), channel_id=1, source_target_pairs={{0,2},{2,0},{4,6},{6,4},{8,10},{10,8},{12,14},{14,12},{16,18},{18,... | collective-permute-start | bytes 1671176 | tf_op jit(solution)/shard_map/ppermute | solution.py:337
  61.6 15.0 %collective-permute-start.5 = (s32[144,1024]{1,0:T(8,128)S(1)}, s32[144,1024]{1,0:T(8,128)S(1)}, u32[]{:S(2)}, u32[]{:S(2)}) collective-permute-start(s32[144,1024]{1,0:T(8,128)S(1)} %get-tuple-element.64), channel_id=1, source_target_pairs={{0,2},{2,4},{4,6},{6,8},{8,10},{10,12},{12,14},{14,16},{16,18},{18... | collective-permute-start | bytes 1769480 | tf_op jit(solution)/shard_map/ppermute | solution.py:334
  70.6 2.0 %collective-permute-start.4 = (s32[136,1024]{1,0:T(8,128)S(1)}, s32[136,1024]{1,0:T(8,128)S(1)}, u32[]{:S(2)}, u32[]{:S(2)}) collective-permute-start(s32[136,1024]{1,0:T(8,128)S(1)} %get-tuple-element.71), channel_id=1, source_target_pairs={{0,2},{2,0},{4,6},{6,4},{8,10},{10,8},{12,14},{14,12},{16,18},{18,... | collective-permute-start | bytes 1671176 | tf_op jit(solution)/shard_map/ppermute | solution.py:337
  72.6 11.9 %collective-permute-start.7 = (s32[144,512]{1,0:T(8,128)S(1)}, s32[144,512]{1,0:T(8,128)S(1)}, u32[]{:S(2)}, u32[]{:S(2)}) collective-permute-start(s32[144,512]{1,0:T(8,128)S(1)} %get-tuple-element.74), channel_id=1, source_target_pairs={{0,2},{2,4},{4,6},{6,8},{8,10},{10,12},{12,14},{14,16},{16,18},{18... | collective-permute-start | bytes 884744 | tf_op jit(solution)/shard_map/ppermute | solution.py:334
  75.6 12.0 %collective-permute-start.9 = (s32[144,512]{1,0:T(8,128)S(1)}, s32[144,512]{1,0:T(8,128)S(1)}, u32[]{:S(2)}, u32[]{:S(2)}) collective-permute-start(s32[144,512]{1,0:T(8,128)S(1)} %get-tuple-element.84), channel_id=1, source_target_pairs={{0,2},{2,4},{4,6},{6,8},{8,10},{10,12},{12,14},{14,16},{16,18},{18... | collective-permute-start | bytes 884744 | tf_op jit(solution)/shard_map/ppermute | solution.py:334
  79.5 2.0 %collective-permute-start.6 = (s32[136,512]{1,0:T(8,128)S(1)}, s32[136,512]{1,0:T(8,128)S(1)}, u32[]{:S(2)}, u32[]{:S(2)}) collective-permute-start(s32[136,512]{1,0:T(8,128)S(1)} %get-tuple-element.81), channel_id=1, source_target_pairs={{0,2},{2,0},{4,6},{6,4},{8,10},{10,8},{12,14},{14,12},{16,18},{18,... | collective-permute-start | bytes 835592 | tf_op jit(solution)/shard_map/ppermute | solution.py:337
  79.6 7.9 %collective-permute-start.8 = (s32[136,512]{1,0:T(8,128)S(1)}, s32[136,512]{1,0:T(8,128)S(1)}, u32[]{:S(2)}, u32[]{:S(2)}) collective-permute-start(s32[136,512]{1,0:T(8,128)S(1)} %get-tuple-element.83), channel_id=1, source_target_pairs={{0,2},{2,0},{4,6},{6,4},{8,10},{10,8},{12,14},{14,12},{16,18},{18,... | collective-permute-start | bytes 835592 | tf_op jit(solution)/shard_map/ppermute | solution.py:337
